TPU v7x, 32 devices: a whole 2x2x4 slice. The times are simulated.
32 devices in a mesh: dp: 4 (over y, x), seq: 4 (over z), fsdp: 2 (over core).
Axes of the slice: x: 2, y: 2, z: 4, core: 2. Of those that a mesh axis runs over, the one named last changes fastest.
Arguments:
- tokens: bfloat16 [4, 1024, 4096], P('dp', ('seq', 'fsdp')), may hold values from -6 to 6
- ffn_gain: float32 [4096], replicated, may hold values from 0.25 to 1.75
- in_proj: bfloat16 [4096, 16384], P(None, ('dp', 'seq', 'fsdp')), may hold values from -0.09375 to 0.09375
- out_proj: bfloat16 [16384, 4096], P(('dp', 'seq', 'fsdp')), may hold values from -0.046875 to 0.046875
- router_score: bfloat16 [4, 1024], P('dp', ('seq', 'fsdp')), may hold values from 0.25 to 2
- tile_counts: int32 [4, 8], P('dp', ('seq', 'fsdp')), may hold values from 1 to 12, 64 in all within a row
- tile_order: int32 [4, 8, 128], P('dp', ('seq', 'fsdp')), may hold values from 0 to 127, each once within a row
- light_qkv: bfloat16 [4, 1024, 3, 2048], P('dp', ('seq', 'fsdp')), may hold values from -16 to 16
- heavy_qkv: bfloat16 [4, 96, 3, 2048], P('dp', ('seq', 'fsdp')), may hold values from -16 to 16
Outputs:
- light_out: bfloat16 [4, 1024, 2048], P('dp', ('seq', 'fsdp'))
- heavy_attn: bfloat16 [4, 96, 2048], P('dp', ('seq', 'fsdp'))
- heavy_ffn: bfloat16 [4, 96, 4096], P('dp', ('seq', 'fsdp'))
Inputs may be any that keep to these rules, and one draw needn't show every extreme that they name: `tile_counts`: each document's counts sum to 64; some tile of each document holds 12.
All inputs are finite; a program needn't handle non-finite values. No bound on the sum of `tile_counts` on one device may be relied on, other than what follows from the above.
Results may differ from a plain program's by a relative error of at most 0.02.
Values may be sent and summed in bfloat16 or wider, within the bound.
No kernel may reach another device: no remote copies, remote signals or barrier semaphores. Data moves between devices by JAX's collectives and lax.ppermute only.
A program may use at most 128 MiB of HBM per device.

v0:
```python
import math

import jax
import jax.numpy as jnp
from jax import lax
from jax.sharding import PartitionSpec as P

HEAD_DIM = 128
LIGHT_HEADS = 16
HEAVY_HEADS = 16
TILE = 128
CAP = 12
HALF_WIN = 64


def padded_2(shard, sides, width):
    for axis, dim in sides:
        peers, length = (lax.axis_size(axis), shard.shape[dim])
        up = [(i, (i + 1) % peers) for i in range(peers - 1)]
        down = [(j, i) for i, j in up]
        last = lax.slice_in_dim(shard, length - width, length, axis=dim)
        first = lax.slice_in_dim(shard, 0, width, axis=dim)
        before = lax.ppermute(last, axis, up)
        after = lax.ppermute(first, axis, down)
        shard = jnp.concatenate([before, shard, after], axis=dim)
    return shard


def light_branch(qkv_here):
    tokens_here = qkv_here.shape[0]
    width = qkv_here.shape[2]
    queries = qkv_here[:, 0].reshape(tokens_here, LIGHT_HEADS, HEAD_DIM)
    padded = padded_2(qkv_here[:, 1:], ((("seq", "fsdp"), 0),), HALF_WIN)
    keys_all = padded[:, 0].reshape(tokens_here + 2 * HALF_WIN, LIGHT_HEADS, HEAD_DIM)
    values_all = padded[:, 1].reshape(tokens_here + 2 * HALF_WIN, LIGHT_HEADS, HEAD_DIM)
    first_pos = lax.axis_index(("seq", "fsdp")) * tokens_here
    doc_length = tokens_here * lax.axis_size("seq") * lax.axis_size("fsdp")
    block_rows = min(tokens_here, 512)
    span = block_rows + 2 * HALF_WIN
    row_ids = jnp.arange(block_rows)[:, None]
    col_ids = jnp.arange(span)[None, :]

    def block_out(block_index):
        begin = block_index * block_rows
        scores = jnp.einsum(
            "qhd,khd->qhk", queries, keys_all, preferred_element_type=jnp.float32
        ) / math.sqrt(HEAD_DIM)
        positions = first_pos + begin - HALF_WIN + col_ids
        inside = (
            (col_ids >= row_ids)
            & (col_ids < row_ids + 2 * HALF_WIN)
            & (positions >= 0)
            & (positions < doc_length)
        )
        usable = inside[:, None, :]
        row_max = jnp.max(jnp.where(usable, scores, -jnp.inf), axis=2, keepdims=True)
        expons = jnp.where(usable, jnp.exp(scores - row_max), 0.0)
        totals = jnp.sum(expons, axis=2)
        mixed = jnp.einsum(
            "qhk,khd->qhd",
            expons.astype(jnp.bfloat16),
            values_all,
            preferred_element_type=jnp.float32,
        )
        return (mixed / totals[:, :, None]).reshape(block_rows, width).astype(jnp.bfloat16)

    blocks = lax.map(block_out, jnp.arange(tokens_here // block_rows))
    return blocks.reshape(tokens_here, width)


def heavy_branch(qkv_here, slot_live):
    slot_count = qkv_here.shape[0]
    width = qkv_here.shape[2]
    queries = qkv_here[:, 0].reshape(slot_count, HEAVY_HEADS, HEAD_DIM)
    live_mark = slot_live.astype(jnp.bfloat16)
    run_max = jnp.full((slot_count, HEAVY_HEADS), -1e30, jnp.float32)
    key_piece = lax.all_gather(qkv_here[:, 1], ("seq", "fsdp"), axis=0, tiled=True)
    value_piece = lax.all_gather(qkv_here[:, 2], ("seq", "fsdp"), axis=0, tiled=True)
    live_piece = lax.all_gather(live_mark, ("seq", "fsdp"), axis=0, tiled=True)
    row_count = key_piece.shape[0]
    scores = jnp.einsum(
        "qhd,khd->qhk",
        queries,
        key_piece.reshape(row_count, HEAVY_HEADS, HEAD_DIM),
        preferred_element_type=jnp.float32,
    ) / math.sqrt(HEAD_DIM)
    usable = (live_piece > 0.5)[None, None, :]
    new_max = jnp.maximum(run_max, jnp.max(jnp.where(usable, scores, -1e30), axis=2))
    expons = jnp.where(usable, jnp.exp(scores - new_max[:, :, None]), 0.0)
    new_sum = jnp.sum(expons, axis=2)
    added = jnp.einsum(
        "qhk,khd->qhd",
        expons.astype(jnp.bfloat16),
        value_piece.reshape(row_count, HEAVY_HEADS, HEAD_DIM),
        preferred_element_type=jnp.float32,
    )
    result = (added / new_sum[:, :, None]).reshape(slot_count, width)
    return jnp.where(slot_live[:, None], result, 0.0).astype(jnp.bfloat16)


def shards(
    tokens, ffn_gain, in_proj, out_proj, router_score, tile_counts, tile_order, light_qkv, heavy_qkv
):
    tokens_doc = tokens[0]
    width = tokens_doc.shape[1]
    counts_here = tile_counts[0]
    tiles_here = counts_here.shape[0]
    ranks = jnp.arange(CAP)
    slot_live = (ranks[None, :] < counts_here[:, None]).reshape(-1)
    picker = (tile_order[0][:, :CAP, None] == jnp.arange(TILE)[None, None, :]).astype(jnp.bfloat16)
    tile_rows = tokens_doc.reshape(tiles_here, TILE, width)
    slot_rows = jnp.einsum(
        "tri,tid->trd", picker, tile_rows, preferred_element_type=jnp.float32
    ).reshape(tiles_here * CAP, width)
    slot_score = jnp.einsum(
        "tri,ti->tr",
        picker,
        router_score[0].reshape(tiles_here, TILE),
        preferred_element_type=jnp.float32,
    ).reshape(-1)
    normed = (
        slot_rows
        * lax.rsqrt(jnp.mean(slot_rows * slot_rows, axis=1, keepdims=True) + 1e-06)
        * ffn_gain
    ).astype(jnp.bfloat16)
    light_out = light_branch(light_qkv[0])
    heavy_attn = heavy_branch(heavy_qkv[0], slot_live)
    in_units, out_units = (
        lax.all_gather(in_proj, ("dp", "fsdp"), axis=1, tiled=True),
        lax.all_gather(out_proj, ("dp", "fsdp"), axis=0, tiled=True),
    )
    hidden = jnp.maximum(
        jnp.dot(
            lax.all_gather(normed, "seq", axis=0, tiled=True),
            in_units,
            preferred_element_type=jnp.float32,
        ),
        0.0,
    ).astype(jnp.bfloat16)
    summed = lax.psum_scatter(
        jnp.dot(hidden, out_units, preferred_element_type=jnp.float32).astype(jnp.bfloat16),
        "seq",
        scatter_dimension=0,
        tiled=True,
    ).astype(jnp.float32)
    heavy_ffn = jnp.where(slot_live[:, None], slot_score[:, None] * summed, 0.0).astype(
        jnp.bfloat16
    )
    return (light_out[None], heavy_attn[None], heavy_ffn[None])


def solution(mesh):
    placed = (
        P("dp", ("seq", "fsdp"), None),
        P(),
        P(None, ("dp", "seq", "fsdp")),
        P(("dp", "seq", "fsdp"), None),
        P("dp", ("seq", "fsdp")),
        P("dp", ("seq", "fsdp")),
        P("dp", ("seq", "fsdp"), None),
        P("dp", ("seq", "fsdp"), None, None),
        P("dp", ("seq", "fsdp"), None, None),
    )
    return jax.shard_map(
        shards,
        mesh=mesh,
        in_specs=placed,
        out_specs=(
            P("dp", ("seq", "fsdp"), None),
            P("dp", ("seq", "fsdp"), None),
            P("dp", ("seq", "fsdp"), None),
        ),
        check_vma=False,
    )
```

profile of v0, /device:TPU:0, one launch (start us, length us, event | category | flops | bytes accessed | tf_op | source)
XLA Modules:
  0.0 398.0 jit_solution(1989799292827402582)
XLA Ops:
  8.7 1.9 copy.24
  10.6 1.7 fusion.50
  12.3 1.5 copy.26
  13.9 1.3 collective-permute-start.1
  15.2 2.4 copy.25
  17.6 4.0 collective-permute-start
  22.4 1.0 slice.46
  25.1 17.3 %all-gather.2 = bf16[4,12,4096]{2,1,0:T(8,128)(2,1)S(1)} all-gather(bf16[1,12,4096]{2,1,0:T(8,128)(2,1)S(1)} %fusion.22), channel_id=1, replica_groups=mesh['dp'=4,'seq'=4,'fsdp'=2] {'seq'}, dimensions={0}, use_global_device_ids=true | all-gather | bytes 491520 | tf_op jit(solution)/shard_map/all_gather | solution.py:134
  42.5 16.4 %all-gather.1 = bf16[96,1,2048]{2,1,0:T(2,128)(2,1)S(1)} all-gather(bf16[12,1,2048]{2,1,0:T(2,128)(2,1)S(1)} %get-tuple-element.41), channel_id=3, replica_groups=mesh['dp'=4,'seq'=4,'fsdp'=2] {'seq','fsdp'}, dimensions={0}, use_global_device_ids=true | all-gather | bytes 442368 | tf_op jit(solution)/shard_map/all_gather | solution.py:78
  58.8 2.3 reduce.2
  61.2 15.5 %all-gather = bf16[96,1,2048]{2,1,0:T(2,128)(2,1)S(1)} all-gather(bf16[12,1,2048]{2,1,0:T(2,128)(2,1)S(1)} %get-tuple-element.42), channel_id=2, replica_groups=mesh['dp'=4,'seq'=4,'fsdp'=2] {'seq','fsdp'}, dimensions={0}, use_global_device_ids=true | all-gather | bytes 442368 | tf_op jit(solution)/shard_map/all_gather | solution.py:77
  76.7 2.3 reduce
  80.5 17.9 %all-reduce = bf16[96]{0:T(256)(128)(2,1)S(1)} all-reduce(bf16[96]{0:T(256)(128)(2,1)S(1)} %dynamic-update-slice), channel_id=1, replica_groups=mesh['dp'=4,'seq'=4,'fsdp'=2] {'seq','fsdp'}, use_global_device_ids=true, to_apply=%add | all-reduce | flops 96 | bytes 384
  102.3 1.5 copy.28
  103.9 1.5 copy.27
  105.4 1.2 pad_maximum_fusion
  107.7 2.2 fusion.51
  109.9 70.0 %all-gather.6.cloned.1.call-done = bf16[4096,4096]{1,0:T(8,128)(2,1)} async-done(((bf16[4096,512]{1,0:T(8,128)(2,1)}), bf16[4096,4096]{1,0:T(8,128)(2,1)}) %all-gather.6.cloned.1.call-update) | async-done | bytes 33554448 | tf_op jit(solution)/shard_map/all_gather | solution.py:129
  180.0 162.6 %all-gather.8.cloned.1.call-done = bf16[4096,4096]{1,0:T(8,128)(2,1)} async-done(((bf16[512,4096]{1,0:T(8,128)(2,1)}), bf16[4096,4096]{1,0:T(8,128)(2,1)}) %all-gather.8.cloned.1.call-update) | async-done | bytes 33554448 | tf_op jit(solution)/shard_map/all_gather | solution.py:130
  342.5 24.2 %convolution_convert_fusion = bf16[48,4096]{1,0:T(8,128)(2,1)S(1)} fusion(bf16[4096,4096]{1,0:T(8,128)(2,1)} %all-gather.8.cloned.1.call-done, bf16[48,4096]{1,0:T(8,128)(2,1)S(1)} %reshape.252, bf16[4096,4096]{1,0:T(8,128)(2,1)} %all-gather.6.cloned.1.call-done), kind=kOutput, calls=%fused_computation.3 | convolution fusion | flops 3221815296 | bytes 67895296 | tf_op jit(solution)/shard_map/dot_general | solution.py:141
  366.8 18.7 %fusion = bf16[16,4096]{1,0:T(8,128)(2,1)S(1)} fusion(bf16[48,4096]{1,0:T(8,128)(2,1)S(1)} %convolution_convert_fusion), kind=kCustom, calls=%all-reduce-scatter | all-reduce-scatter fusion | flops 262145 | bytes 524800
  385.5 1.8 collective-permute-start.2
  387.3 1.7 fusion.8
  389.1 1.0 copy.36
  (60 shorter events, 9.6 us)
Async XLA Ops:
  7.2 17.4 %copy-start = (bf16[1,128,4096]{2,1,0:T(8,128)(2,1)S(1)}, bf16[1,128,4096]{2,1,0:T(8,128)(2,1)}, u32[]{:S(2)}) copy-start(bf16[1,128,4096]{2,1,0:T(8,128)(2,1)} %param.9) | copy-start | bytes 3145732
  7.2 172.8 %all-gather.6.cloned.1.call-start = ((), (), s32[]{:S(2)}) async-start(), calls=%async_computation | async-start | bytes 37748736 | tf_op jit(solution)/shard_map/all_gather | solution.py:129
  7.9 334.6 %all-gather.8.cloned.1.call-start = ((), (), s32[]{:S(2)}) async-start(), calls=%async_computation.1 | async-start | bytes 37748736 | tf_op jit(solution)/shard_map/all_gather | solution.py:130
  13.9 88.5 %collective-permute-start.1 = (bf16[64,2,2048]{2,0,1:T(8,128)(2,1)S(1)}, bf16[64,2,2048]{2,0,1:T(8,128)(2,1)}, u32[]{:S(2)}, u32[]{:S(2)}) collective-permute-start(bf16[64,2,2048]{2,0,1:T(8,128)(2,1)S(1)} %copy.26), channel_id=1, source_target_pairs={{1,0},{2,1},{3,2},{4,3},{5,4},{6,5},{7,6},{9,8},{10,9},{11,10},{12... | collective-permute-start | bytes 1572872 | tf_op jit(solution)/shard_map/ppermute | solution.py:24
  15.2 8.9 %copy-start.4 = (bf16[1,12,3,2048]{3,2,1,0:T(4,128)(2,1)S(1)}, bf16[1,12,3,2048]{3,2,1,0:T(4,128)(2,1)}, u32[]{:S(2)}) copy-start(bf16[1,12,3,2048]{3,2,1,0:T(4,128)(2,1)} %param.17) | copy-start | bytes 442372
  17.5 7.0 %copy-start.8 = (s32[1,1,128]{2,1,0:T(1,128)S(1)}, s32[1,1,128]{2,1,0:T(1,128)}, u32[]{:S(2)}) copy-start(s32[1,1,128]{2,1,0:T(1,128)} %param.15) | copy-start | bytes 1540
  17.6 86.3 %collective-permute-start = (bf16[64,2,2048]{2,0,1:T(8,128)(2,1)}, bf16[64,2,2048]{2,0,1:T(8,128)(2,1)}, u32[]{:S(2)}, u32[]{:S(2)}) collective-permute-start(bf16[64,2,2048]{2,0,1:T(8,128)(2,1)} %copy.25), channel_id=1, source_target_pairs={{0,1},{1,2},{2,3},{3,4},{4,5},{5,6},{6,7},{8,9},{9,10},{10,11},{11... | collective-permute-start | bytes 1572872 | tf_op jit(solution)/shard_map/ppermute | solution.py:23
  22.4 2.6 copy-start.6
  42.5 36.5 %copy-start.10 = (u32[32]{0:T(128)S(1)}, u32[32]{0:T(128)}, u32[]{:S(2)}) copy-start(u32[32]{0:T(128)} %constant.68) | copy-start | bytes 388
  61.1 38.3 %copy-start.7 = (u32[32]{0:T(128)S(1)}, u32[32]{0:T(128)}, u32[]{:S(2)}) copy-start(u32[32]{0:T(128)} %constant.74) | copy-start | bytes 388
  61.1 39.5 %copy-start.9 = (bf16[1,128]{1,0:T(2,128)(2,1)S(1)}, bf16[1,128]{1,0:T(2,128)(2,1)}, u32[]{:S(2)}) copy-start(bf16[1,128]{1,0:T(2,128)(2,1)} %param.13) | copy-start | bytes 772
  99.0 6.4 %copy-start.2 = (bf16[128,2,2048]{0,2,1:T(8,128)(2,1)S(1)}, bf16[128,2,2048]{0,2,1:T(8,128)(2,1)}, u32[]{:S(2)}) copy-start(bf16[128,2,2048]{0,2,1:T(8,128)(2,1)} %slice.46) | copy-start | bytes 3145732
  106.6 1.0 copy-start.3
  106.7 1.0 copy-start.5
  385.5 4.5 %collective-permute-start.2 = (bf16[12,4096]{1,0:T(8,128)(2,1)S(1)}, bf16[12,4096]{1,0:T(8,128)(2,1)S(1)}, u32[]{:S(2)}, u32[]{:S(2)}) collective-permute-start(bf16[12,4096]{1,0:T(8,128)(2,1)S(1)} %slice.54), channel_id=1, source_target_pairs={{0,2},{2,4},{4,6},{1,3},{3,5},{5,7},{8,10},{10,12},{12,14},{9,11},... | collective-permute-start | bytes 294920
  387.3 3.8 copy-start.1
Sparse Core Ops, SparseCore 0:
  9.9 170.0 all-gather.5
  181.8 160.6 all-gather.7
where the time goes:
time: 398 us
  waiting for transfers between devices  234 us (59%)
  blocking collectives  85.7 us (22%)
  matrix products  29.5 us (7%)
  local copies, waits for them, and re-layouts  16.9 us (4%)
  between operations  16.4 us (4%)
  other arithmetic  8.4 us (2%)
  starting transfers between devices  7.11 us (2%)
    all_gather x1, waiting for transfers between devices, shards(): lax.all_gather(out_proj, ('dp', 'fsdp'), axis=0, tiled=True)  163 us
    all_gather x1, waiting for transfers between devices, shards(): lax.all_gather(in_proj, ('dp', 'fsdp'), axis=1, tiled=True)  70 us
    unnamed x2, blocking collectives  36.6 us
    dot_general x1, matrix products, shards(): jnp.dot(hidden, out_units, preferred_element_type=jnp.float32)  24.2 us
    all_gather x1, blocking collectives, shards(): lax.all_gather(normed, 'seq', axis=0, tiled=True)  17.3 us
    all_gather x1, blocking collectives, heavy_branch(): lax.all_gather(qkv_here[:, 2], ('seq', 'fsdp'), axis=0, tiled=True)  16.4 us
    all_gather x1, blocking collectives, heavy_branch(): lax.all_gather(qkv_here[:, 1], ('seq', 'fsdp'), axis=0, tiled=True)  15.5 us
  transfers between devices with their start and end apart: 5, of which 2 were waited for; matrix products, arithmetic and copies ran while one was open for 7% of the time, Pallas kernels for 0%

commit v1 on v0

v1 whole, which is shorter than its diff:
```python
import functools
import math

import jax
import jax.numpy as jnp
from jax import lax
from jax.experimental import pallas as pl
from jax.experimental.pallas import tpu as pltpu
from jax.sharding import PartitionSpec as P

HEAD_DIM = 128
LIGHT_HEADS = 16
HEAVY_HEADS = 16
TILE = 128
CAP = 12
MEAN_LIVE = 8
HALF_WIN = 64
MARK = 1048576.0
F32, BF16 = jnp.float32, jnp.bfloat16
VMEM = pl.BlockSpec(memory_space=pltpu.VMEM)
SMEM = pl.BlockSpec(memory_space=pltpu.SMEM)


def iota(shape, dim):
    return lax.broadcasted_iota(jnp.int32, shape, dim)


def call(body, outs, args, scalars, flops, **kw):
    size = sum(math.prod(a.shape) * a.dtype.itemsize for a in (*args, *outs))
    return pl.pallas_call(
        body,
        out_shape=outs,
        in_specs=[SMEM] * scalars + [VMEM] * (len(args) - scalars),
        out_specs=[VMEM] * len(outs),
        cost_estimate=pl.CostEstimate(flops=flops, bytes_accessed=size, transcendentals=0),
        **kw,
    )(*args)


def struct(shape, dtype=BF16):
    return jax.ShapeDtypeStruct(shape, dtype)


def swap_core(x):
    return lax.ppermute(x, "fsdp", [(0, 1), (1, 0)])


def swap_seq(x, mask):
    n = lax.axis_size("seq")
    return lax.ppermute(x, "seq", [(i, i ^ mask) for i in range(n)])


def swap_doc(x, first):
    masks = (2, 1) if first else (1, 2)
    pairs = [(2 * d + c, 2 * (d ^ masks[c]) + c) for d in range(lax.axis_size("dp")) for c in range(2)]
    return lax.ppermute(x, ("dp", "fsdp"), pairs)


def seq_stages():
    n, stride, out = lax.axis_size("seq"), 1, []
    while stride < n:
        radix = min(4, n // stride)
        out.append((stride, radix))
        stride *= radix
    return out


def gather_seq(x):
    parts = [x]
    for stride, radix in seq_stages():
        x = jnp.concatenate(parts, axis=0) if len(parts) > 1 else parts[0]
        parts = [x] + [swap_seq(x, k * stride) for k in range(1, radix)]
    return parts


def scatter_seq(parts):
    stages = seq_stages()
    for at in range(len(stages) - 1, -1, -1):
        stride, radix = stages[at]
        total = parts[0].astype(F32)
        for k in range(1, radix):
            total = total + swap_seq(parts[k], k * stride).astype(F32)
        total = total.astype(BF16)
        if at:
            parts = jnp.split(total, stages[at - 1][1], axis=0)
    return total


def slot_rows_of(order_ref, rows, shift):
    lanes = iota((rows, TILE), 1)
    wanted = iota((rows, TILE), 0) - shift
    order = jnp.broadcast_to(order_ref[...], (rows, TILE))
    return jnp.sum(jnp.where(lanes == wanted, order, 0), axis=1, keepdims=True)


def pick_kernel(core_ref, count_ref, tokens_ref, order_ref, gain_ref, mine_ref, send_ref, all_ref):
    rows, half = mine_ref.shape
    core = core_ref[0]
    shift = core * CAP
    slot = iota((rows, 1), 0) - shift
    own = (slot >= 0) & (slot < CAP)
    picker = (slot_rows_of(order_ref, rows, shift) == iota((rows, TILE), 1)) & own
    x = jnp.dot(picker.astype(BF16), tokens_ref[...], preferred_element_type=F32)
    scale = lax.rsqrt(jnp.mean(x * x, axis=1, keepdims=True) + 1e-06)
    dead = own & (slot >= count_ref[0, 0])
    all_ref[...] = jnp.where(dead, MARK, x * scale * gain_ref[...]).astype(BF16)
    mine_ref[...] = all_ref[:, pl.ds(pl.multiple_of(core * half, 128), half)]
    send_ref[...] = all_ref[:, pl.ds(pl.multiple_of((1 - core) * half, 128), half)]


def pick_rows(core, counts, tokens, order, gain):
    rows, width = 2 * CAP, tokens.shape[1]
    return call(
        pick_kernel,
        [struct((rows, width // 2))] * 2,
        [core, counts, tokens, order, gain],
        2,
        2 * rows * TILE * width,
        scratch_shapes=[pltpu.VMEM((rows, width), BF16)],
    )


def compact_kernel(parts, *refs):
    ins, (out_ref, place_ref) = refs[:parts], refs[parts:]
    live_rows, width = out_ref.shape
    n = ins[0].shape[0]
    up, side = iota((n, n), 0), iota((n, n), 1)
    base = jnp.zeros((1, 1), F32)
    total = jnp.zeros((live_rows, width), F32)
    for k, ref in enumerate(ins):
        live = jnp.where(ref[:, 0:128].astype(F32)[:, 0:1] < MARK / 2, 1.0, 0.0)
        live_row = jnp.sum(jnp.where(up == side, live, 0.0), axis=0, keepdims=True)
        ahead_row = jnp.sum(jnp.where(up < side, live, 0.0), axis=0, keepdims=True) + base
        ahead = jnp.sum(jnp.where(side < up, live_row, 0.0), axis=1, keepdims=True) + base
        to_row = iota((live_rows, n), 0).astype(F32) == ahead_row
        pick = jnp.where(to_row & (live_row > 0.5), 1.0, 0.0).astype(BF16)
        total = total + jnp.dot(pick, ref[...], preferred_element_type=F32)
        at = iota((n, live_rows), 1).astype(F32) == ahead
        place_ref[k, :, :] = jnp.where(at & (live > 0.5), 1.0, 0.0).astype(BF16)
        base = base + jnp.sum(live, axis=0, keepdims=True)
    out_ref[...] = total.astype(BF16)


def compact(parts, live_rows):
    n, width = parts[0].shape
    return call(
        functools.partial(compact_kernel, len(parts)),
        [struct((live_rows, width)), struct((len(parts), n, live_rows))],
        parts,
        0,
        2 * len(parts) * n * live_rows * width,
    )


def spread_kernel(parts, place_ref, rows_ref, *outs):
    for k in range(parts):
        outs[k][...] = jnp.dot(
            place_ref[k, :, :], rows_ref[...], preferred_element_type=F32
        ).astype(BF16)


def spread(place, rows):
    parts, n, live_rows = place.shape
    width = rows.shape[1]
    return call(
        functools.partial(spread_kernel, parts),
        [struct((n, width))] * parts,
        [place, rows],
        0,
        2 * parts * n * live_rows * width,
    )


def ffn_kernel(core_ref, *refs):
    mine, peer, (win_ref, wout_ref), send, keep = (
        refs[0:4],
        refs[4:8],
        refs[8:10],
        refs[10:14],
        refs[14:18],
    )
    core = core_ref[0]
    rows, half = mine[0].shape
    units = win_ref.shape[1]
    at_mine = pl.multiple_of(core * half, 128)
    at_peer = pl.multiple_of((1 - core) * half, 128)
    group = max(1, min(4, 256 // rows))
    step = 256
    for first in range(0, 4, group):
        roles = range(first, first + group)
        x_mine = jnp.concatenate([mine[r][...] for r in roles], axis=0)
        x_peer = jnp.concatenate([peer[r][...] for r in roles], axis=0)
        total = jnp.dot(x_mine, win_ref[pl.ds(at_mine, half), :], preferred_element_type=F32)
        total = total + jnp.dot(x_peer, win_ref[pl.ds(at_peer, half), :], preferred_element_type=F32)
        hidden = jnp.maximum(total, 0.0).astype(BF16)

        def columns(i, carry, hidden=hidden, roles=roles):
            off = pl.multiple_of(i * step, step)
            for start, targets in ((at_peer, send), (at_mine, keep)):
                y = jnp.dot(
                    hidden, wout_ref[:, pl.ds(start + off, step)], preferred_element_type=F32
                ).astype(BF16)
                for j, r in enumerate(roles):
                    targets[r][:, pl.ds(off, step)] = y[j * rows : (j + 1) * rows]
            return carry

        lax.fori_loop(0, half // step, columns, 0)


def ffn(core, mine, peer, win, wout):
    rows, half = mine[0].shape
    units = win.shape[1]
    outs = call(
        ffn_kernel,
        [struct((rows, half))] * 8,
        [core, *mine, *peer, win, wout],
        1,
        4 * 4 * rows * 2 * half * units,
    )
    return outs[:4], outs[4:]


def finish_kernel(core_ref, count_ref, mine_ref, peer_ref, order_ref, score_ref, out_ref):
    rows, half = mine_ref.shape
    core = core_ref[0]
    pick = (iota((CAP, rows), 1) == iota((CAP, rows), 0) + core * CAP).astype(BF16)
    at = slot_rows_of(order_ref, CAP, 0) == iota((CAP, TILE), 1)
    score = jnp.sum(jnp.where(at, score_ref[...].astype(F32), 0.0), axis=1, keepdims=True)
    score = jnp.where(iota((CAP, 1), 0) < count_ref[0, 0], score, 0.0)
    for ref, start in ((mine_ref, core * half), (peer_ref, (1 - core) * half)):
        y = jnp.dot(pick, ref[...], preferred_element_type=F32)
        out_ref[:, pl.ds(pl.multiple_of(start, 128), half)] = (score * y).astype(BF16)


def finish(core, counts, mine, peer, order, score):
    rows, half = mine.shape
    return call(
        finish_kernel,
        [struct((CAP, 2 * half))],
        [core, counts, mine, peer, order, score],
        2,
        4 * CAP * rows * half,
    )[0]


def routed_ffn(core, tokens, gain, win, wout, score, counts, order):
    devices = lax.axis_size("seq") * lax.axis_size("fsdp")
    mine, send = pick_rows(core, counts, tokens, order, gain)
    pair = mine + swap_core(send)
    x0, place = compact(gather_seq(pair), MEAN_LIVE * devices)
    x1 = swap_doc(x0, True)
    x2 = swap_doc(x0, False)
    x3 = swap_doc(x1, False)
    mine = (x0, x1, x2, x3)
    p0, p2, p1, p3 = [swap_core(x) for x in mine]
    send, keep = ffn(core, mine, (p0, p1, p2, p3), win, wout)
    back = [swap_core(s) for s in send]

    def total(*terms):
        return sum(t.astype(F32) for t in terms).astype(BF16)

    got1 = swap_doc(total(keep[3], back[3]), True)
    got2 = swap_doc(total(keep[1], back[2]), True)
    got3 = swap_doc(total(keep[2], back[1], got1), False)
    own = total(keep[0], back[0], got2, got3)
    summed = scatter_seq(spread(place, own))
    return finish(core, counts, summed, swap_core(summed), order, score)


def light_kernel(info_ref, qkv_ref, far_ref, near_ref, out_ref):
    rows = qkv_ref.shape[1]
    core, first_pos, length = info_ref[0], info_ref[1], info_ref[2]
    span = rows + 2 * HALF_WIN
    lane = iota((rows, span), 1)
    row = iota((rows, span), 0)
    turn = jnp.where(core == 0, 0, rows + HALF_WIN)
    col = jnp.where(
        lane < HALF_WIN,
        lane + turn,
        jnp.where(lane < HALF_WIN + rows, lane, lane - turn),
    )
    pos = first_pos - HALF_WIN + col
    inside = (col >= row) & (col < row + 2 * HALF_WIN) & (pos >= 0) & (pos < length)
    bias = jnp.where(inside, 0.0, -1e30)
    for h in range(out_ref.shape[1] // HEAD_DIM):
        at = slice(h * HEAD_DIM, (h + 1) * HEAD_DIM)
        keys = jnp.concatenate([far_ref[0, :, at], qkv_ref[1, :, at], near_ref[0, :, at]], axis=0)
        values = jnp.concatenate([far_ref[1, :, at], qkv_ref[2, :, at], near_ref[1, :, at]], axis=0)
        s = lax.dot_general(
            qkv_ref[0, :, at], keys, (((1,), (1,)), ((), ())), preferred_element_type=F32
        )
        s = s * (1.0 / math.sqrt(HEAD_DIM)) + bias
        e = jnp.exp(s - jnp.max(s, axis=1, keepdims=True))
        y = jnp.dot(e.astype(BF16), values, preferred_element_type=F32)
        out_ref[:, at] = (y / jnp.sum(e, axis=1, keepdims=True)).astype(BF16)


def light_branch(core, qkv):
    rows, _, width = qkv.shape
    planes = jnp.transpose(qkv, (1, 0, 2))
    last = rows - HALF_WIN
    edge = core[0] * last
    far = lax.dynamic_slice(planes, (1, edge, 0), (2, HALF_WIN, width))
    near = lax.dynamic_slice(planes, (1, last - edge, 0), (2, HALF_WIN, width))
    n = lax.axis_size("seq") * lax.axis_size("fsdp")
    pairs = [(i, i + 1) for i in range(1, n - 1, 2)]
    far = lax.ppermute(far, ("seq", "fsdp"), pairs + [(j, i) for i, j in pairs])
    near = swap_core(near)
    first_pos = lax.axis_index(("seq", "fsdp")) * rows
    info = jnp.stack([core[0], first_pos, jnp.int32(n * rows)])
    wide = 4 * HEAD_DIM
    return pl.pallas_call(
        light_kernel,
        out_shape=struct((rows, width)),
        grid=(width // wide,),
        in_specs=[
            SMEM,
            pl.BlockSpec((3, rows, wide), lambda i: (0, 0, i)),
            pl.BlockSpec((2, HALF_WIN, wide), lambda i: (0, 0, i)),
            pl.BlockSpec((2, HALF_WIN, wide), lambda i: (0, 0, i)),
        ],
        out_specs=pl.BlockSpec((rows, wide), lambda i: (0, i)),
        cost_estimate=pl.CostEstimate(
            flops=4 * rows * 2 * rows * width,
            bytes_accessed=12 * rows * width,
            transcendentals=2 * rows * rows * LIGHT_HEADS,
        ),
    )(info, planes, far, near)


def heavy_kernel(q_ref, near_ref, far_ref, out_ref):
    rows, width = q_ref.shape
    n = 2 * near_ref.shape[0]
    kv = jnp.concatenate([near_ref[...], far_ref[...]], axis=0)
    first = (iota((8, HEAD_DIM), 1) == 0).astype(BF16)
    marks = lax.dot_general(
        first, kv[:, :HEAD_DIM], (((1,), (1,)), ((), ())), preferred_element_type=F32
    )[0:1]
    lane, row = iota((rows, n), 1), iota((rows, n), 0)
    same = (lax.rem(lane, 2 * CAP) < CAP) == (row < CAP)
    usable = same & (marks < MARK / 2)
    for h in range(width // HEAD_DIM):
        at = slice(h * HEAD_DIM, (h + 1) * HEAD_DIM)
        s = lax.dot_general(
            q_ref[:, at], kv[:, at], (((1,), (1,)), ((), ())), preferred_element_type=F32
        )
        s = jnp.where(usable, s * (1.0 / math.sqrt(HEAD_DIM)), -1e30)
        e = jnp.exp(s - jnp.max(s, axis=1, keepdims=True))
        y = jnp.dot(
            e.astype(BF16),
            kv[:, width + h * HEAD_DIM : width + (h + 1) * HEAD_DIM],
            preferred_element_type=F32,
        )
        out_ref[:, at] = (y / jnp.sum(e, axis=1, keepdims=True)).astype(BF16)


def heavy_branch(qkv, slot_live):
    slots, _, width = qkv.shape
    half = width // 2

    def stacked(x):
        return jnp.concatenate([x[:, :half], x[:, half:]], axis=0)

    q = stacked(qkv[:, 0])
    keys = jnp.where(slot_live[:, None], qkv[:, 1], jnp.bfloat16(MARK))
    kv = jnp.concatenate([stacked(keys), stacked(qkv[:, 2])], axis=1)
    near = jnp.concatenate(gather_seq(kv), axis=0)
    far = swap_core(near)
    out = call(
        heavy_kernel,
        [struct((2 * slots, half))],
        [q, near, far],
        0,
        4 * 2 * slots * 2 * near.shape[0] * half,
    )[0]
    out = jnp.concatenate([out[:slots], out[slots:]], axis=1)
    return jnp.where(slot_live[:, None], out, jnp.bfloat16(0))


def shards(
    tokens, ffn_gain, in_proj, out_proj, router_score, tile_counts, tile_order, light_qkv, heavy_qkv
):
    assert tile_order.shape[1] == 1 and lax.axis_size("fsdp") == 2 and lax.axis_size("dp") == 4
    core = lax.axis_index("fsdp").astype(jnp.int32).reshape(1)
    slot_live = jnp.arange(CAP) < tile_counts[0, 0]
    heavy_ffn = routed_ffn(
        core,
        tokens[0],
        ffn_gain[None],
        in_proj,
        out_proj,
        router_score,
        tile_counts,
        tile_order[0],
    )
    light_out = light_branch(core, light_qkv[0])
    heavy_attn = heavy_branch(heavy_qkv[0], slot_live)
    return (light_out[None], heavy_attn[None], heavy_ffn[None])


def solution(mesh):
    placed = (
        P("dp", ("seq", "fsdp"), None),
        P(),
        P(None, ("dp", "seq", "fsdp")),
        P(("dp", "seq", "fsdp"), None),
        P("dp", ("seq", "fsdp")),
        P("dp", ("seq", "fsdp")),
        P("dp", ("seq", "fsdp"), None),
        P("dp", ("seq", "fsdp"), None, None),
        P("dp", ("seq", "fsdp"), None, None),
    )
    return jax.shard_map(
        shards,
        mesh=mesh,
        in_specs=placed,
        out_specs=(
            P("dp", ("seq", "fsdp"), None),
            P("dp", ("seq", "fsdp"), None),
            P("dp", ("seq", "fsdp"), None),
        ),
        check_vma=False,
    )
```

time: 398 us -> 102 us (0.26)
  waiting for transfers between devices: 234 us -> 28.8 us
  blocking collectives: 85.7 us -> 0 us
  matrix products: 29.5 us -> 0 us
  Pallas kernels: 0 us -> 26.2 us
  starting transfers between devices: 7.11 us -> 25.8 us
  between operations: 16.4 us -> 1.56 us
  local copies, waits for them, and re-layouts: 16.9 us -> 6.92 us
    all_gather x2 -> x0, waiting for transfers between devices: 233 us -> none  [the longest x1 163 us: shards(): lax.all_gather(out_proj, ('dp', 'fsdp'), axis=0, tiled=True)]
    all_gather x3 -> x0, blocking collectives: 49.2 us -> none  [the longest x1 17.3 us: shards(): lax.all_gather(normed, 'seq', axis=0, tiled=True)]
    unnamed x2 -> x0, blocking collectives: 36.6 us -> none
    ppermute x2 -> x28, waiting for transfers between devices: 0.01 us -> 28.8 us  [the longest x9 14.1 us: swap_seq(): return lax.ppermute(x, 'seq', [(i, i ^ mask) for i in range(n)])]
    dot_general x6 -> x0, matrix products: 27.2 us -> none  [the longest x1 24.2 us: shards(): jnp.dot(hidden, out_units, preferred_element_type=jnp.float32)]
    pallas_call x0 -> x7, Pallas kernels: none -> 26.2 us  [the longest x6 21.1 us: call(): pl.pallas_call(body, out_shape=outs, in_specs=[SMEM] * scalars + [VMEM] *...]
    ppermute x2 -> x28, starting transfers between devices: 5.26 us -> 25.8 us  [the longest x9 15.2 us: swap_seq(): return lax.ppermute(x, 'seq', [(i, i ^ mask) for i in range(n)])]
    slice x8 -> x2, local copies, waits for them, and re-layouts: 8.08 us -> 0.63 us  [stacked(): return jnp.concatenate([x[:, :half], x[:, half:]], axis=0)]
  transfers between devices with their start and end apart: 5 -> 28, of which waited for: 2 -> 7; matrix products, arithmetic and copies ran while one was open for 7% -> 14% of each run, Pallas kernels for 0% -> 20%
where the time goes in v1:
time: 102 us; the launch traced here: 101 us
  waiting for transfers between devices  28.8 us (28%)
  Pallas kernels  26.2 us (26%)
  starting transfers between devices  25.8 us (25%)
  other arithmetic  12.1 us (12%)
  local copies, waits for them, and re-layouts  6.92 us (7%)
  between operations  1.56 us (2%)
    pallas_call x6, Pallas kernels, call(): pl.pallas_call(body, out_shape=outs, in_specs=[SMEM] * scalars + [VMEM] *...  21.1 us
    ppermute x9, starting transfers between devices, swap_seq(): return lax.ppermute(x, 'seq', [(i, i ^ mask) for i in range(n)])  15.2 us
    ppermute x9, waiting for transfers between devices, swap_seq(): return lax.ppermute(x, 'seq', [(i, i ^ mask) for i in range(n)])  14.1 us
    ppermute x6, waiting for transfers between devices, swap_doc(): return lax.ppermute(x, ('dp', 'fsdp'), pairs)  13.4 us
    convert_element_type x4, other arithmetic, total(): return sum((t.astype(F32) for t in terms)).astype(BF16)  6.55 us
    ppermute x6, starting transfers between devices, swap_doc(): return lax.ppermute(x, ('dp', 'fsdp'), pairs)  5.75 us
    unnamed x41, local copies, waits for them, and re-layouts  5.34 us
    pallas_call x1, Pallas kernels, light_branch(): pl.pallas_call(light_kernel, out_shape=struct((rows, width)), grid=(width...  5.07 us
  transfers between devices with their start and end apart: 28, of which 7 were waited for; matrix products, arithmetic and copies ran while one was open for 14% of the time, Pallas kernels for 20%

profile of v1, /device:TPU:0, one launch (start us, length us, event | category | flops | bytes accessed | tf_op | source)
XLA Modules:
  0.0 101.4 jit_solution(9775061867807695063)
XLA Ops:
  1.3 2.4 %shard_map.114 = (bf16[24,2048]{1,0:T(8,128)(2,1)}, bf16[24,2048]{1,0:T(8,128)(2,1)}) custom-call(s32[1]{0:T(128)} %bitcast.core_ref, s32[1,1]{1,0:T(1,128)} %copy.15.count_ref, bf16[128,4096]{1,0:T(8,128)(2,1)} %bitcast.36, s32[1,128]{1,0:T(1,128)} %bitcast.42, f32[1,4096]{1,0:T(1,128)} %bitcast.41), custom_call_target="tpu_custom_call" | custom-call | flops 25165824 | bytes 1262088 | tf_op jit(solution)/shard_map/pallas_call | solution.py:30
  6.3 3.0 %collective-permute-start.7 = (bf16[24,2048]{1,0:T(8,128)(2,1)S(1)}, bf16[24,2048]{1,0:T(8,128)(2,1)S(1)}, u32[]{:S(2)}, u32[]{:S(2)}) collective-permute-start(bf16[24,2048]{1,0:T(8,128)(2,1)S(1)} %add.46.refs_0_), channel_id=1, source_target_pairs={{0,2},{2,0},{4,6},{6,4},{1,3},{3,1},{5,7},{7,5},{8,10},{10,8},{12,... | collective-permute-start | bytes 294920 | tf_op jit(solution)/shard_map/ppermute | solution.py:50
  9.3 2.6 %collective-permute-start.8 = (bf16[24,2048]{1,0:T(8,128)(2,1)S(1)}, bf16[24,2048]{1,0:T(8,128)(2,1)S(1)}, u32[]{:S(2)}, u32[]{:S(2)}) collective-permute-start(bf16[24,2048]{1,0:T(8,128)(2,1)S(1)} %add.46.refs_0_), channel_id=1, source_target_pairs={{0,4},{2,6},{4,0},{6,2},{1,5},{3,7},{5,1},{7,3},{8,12},{10,14},{12... | collective-permute-start | bytes 294920 | tf_op jit(solution)/shard_map/ppermute | solution.py:50
  12.9 7.0 %collective-permute-done.8.refs_2_ = bf16[24,2048]{1,0:T(8,128)(2,1)S(1)} collective-permute-done((bf16[24,2048]{1,0:T(8,128)(2,1)S(1)}, bf16[24,2048]{1,0:T(8,128)(2,1)S(1)}, u32[]{:S(2)}, u32[]{:S(2)}) %collective-permute-start.8) | collective-permute-done | bytes 98336 | tf_op jit(solution)/shard_map/ppermute | solution.py:50
  21.2 2.2 %shard_map.115 = (bf16[64,2048]{1,0:T(8,128)(2,1)}, bf16[4,24,64]{2,1,0:T(8,128)(2,1)}) custom-call(bf16[24,2048]{1,0:T(8,128)(2,1)} %copy-done.5, bf16[24,2048]{1,0:T(8,128)(2,1)} %copy-done.17, bf16[24,2048]{1,0:T(8,128)(2,1)} %copy-done.18, bf16[24,2048]{1,0:T(8,128)(2,1)} %copy-done.19), custom_call_target="tpu_custom_call" | custom-call | flops 25165824 | bytes 667648 | tf_op jit(solution)/shard_map/pallas_call | solution.py:30
  25.0 1.6 %collective-permute-start.11 = (bf16[64,2048]{1,0:T(8,128)(2,1)}, bf16[64,2048]{1,0:T(8,128)(2,1)S(1)}, u32[]{:S(2)}, u32[]{:S(2)}) collective-permute-start(bf16[64,2048]{1,0:T(8,128)(2,1)} %get-tuple-element.22.refs_0_), channel_id=1, source_target_pairs={{0,8},{1,17},{8,0},{9,25},{16,24},{17,1},{24,16},{25,9},{2,10},{3,... | collective-permute-start | bytes 786440 | tf_op jit(solution)/shard_map/ppermute | solution.py:56
  26.6 5.9 %collective-permute-done.10.refs_1_ = bf16[64,2048]{1,0:T(8,128)(2,1)S(1)} collective-permute-done((bf16[64,2048]{1,0:T(8,128)(2,1)}, bf16[64,2048]{1,0:T(8,128)(2,1)S(1)}, u32[]{:S(2)}, u32[]{:S(2)}) %collective-permute-start.10) | collective-permute-done | bytes 262176 | tf_op jit(solution)/shard_map/ppermute | solution.py:56
  33.8 5.0 %collective-permute-done.12.refs_3_ = bf16[64,2048]{1,0:T(8,128)(2,1)S(1)} collective-permute-done((bf16[64,2048]{1,0:T(8,128)(2,1)S(1)}, bf16[64,2048]{1,0:T(8,128)(2,1)S(1)}, u32[]{:S(2)}, u32[]{:S(2)}) %collective-permute-start.12) | collective-permute-done | bytes 262176 | tf_op jit(solution)/shard_map/ppermute | solution.py:56
  41.0 1.7 %collective-permute-start.3 = (bf16[24,2048]{1,0:T(8,128)(2,1)}, bf16[24,2048]{1,0:T(8,128)(2,1)}, u32[]{:S(2)}, u32[]{:S(2)}) collective-permute-start(bf16[24,2048]{1,0:T(8,128)(2,1)} %maximum_maximum_fusion), channel_id=1, source_target_pairs={{0,4},{2,6},{4,0},{6,2},{1,5},{3,7},{5,1},{7,3},{8,12},{10,14},{12... | collective-permute-start | bytes 294920 | tf_op jit(solution)/shard_map/ppermute | solution.py:50
  45.3 9.1 %shard_map.116 = (bf16[64,2048]{1,0:T(8,128)(2,1)}, bf16[64,2048]{1,0:T(8,128)(2,1)}, bf16[64,2048]{1,0:T(8,128)(2,1)}, bf16[64,2048]{1,0:T(8,128)(2,1)}, bf16[6...) custom-call(s32[1]{0:T(128)} %bitcast.core_ref, ...), custom_call_target="tpu_custom_call" | custom-call | flops 2147483648 | bytes 12582916 | tf_op jit(solution)/shard_map/pallas_call | solution.py:30
  57.8 1.6 %collective-permute-start.22 = (bf16[64,2048]{1,0:T(8,128)(2,1)S(1)}, bf16[64,2048]{1,0:T(8,128)(2,1)S(1)}, u32[]{:S(2)}, u32[]{:S(2)}) collective-permute-start(bf16[64,2048]{1,0:T(8,128)(2,1)S(1)} %add_convert_fusion.2), channel_id=1, source_target_pairs={{0,16},{1,9},{8,24},{9,1},{16,0},{17,25},{24,8},{25,17},{2,18},{3,... | collective-permute-start | bytes 786440 | tf_op jit(solution)/shard_map/ppermute | solution.py:56
  59.4 1.7 %add_convert_fusion.3 = bf16[64,2048]{1,0:T(8,128)(2,1)} fusion(bf16[64,2048]{1,0:T(8,128)(2,1)S(1)} %collective-permute-done.18, bf16[64,2048]{1,0:T(8,128)(2,1)} %get-tuple-element.25), kind=kLoop, calls=%fused_computation.3 | loop fusion | flops 524288 | bytes 786432 | tf_op jit(solution)/shard_map/convert_element_type | solution.py:260
  61.6 2.6 %collective-permute-done.22 = bf16[64,2048]{1,0:T(8,128)(2,1)S(1)} collective-permute-done((bf16[64,2048]{1,0:T(8,128)(2,1)S(1)}, bf16[64,2048]{1,0:T(8,128)(2,1)S(1)}, u32[]{:S(2)}, u32[]{:S(2)}) %collective-permute-start.22) | collective-permute-done | bytes 262176 | tf_op jit(solution)/shard_map/ppermute | solution.py:56
  64.2 1.8 %add_convert_fusion.1 = bf16[64,2048]{1,0:T(8,128)(2,1)} fusion(bf16[64,2048]{1,0:T(8,128)(2,1)S(1)} %collective-permute-done.22, bf16[64,2048]{1,0:T(8,128)(2,1)S(1)} %collective-permute-done.20, bf16[64,2048]{1,0:T(8,128)(2,1)} %get-tuple-element.27), kind=kLoop, calls=%fused_computation.1 | loop fusion | flops 786432 | bytes 1048576 | tf_op jit(solution)/shard_map/convert_element_type | solution.py:260
  68.5 1.9 %collective-permute-start.1 = (bf16[2,64,2048]{2,1,0:T(8,128)(2,1)S(1)}, bf16[2,64,2048]{2,1,0:T(8,128)(2,1)S(1)}, u32[]{:S(2)}, u32[]{:S(2)}) collective-permute-start(bf16[2,64,2048]{2,1,0:T(8,128)(2,1)S(1)} %get-tuple-element.35), channel_id=1, source_target_pairs={{0,1},{1,0},{2,3},{3,2},{4,5},{5,4},{6,7},{7,6},{8,9},{9,8},{10,11... | collective-permute-start | bytes 1572872 | tf_op jit(solution)/shard_map/ppermute | solution.py:45
  70.4 3.7 %shard_map.113 = bf16[24,1024]{1,0:T(8,128)(2,1)} custom-call(bf16[24,1024]{1,0:T(8,128)(2,1)} %pad_maximum_fusion.1.q_ref, bf16[96,2048]{1,0:T(8,128)(2,1)} %copy-done.1, bf16[96,2048]{1,0:T(8,128)(2,1)} %copy-done.4), custom_call_target="tpu_custom_call" | custom-call | flops 18874368 | bytes 884736 | tf_op jit(solution)/shard_map/pallas_call | solution.py:30
  74.1 2.0 %add_convert_fusion.rows_ref = bf16[64,2048]{1,0:T(8,128)(2,1)} fusion(bf16[64,2048]{1,0:T(8,128)(2,1)} %collective-permute-done.23, bf16[64,2048]{1,0:T(8,128)(2,1)} %collective-permute-done.19, bf16[64,2048]{1,0:T(8,128)(2,1)} %collective-permute-done.17, bf16[64,2048]{1,0:T(8,128)(2,1)} %get-tuple-element.23), kind=kLoop, calls=%fused_computation | loop fusion | flops 1048576 | bytes 1310720 | tf_op jit(solution)/shard_map/convert_element_type | solution.py:260
  76.1 1.9 %shard_map.117 = (bf16[24,2048]{1,0:T(8,128)(2,1)}, bf16[24,2048]{1,0:T(8,128)(2,1)}, bf16[24,2048]{1,0:T(8,128)(2,1)}, bf16[24,2048]{1,0:T(8,128)(2,1)}) custom-call(bf16[4,24,64]{2,1,0:T(8,128)(2,1)} %get-tuple-element.21.place_ref, bf16[64,2048]{1,0:T(8,128)(2,1)} %add_convert_fusion.rows_ref), custom_call_target="tpu_custom_call" | custom-call | flops 25165824 | bytes 667648 | tf_op jit(solution)/shard_map/pallas_call | solution.py:30
  78.0 2.1 %collective-permute-start.24 = (bf16[24,2048]{1,0:T(8,128)(2,1)}, bf16[24,2048]{1,0:T(8,128)(2,1)S(1)}, u32[]{:S(2)}, u32[]{:S(2)}) collective-permute-start(bf16[24,2048]{1,0:T(8,128)(2,1)} %get-tuple-element.32), channel_id=1, source_target_pairs={{0,2},{2,0},{4,6},{6,4},{1,3},{3,1},{5,7},{7,5},{8,10},{10,8},{12,... | collective-permute-start | bytes 294920 | tf_op jit(solution)/shard_map/ppermute | solution.py:50
  80.1 2.3 %collective-permute-start.25 = (bf16[24,2048]{1,0:T(8,128)(2,1)}, bf16[24,2048]{1,0:T(8,128)(2,1)S(1)}, u32[]{:S(2)}, u32[]{:S(2)}) collective-permute-start(bf16[24,2048]{1,0:T(8,128)(2,1)} %get-tuple-element.33), channel_id=1, source_target_pairs={{0,4},{2,6},{4,0},{6,2},{1,5},{3,7},{5,1},{7,3},{8,12},{10,14},{12... | collective-permute-start | bytes 294920 | tf_op jit(solution)/shard_map/ppermute | solution.py:50
  84.1 1.9 %collective-permute-done.25 = bf16[24,2048]{1,0:T(8,128)(2,1)S(1)} collective-permute-done((bf16[24,2048]{1,0:T(8,128)(2,1)}, bf16[24,2048]{1,0:T(8,128)(2,1)S(1)}, u32[]{:S(2)}, u32[]{:S(2)}) %collective-permute-start.25) | collective-permute-done | bytes 98336 | tf_op jit(solution)/shard_map/ppermute | solution.py:50
  85.9 5.2 %collective-permute-done.26 = bf16[24,2048]{1,0:T(8,128)(2,1)S(1)} collective-permute-done((bf16[24,2048]{1,0:T(8,128)(2,1)}, bf16[24,2048]{1,0:T(8,128)(2,1)S(1)}, u32[]{:S(2)}, u32[]{:S(2)}) %collective-permute-start.26) | collective-permute-done | bytes 98336 | tf_op jit(solution)/shard_map/ppermute | solution.py:50
  93.9 5.1 %shard_map.112 = bf16[128,2048]{1,0:T(8,128)(2,1)} custom-call(s32[3]{0:T(128)} %pad_add_fusion.info_ref, bf16[3,128,2048]{2,1,0:T(8,128)(2,1)} %bitcast.35, bf16[2,64,2048]{2,1,0:T(8,128)(2,1)} %copy-done.2, bf16[2,64,2048]{2,1,0:T(8,128)(2,1)} %copy-done.3), custom_call_target="tpu_custom_call" | custom-call | flops 268435456 | bytes 3145728 | tf_op jit(solution)/shard_map/pallas_call | solution.py:312
  99.6 1.8 %shard_map.118 = bf16[12,4096]{1,0:T(8,128)(2,1)} custom-call(s32[1]{0:T(128)} %bitcast.core_ref, s32[1,1]{1,0:T(1,128)} %copy.15.count_ref, bf16[24,2048]{1,0:T(8,128)(2,1)} %copy-done.6, bf16[24,2048]{1,0:T(8,128)(2,1)} %copy-done.16, s32[1,128]{1,0:T(1,128)} %bitcast.43, bf16[1,128]{1,0:T(2,128)(2,1)} %score_ref.1), custom_call_target="tpu_custom_call" | custom-call | flops 2359296 | bytes 295688 | tf_op jit(solution)/shard_map/pallas_call | solution.py:30
  (98 shorter events, 23.8 us)
Async XLA Ops:
  6.3 6.6 %collective-permute-start.7 = (bf16[24,2048]{1,0:T(8,128)(2,1)S(1)}, bf16[24,2048]{1,0:T(8,128)(2,1)S(1)}, u32[]{:S(2)}, u32[]{:S(2)}) collective-permute-start(bf16[24,2048]{1,0:T(8,128)(2,1)S(1)} %add.46.refs_0_), channel_id=1, source_target_pairs={{0,2},{2,0},{4,6},{6,4},{1,3},{3,1},{5,7},{7,5},{8,10},{10,8},{12,... | collective-permute-start | bytes 294920 | tf_op jit(solution)/shard_map/ppermute | solution.py:50
  9.3 10.7 %collective-permute-start.8 = (bf16[24,2048]{1,0:T(8,128)(2,1)S(1)}, bf16[24,2048]{1,0:T(8,128)(2,1)S(1)}, u32[]{:S(2)}, u32[]{:S(2)}) collective-permute-start(bf16[24,2048]{1,0:T(8,128)(2,1)S(1)} %add.46.refs_0_), channel_id=1, source_target_pairs={{0,4},{2,6},{4,0},{6,2},{1,5},{3,7},{5,1},{7,3},{8,12},{10,14},{12... | collective-permute-start | bytes 294920 | tf_op jit(solution)/shard_map/ppermute | solution.py:50
  11.9 8.1 %collective-permute-start.9 = (bf16[24,2048]{1,0:T(8,128)(2,1)S(1)}, bf16[24,2048]{1,0:T(8,128)(2,1)S(1)}, u32[]{:S(2)}, u32[]{:S(2)}) collective-permute-start(bf16[24,2048]{1,0:T(8,128)(2,1)S(1)} %add.46.refs_0_), channel_id=1, source_target_pairs={{0,6},{2,4},{4,2},{6,0},{1,7},{3,5},{5,3},{7,1},{8,14},{10,12},{12... | collective-permute-start | bytes 294920 | tf_op jit(solution)/shard_map/ppermute | solution.py:50
  23.4 9.0 %collective-permute-start.10 = (bf16[64,2048]{1,0:T(8,128)(2,1)}, bf16[64,2048]{1,0:T(8,128)(2,1)S(1)}, u32[]{:S(2)}, u32[]{:S(2)}) collective-permute-start(bf16[64,2048]{1,0:T(8,128)(2,1)} %get-tuple-element.22.refs_0_), channel_id=1, source_target_pairs={{0,16},{1,9},{8,24},{9,1},{16,0},{17,25},{24,8},{25,17},{2,18},{3,... | collective-permute-start | bytes 786440 | tf_op jit(solution)/shard_map/ppermute | solution.py:56
  25.0 8.7 %collective-permute-start.11 = (bf16[64,2048]{1,0:T(8,128)(2,1)}, bf16[64,2048]{1,0:T(8,128)(2,1)S(1)}, u32[]{:S(2)}, u32[]{:S(2)}) collective-permute-start(bf16[64,2048]{1,0:T(8,128)(2,1)} %get-tuple-element.22.refs_0_), channel_id=1, source_target_pairs={{0,8},{1,17},{8,0},{9,25},{16,24},{17,1},{24,16},{25,9},{2,10},{3,... | collective-permute-start | bytes 786440 | tf_op jit(solution)/shard_map/ppermute | solution.py:56
  32.4 6.4 %collective-permute-start.12 = (bf16[64,2048]{1,0:T(8,128)(2,1)S(1)}, bf16[64,2048]{1,0:T(8,128)(2,1)S(1)}, u32[]{:S(2)}, u32[]{:S(2)}) collective-permute-start(bf16[64,2048]{1,0:T(8,128)(2,1)S(1)} %collective-permute-done.10.refs_1_), channel_id=1, source_target_pairs={{0,8},{1,17},{8,0},{9,25},{16,24},{17,1},{24,16},{25,9},{2,10},{3,... | collective-permute-start | bytes 786440 | tf_op jit(solution)/shard_map/ppermute | solution.py:56
  33.2 7.8 %collective-permute-start.13 = (bf16[64,2048]{1,0:T(8,128)(2,1)}, bf16[64,2048]{1,0:T(8,128)(2,1)S(1)}, u32[]{:S(2)}, u32[]{:S(2)}) collective-permute-start(bf16[64,2048]{1,0:T(8,128)(2,1)} %get-tuple-element.22.refs_0_), channel_id=1, source_target_pairs={{0,1},{1,0},{2,3},{3,2},{4,5},{5,4},{6,7},{7,6},{8,9},{9,8},{10,11... | collective-permute-start | bytes 786440 | tf_op jit(solution)/shard_map/ppermute | solution.py:45
  33.2 9.5 %collective-permute-start.15 = (bf16[64,2048]{1,0:T(8,128)(2,1)S(1)}, bf16[64,2048]{1,0:T(8,128)(2,1)S(1)}, u32[]{:S(2)}, u32[]{:S(2)}) collective-permute-start(bf16[64,2048]{1,0:T(8,128)(2,1)S(1)} %collective-permute-done.10.refs_1_), channel_id=1, source_target_pairs={{0,1},{1,0},{2,3},{3,2},{4,5},{5,4},{6,7},{7,6},{8,9},{9,8},{10,11... | collective-permute-start | bytes 786440 | tf_op jit(solution)/shard_map/ppermute | solution.py:45
  33.7 10.2 %collective-permute-start.14 = (bf16[64,2048]{1,0:T(8,128)(2,1)S(1)}, bf16[64,2048]{1,0:T(8,128)(2,1)S(1)}, u32[]{:S(2)}, u32[]{:S(2)}) collective-permute-start(bf16[64,2048]{1,0:T(8,128)(2,1)S(1)} %collective-permute-done.11.refs_2_), channel_id=1, source_target_pairs={{0,1},{1,0},{2,3},{3,2},{4,5},{5,4},{6,7},{7,6},{8,9},{9,8},{10,11... | collective-permute-start | bytes 786440 | tf_op jit(solution)/shard_map/ppermute | solution.py:45
  39.5 15.0 %collective-permute-start.2 = (bf16[24,2048]{1,0:T(8,128)(2,1)}, bf16[24,2048]{1,0:T(8,128)(2,1)}, u32[]{:S(2)}, u32[]{:S(2)}) collective-permute-start(bf16[24,2048]{1,0:T(8,128)(2,1)} %maximum_maximum_fusion), channel_id=1, source_target_pairs={{0,2},{2,0},{4,6},{6,4},{1,3},{3,1},{5,7},{7,5},{8,10},{10,8},{12,... | collective-permute-start | bytes 294920 | tf_op jit(solution)/shard_map/ppermute | solution.py:50
  41.0 13.5 %collective-permute-start.3 = (bf16[24,2048]{1,0:T(8,128)(2,1)}, bf16[24,2048]{1,0:T(8,128)(2,1)}, u32[]{:S(2)}, u32[]{:S(2)}) collective-permute-start(bf16[24,2048]{1,0:T(8,128)(2,1)} %maximum_maximum_fusion), channel_id=1, source_target_pairs={{0,4},{2,6},{4,0},{6,2},{1,5},{3,7},{5,1},{7,3},{8,12},{10,14},{12... | collective-permute-start | bytes 294920 | tf_op jit(solution)/shard_map/ppermute | solution.py:50
  42.8 11.8 %collective-permute-start.4 = (bf16[24,2048]{1,0:T(8,128)(2,1)}, bf16[24,2048]{1,0:T(8,128)(2,1)}, u32[]{:S(2)}, u32[]{:S(2)}) collective-permute-start(bf16[24,2048]{1,0:T(8,128)(2,1)} %maximum_maximum_fusion), channel_id=1, source_target_pairs={{0,6},{2,4},{4,2},{6,0},{1,7},{3,5},{5,3},{7,1},{8,14},{10,12},{12... | collective-permute-start | bytes 294920 | tf_op jit(solution)/shard_map/ppermute | solution.py:50
  55.6 12.9 %collective-permute-start.5 = (bf16[96,2048]{1,0:T(8,128)(2,1)S(1)}, bf16[96,2048]{1,0:T(8,128)(2,1)S(1)}, u32[]{:S(2)}, u32[]{:S(2)}) collective-permute-start(bf16[96,2048]{1,0:T(8,128)(2,1)S(1)} %pad_maximum_fusion.near_ref), channel_id=1, source_target_pairs={{0,1},{1,0},{2,3},{3,2},{4,5},{5,4},{6,7},{7,6},{8,9},{9,8},{10,11... | collective-permute-start | bytes 1179656 | tf_op jit(solution)/shard_map/ppermute | solution.py:45
  56.2 5.4 %collective-permute-start.20 = (bf16[64,2048]{1,0:T(8,128)(2,1)}, bf16[64,2048]{1,0:T(8,128)(2,1)S(1)}, u32[]{:S(2)}, u32[]{:S(2)}) collective-permute-start(bf16[64,2048]{1,0:T(8,128)(2,1)} %get-tuple-element.28), channel_id=1, source_target_pairs={{0,1},{1,0},{2,3},{3,2},{4,5},{5,4},{6,7},{7,6},{8,9},{9,8},{10,11... | collective-permute-start | bytes 786440 | tf_op jit(solution)/shard_map/ppermute | solution.py:45
  56.7 17.4 %collective-permute-start.17 = (bf16[64,2048]{1,0:T(8,128)(2,1)}, bf16[64,2048]{1,0:T(8,128)(2,1)}, u32[]{:S(2)}, u32[]{:S(2)}) collective-permute-start(bf16[64,2048]{1,0:T(8,128)(2,1)} %get-tuple-element.24), channel_id=1, source_target_pairs={{0,1},{1,0},{2,3},{3,2},{4,5},{5,4},{6,7},{7,6},{8,9},{9,8},{10,11... | collective-permute-start | bytes 786440 | tf_op jit(solution)/shard_map/ppermute | solution.py:45
  57.8 6.4 %collective-permute-start.22 = (bf16[64,2048]{1,0:T(8,128)(2,1)S(1)}, bf16[64,2048]{1,0:T(8,128)(2,1)S(1)}, u32[]{:S(2)}, u32[]{:S(2)}) collective-permute-start(bf16[64,2048]{1,0:T(8,128)(2,1)S(1)} %add_convert_fusion.2), channel_id=1, source_target_pairs={{0,16},{1,9},{8,24},{9,1},{16,0},{17,25},{24,8},{25,17},{2,18},{3,... | collective-permute-start | bytes 786440 | tf_op jit(solution)/shard_map/ppermute | solution.py:56
  61.1 13.0 %collective-permute-start.19 = (bf16[64,2048]{1,0:T(8,128)(2,1)}, bf16[64,2048]{1,0:T(8,128)(2,1)}, u32[]{:S(2)}, u32[]{:S(2)}) collective-permute-start(bf16[64,2048]{1,0:T(8,128)(2,1)} %add_convert_fusion.3), channel_id=1, source_target_pairs={{0,16},{1,9},{8,24},{9,1},{16,0},{17,25},{24,8},{25,17},{2,18},{3,... | collective-permute-start | bytes 786440 | tf_op jit(solution)/shard_map/ppermute | solution.py:56
  66.0 8.1 %collective-permute-start.23 = (bf16[64,2048]{1,0:T(8,128)(2,1)}, bf16[64,2048]{1,0:T(8,128)(2,1)}, u32[]{:S(2)}, u32[]{:S(2)}) collective-permute-start(bf16[64,2048]{1,0:T(8,128)(2,1)} %add_convert_fusion.1), channel_id=1, source_target_pairs={{0,8},{1,17},{8,0},{9,25},{16,24},{17,1},{24,16},{25,9},{2,10},{3,... | collective-permute-start | bytes 786440 | tf_op jit(solution)/shard_map/ppermute | solution.py:56
  66.6 26.3 %collective-permute-start = (bf16[2,64,2048]{2,1,0:T(8,128)(2,1)S(1)}, bf16[2,64,2048]{2,1,0:T(8,128)(2,1)S(1)}, u32[]{:S(2)}, u32[]{:S(2)}) collective-permute-start(bf16[2,64,2048]{2,1,0:T(8,128)(2,1)S(1)} %get-tuple-element.36), channel_id=1, source_target_pairs={{1,2},{3,4},{5,6},{2,1},{4,3},{6,5},{9,10},{11,12},{13,14},{10,9},... | collective-permute-start | bytes 1572872 | tf_op jit(solution)/shard_map/ppermute | solution.py:307
  68.5 24.4 %collective-permute-start.1 = (bf16[2,64,2048]{2,1,0:T(8,128)(2,1)S(1)}, bf16[2,64,2048]{2,1,0:T(8,128)(2,1)S(1)}, u32[]{:S(2)}, u32[]{:S(2)}) collective-permute-start(bf16[2,64,2048]{2,1,0:T(8,128)(2,1)S(1)} %get-tuple-element.35), channel_id=1, source_target_pairs={{0,1},{1,0},{2,3},{3,2},{4,5},{5,4},{6,7},{7,6},{8,9},{9,8},{10,11... | collective-permute-start | bytes 1572872 | tf_op jit(solution)/shard_map/ppermute | solution.py:45
  78.0 6.0 %collective-permute-start.24 = (bf16[24,2048]{1,0:T(8,128)(2,1)}, bf16[24,2048]{1,0:T(8,128)(2,1)S(1)}, u32[]{:S(2)}, u32[]{:S(2)}) collective-permute-start(bf16[24,2048]{1,0:T(8,128)(2,1)} %get-tuple-element.32), channel_id=1, source_target_pairs={{0,2},{2,0},{4,6},{6,4},{1,3},{3,1},{5,7},{7,5},{8,10},{10,8},{12,... | collective-permute-start | bytes 294920 | tf_op jit(solution)/shard_map/ppermute | solution.py:50
  80.1 5.9 %collective-permute-start.25 = (bf16[24,2048]{1,0:T(8,128)(2,1)}, bf16[24,2048]{1,0:T(8,128)(2,1)S(1)}, u32[]{:S(2)}, u32[]{:S(2)}) collective-permute-start(bf16[24,2048]{1,0:T(8,128)(2,1)} %get-tuple-element.33), channel_id=1, source_target_pairs={{0,4},{2,6},{4,0},{6,2},{1,5},{3,7},{5,1},{7,3},{8,12},{10,14},{12... | collective-permute-start | bytes 294920 | tf_op jit(solution)/shard_map/ppermute | solution.py:50
  82.4 8.8 %collective-permute-start.26 = (bf16[24,2048]{1,0:T(8,128)(2,1)}, bf16[24,2048]{1,0:T(8,128)(2,1)S(1)}, u32[]{:S(2)}, u32[]{:S(2)}) collective-permute-start(bf16[24,2048]{1,0:T(8,128)(2,1)} %get-tuple-element.34), channel_id=1, source_target_pairs={{0,6},{2,4},{4,2},{6,0},{1,7},{3,5},{5,3},{7,1},{8,14},{10,12},{12... | collective-permute-start | bytes 294920 | tf_op jit(solution)/shard_map/ppermute | solution.py:50
  92.1 6.9 %collective-permute-start.27 = (bf16[24,2048]{1,0:T(8,128)(2,1)S(1)}, bf16[24,2048]{1,0:T(8,128)(2,1)S(1)}, u32[]{:S(2)}, u32[]{:S(2)}) collective-permute-start(bf16[24,2048]{1,0:T(8,128)(2,1)S(1)} %add_convert_fusion.4.mine_ref), channel_id=1, source_target_pairs={{0,1},{1,0},{2,3},{3,2},{4,5},{5,4},{6,7},{7,6},{8,9},{9,8},{10,11... | collective-permute-start | bytes 294920 | tf_op jit(solution)/shard_map/ppermute | solution.py:45
  (24 other events, 146.4 us)

commit v2 on v1

--- a/solution.py
+++ b/solution.py
@@ -8,9 +8,9 @@
 from jax.experimental.pallas import tpu as pltpu
 from jax.sharding import PartitionSpec as P
 
+
 HEAD_DIM = 128
 LIGHT_HEADS = 16
-HEAVY_HEADS = 16
 TILE = 128
 CAP = 12
 MEAN_LIVE = 8
@@ -25,7 +25,7 @@
     return lax.broadcasted_iota(jnp.int32, shape, dim)
 
 
-def call(body, outs, args, scalars, flops, **kw):
+def call(body, outs, args, scalars, flops, room=4 << 20, **kw):
     size = sum(math.prod(a.shape) * a.dtype.itemsize for a in (*args, *outs))
     return pl.pallas_call(
         body,
@@ -33,6 +33,7 @@
         in_specs=[SMEM] * scalars + [VMEM] * (len(args) - scalars),
         out_specs=[VMEM] * len(outs),
         cost_estimate=pl.CostEstimate(flops=flops, bytes_accessed=size, transcendentals=0),
+        compiler_params=pltpu.CompilerParams(vmem_limit_bytes=min(60 << 20, size + room)),
         **kw,
     )(*args)
 
@@ -69,7 +70,8 @@
     parts = [x]
     for stride, radix in seq_stages():
         x = jnp.concatenate(parts, axis=0) if len(parts) > 1 else parts[0]
-        parts = [x] + [swap_seq(x, k * stride) for k in range(1, radix)]
+        far = {k: swap_seq(x, k * stride) for k in range(radix - 1, 0, -1)}
+        parts = [x] + [far[k] for k in range(1, radix)]
     return parts
 
 
@@ -77,9 +79,10 @@
     stages = seq_stages()
     for at in range(len(stages) - 1, -1, -1):
         stride, radix = stages[at]
+        far = {k: swap_seq(parts[k], k * stride) for k in range(radix - 1, 0, -1)}
         total = parts[0].astype(F32)
         for k in range(1, radix):
-            total = total + swap_seq(parts[k], k * stride).astype(F32)
+            total = total + far[k].astype(F32)
         total = total.astype(BF16)
         if at:
             parts = jnp.split(total, stages[at - 1][1], axis=0)
@@ -181,7 +184,6 @@
     )
     core = core_ref[0]
     rows, half = mine[0].shape
-    units = win_ref.shape[1]
     at_mine = pl.multiple_of(core * half, 128)
     at_peer = pl.multiple_of((1 - core) * half, 128)
     group = max(1, min(4, 256 // rows))
@@ -243,10 +245,38 @@
     )[0]
 
 
-def routed_ffn(core, tokens, gain, win, wout, score, counts, order):
+def load_kernel(*refs):
+    n = len(refs) // 2
+    copies = [pltpu.make_async_copy(refs[i], refs[n + i], refs[2 * n].at[i]) for i in range(n)]
+    for c in copies:
+        c.start()
+    for c in copies:
+        c.wait()
+
+
+def load(*arrays):
+    n = len(arrays)
+    return pl.pallas_call(
+        load_kernel,
+        out_shape=[struct(a.shape, a.dtype) for a in arrays],
+        in_specs=[pl.BlockSpec(memory_space=pltpu.HBM)] * n,
+        out_specs=[VMEM] * n,
+        scratch_shapes=[pltpu.SemaphoreType.DMA((n,))],
+        cost_estimate=pl.CostEstimate(
+            flops=0, bytes_accessed=sum(2 * a.size for a in arrays), transcendentals=0
+        ),
+        compiler_params=pltpu.CompilerParams(
+            vmem_limit_bytes=46 << 20
+        ),
+    )(*arrays)
+
+
+def routed_ffn(core, tokens, gain, win, wout, score, counts, order, heavy_qkv):
     devices = lax.axis_size("seq") * lax.axis_size("fsdp")
     mine, send = pick_rows(core, counts, tokens, order, gain)
     pair = mine + swap_core(send)
+    heavy_qkv, _ = lax.optimization_barrier((heavy_qkv, pair))
+    win, wout = load(win, wout)
     x0, place = compact(gather_seq(pair), MEAN_LIVE * devices)
     x1 = swap_doc(x0, True)
     x2 = swap_doc(x0, False)
@@ -254,7 +284,7 @@
     mine = (x0, x1, x2, x3)
     p0, p2, p1, p3 = [swap_core(x) for x in mine]
     send, keep = ffn(core, mine, (p0, p1, p2, p3), win, wout)
-    back = [swap_core(s) for s in send]
+    back = {i: swap_core(send[i]) for i in (3, 2, 1, 0)}
 
     def total(*terms):
         return sum(t.astype(F32) for t in terms).astype(BF16)
@@ -264,7 +294,7 @@
     got3 = swap_doc(total(keep[2], back[1], got1), False)
     own = total(keep[0], back[0], got2, got3)
     summed = scatter_seq(spread(place, own))
-    return finish(core, counts, summed, swap_core(summed), order, score)
+    return finish(core, counts, summed, swap_core(summed), order, score), heavy_qkv
 
 
 def light_kernel(info_ref, qkv_ref, far_ref, near_ref, out_ref):
@@ -325,6 +355,7 @@
             bytes_accessed=12 * rows * width,
             transcendentals=2 * rows * rows * LIGHT_HEADS,
         ),
+        compiler_params=pltpu.CompilerParams(vmem_limit_bytes=12 << 20),
     )(info, planes, far, near)
 
 
@@ -377,13 +408,13 @@
     return jnp.where(slot_live[:, None], out, jnp.bfloat16(0))
 
 
-def shards(
+def layer(
     tokens, ffn_gain, in_proj, out_proj, router_score, tile_counts, tile_order, light_qkv, heavy_qkv
 ):
     assert tile_order.shape[1] == 1 and lax.axis_size("fsdp") == 2 and lax.axis_size("dp") == 4
     core = lax.axis_index("fsdp").astype(jnp.int32).reshape(1)
     slot_live = jnp.arange(CAP) < tile_counts[0, 0]
-    heavy_ffn = routed_ffn(
+    heavy_ffn, heavy_qkv = routed_ffn(
         core,
         tokens[0],
         ffn_gain[None],
@@ -392,6 +423,7 @@
         router_score,
         tile_counts,
         tile_order[0],
+        heavy_qkv,
     )
     light_out = light_branch(core, light_qkv[0])
     heavy_attn = heavy_branch(heavy_qkv[0], slot_live)
@@ -411,7 +443,7 @@
         P("dp", ("seq", "fsdp"), None, None),
     )
     return jax.shard_map(
-        shards,
+        layer,
         mesh=mesh,
         in_specs=placed,
         out_specs=(

time: 102 us -> 93 us (0.912)
  other arithmetic: 12.1 us -> 3.94 us
  Pallas kernels: 26.2 us -> 18.1 us
  waiting for transfers between devices: 28.8 us -> 33.5 us
  local copies, waits for them, and re-layouts: 6.92 us -> 10 us
    pallas_call x6, Pallas kernels: 21.1 us -> 8.44 us  [call(): pl.pallas_call(body, out_shape=outs, in_specs=[SMEM] * scalars + [VMEM] *...]
    pallas_call x0 -> x1, Pallas kernels: none -> 5.47 us  [load(): pl.pallas_call(load_kernel, out_shape=[struct(a.shape, a.dtype) for a in...]
    unnamed x41 -> x24, local copies, waits for them, and re-layouts: 5.34 us -> 9 us
    convert_element_type x4, other arithmetic: 6.55 us -> 2.91 us  [total(): return sum((t.astype(F32) for t in terms)).astype(BF16)]
    ppermute x6, waiting for transfers between devices: 13.4 us -> 16 us  [swap_doc(): return lax.ppermute(x, ('dp', 'fsdp'), pairs)]
    ppermute x12, waiting for transfers between devices: 1.18 us -> 2.49 us  [swap_core(): return lax.ppermute(x, 'fsdp', [(0, 1), (1, 0)])]
  transfers between devices with their start and end apart: 28 -> 28, of which waited for: 7 -> 11; matrix products, arithmetic and copies ran while one was open for 14% -> 4% of each run, Pallas kernels for 20% -> 17%
where the time goes in v2:
time: 93 us; the launch traced here: 92.6 us
  waiting for transfers between devices  33.5 us (36%)
  starting transfers between devices  25.6 us (28%)
  Pallas kernels  18.1 us (19%)
  local copies, waits for them, and re-layouts  10 us (11%)
  other arithmetic  3.94 us (4%)
  between operations  1.48 us (2%)
    ppermute x6, waiting for transfers between devices, swap_doc(): return lax.ppermute(x, ('dp', 'fsdp'), pairs)  16 us
    ppermute x9, waiting for transfers between devices, swap_seq(): return lax.ppermute(x, 'seq', [(i, i ^ mask) for i in range(n)])  15 us
    ppermute x9, starting transfers between devices, swap_seq(): return lax.ppermute(x, 'seq', [(i, i ^ mask) for i in range(n)])  14.3 us
    unnamed x24, local copies, waits for them, and re-layouts  9 us
    pallas_call x6, Pallas kernels, call(): pl.pallas_call(body, out_shape=outs, in_specs=[SMEM] * scalars + [VMEM] *...  8.44 us
    ppermute x6, starting transfers between devices, swap_doc(): return lax.ppermute(x, ('dp', 'fsdp'), pairs)  6.41 us
    pallas_call x1, Pallas kernels, load(): pl.pallas_call(load_kernel, out_shape=[struct(a.shape, a.dtype) for a in...  5.47 us
    ppermute x12, starting transfers between devices, swap_core(): return lax.ppermute(x, 'fsdp', [(0, 1), (1, 0)])  4.22 us
  transfers between devices with their start and end apart: 28, of which 11 were waited for; matrix products, arithmetic and copies ran while one was open for 4% of the time, Pallas kernels for 17%

profile of v2, /device:TPU:0, one launch (start us, length us, event | category | flops | bytes accessed | tf_op | source)
XLA Modules:
  0.0 92.6 jit_solution(1276566718838718945)
XLA Ops:
  4.9 5.5 %shard_map.116 = (bf16[4096,512]{1,0:T(8,128)(2,1)S(1)}, bf16[512,4096]{1,0:T(8,128)(2,1)}) custom-call(bf16[4096,512]{1,0:T(8,128)(2,1)} %refs_0_.1, bf16[512,4096]{1,0:T(8,128)(2,1)} %refs_1_.1), custom_call_target="tpu_custom_call" | custom-call | bytes 8388608 | tf_op jit(solution)/shard_map/pallas_call | solution.py:259
  10.4 2.0 %copy-done.1 = bf16[4096,512]{1,0:T(8,128)(2,1)} copy-done((bf16[4096,512]{1,0:T(8,128)(2,1)}, bf16[4096,512]{1,0:T(8,128)(2,1)S(1)}, u32[]{:S(2)}) %copy-start.1) | copy-done | bytes 4194328
  12.5 2.7 %collective-permute-start.7 = (bf16[24,2048]{1,0:T(8,128)(2,1)S(1)}, bf16[24,2048]{1,0:T(8,128)(2,1)S(1)}, u32[]{:S(2)}, u32[]{:S(2)}) collective-permute-start(bf16[24,2048]{1,0:T(8,128)(2,1)S(1)} %add.46.refs_0_), channel_id=1, source_target_pairs={{0,2},{2,0},{4,6},{6,4},{1,3},{3,1},{5,7},{7,5},{8,10},{10,8},{12,... | collective-permute-start | bytes 294920 | tf_op jit(solution)/shard_map/ppermute | solution.py:51
  15.1 2.6 %collective-permute-start.8 = (bf16[24,2048]{1,0:T(8,128)(2,1)S(1)}, bf16[24,2048]{1,0:T(8,128)(2,1)S(1)}, u32[]{:S(2)}, u32[]{:S(2)}) collective-permute-start(bf16[24,2048]{1,0:T(8,128)(2,1)S(1)} %add.46.refs_0_), channel_id=1, source_target_pairs={{0,4},{2,6},{4,0},{6,2},{1,5},{3,7},{5,1},{7,3},{8,12},{10,14},{12... | collective-permute-start | bytes 294920 | tf_op jit(solution)/shard_map/ppermute | solution.py:51
  18.6 7.3 %collective-permute-done.8.refs_2_ = bf16[24,2048]{1,0:T(8,128)(2,1)S(1)} collective-permute-done((bf16[24,2048]{1,0:T(8,128)(2,1)S(1)}, bf16[24,2048]{1,0:T(8,128)(2,1)S(1)}, u32[]{:S(2)}, u32[]{:S(2)}) %collective-permute-start.8) | collective-permute-done | bytes 98336 | tf_op jit(solution)/shard_map/ppermute | solution.py:51
  26.4 1.6 %collective-permute-start.10 = (bf16[64,2048]{1,0:T(8,128)(2,1)S(1)}, bf16[64,2048]{1,0:T(8,128)(2,1)S(1)}, u32[]{:S(2)}, u32[]{:S(2)}) collective-permute-start(bf16[64,2048]{1,0:T(8,128)(2,1)S(1)} %get-tuple-element.26.refs_0_), channel_id=1, source_target_pairs={{0,16},{1,9},{8,24},{9,1},{16,0},{17,25},{24,8},{25,17},{2,18},{3,... | collective-permute-start | bytes 786440 | tf_op jit(solution)/shard_map/ppermute | solution.py:57
  28.0 1.6 %collective-permute-start.11 = (bf16[64,2048]{1,0:T(8,128)(2,1)S(1)}, bf16[64,2048]{1,0:T(8,128)(2,1)S(1)}, u32[]{:S(2)}, u32[]{:S(2)}) collective-permute-start(bf16[64,2048]{1,0:T(8,128)(2,1)S(1)} %get-tuple-element.26.refs_0_), channel_id=1, source_target_pairs={{0,8},{1,17},{8,0},{9,25},{16,24},{17,1},{24,16},{25,9},{2,10},{3,... | collective-permute-start | bytes 786440 | tf_op jit(solution)/shard_map/ppermute | solution.py:57
  29.6 6.1 %collective-permute-done.10.refs_1_ = bf16[64,2048]{1,0:T(8,128)(2,1)S(1)} collective-permute-done((bf16[64,2048]{1,0:T(8,128)(2,1)S(1)}, bf16[64,2048]{1,0:T(8,128)(2,1)S(1)}, u32[]{:S(2)}, u32[]{:S(2)}) %collective-permute-start.10) | collective-permute-done | bytes 262176 | tf_op jit(solution)/shard_map/ppermute | solution.py:57
  36.4 5.6 %collective-permute-done.12.refs_3_ = bf16[64,2048]{1,0:T(8,128)(2,1)S(1)} collective-permute-done((bf16[64,2048]{1,0:T(8,128)(2,1)S(1)}, bf16[64,2048]{1,0:T(8,128)(2,1)S(1)}, u32[]{:S(2)}, u32[]{:S(2)}) %collective-permute-start.12) | collective-permute-done | bytes 262176 | tf_op jit(solution)/shard_map/ppermute | solution.py:57
  42.1 2.0 %collective-permute-start.3 = (bf16[24,2048]{1,0:T(8,128)(2,1)S(1)}, bf16[24,2048]{1,0:T(8,128)(2,1)S(1)}, u32[]{:S(2)}, u32[]{:S(2)}) collective-permute-start(bf16[24,2048]{1,0:T(8,128)(2,1)S(1)} %maximum_maximum_fusion), channel_id=1, source_target_pairs={{0,2},{2,0},{4,6},{6,4},{1,3},{3,1},{5,7},{7,5},{8,10},{10,8},{12,... | collective-permute-start | bytes 294920 | tf_op jit(solution)/shard_map/ppermute | solution.py:51
  45.2 1.4 %collective-permute-start.5 = (bf16[24,2048]{1,0:T(8,128)(2,1)S(1)}, bf16[24,2048]{1,0:T(8,128)(2,1)S(1)}, u32[]{:S(2)}, u32[]{:S(2)}) collective-permute-start(bf16[24,2048]{1,0:T(8,128)(2,1)S(1)} %maximum_maximum_fusion), channel_id=1, source_target_pairs={{0,6},{2,4},{4,2},{6,0},{1,7},{3,5},{5,3},{7,1},{8,14},{10,12},{12... | collective-permute-start | bytes 294920 | tf_op jit(solution)/shard_map/ppermute | solution.py:51
  46.6 2.2 %copy-done.2 = bf16[4096,512]{1,0:T(8,128)(2,1)S(1)} copy-done((bf16[4096,512]{1,0:T(8,128)(2,1)S(1)}, bf16[4096,512]{1,0:T(8,128)(2,1)}, u32[]{:S(2)}) %copy-start.2) | copy-done | bytes 4194328
  48.8 2.2 %copy-done.3 = bf16[512,4096]{1,0:T(8,128)(2,1)S(1)} copy-done((bf16[512,4096]{1,0:T(8,128)(2,1)S(1)}, bf16[512,4096]{1,0:T(8,128)(2,1)}, u32[]{:S(2)}) %copy-start.3) | copy-done | bytes 4194328
  51.0 4.4 %shard_map.117 = (bf16[64,2048]{1,0:T(8,128)(2,1)}, bf16[64,2048]{1,0:T(8,128)(2,1)S(1)}, bf16[64,2048]{1,0:T(8,128)(2,1)S(1)}, bf16[64,2048]{1,0:T(8,128)(2,1)S...) custom-call(s32[1]{0:T(128)} %bitcast.core_ref, ...), custom_call_target="tpu_custom_call" | custom-call | flops 2147483648 | bytes 12582916 | tf_op jit(solution)/shard_map/pallas_call | solution.py:30
  57.0 2.3 %collective-permute-start.1 = (bf16[2,64,2048]{2,1,0:T(8,128)(2,1)}, bf16[2,64,2048]{2,1,0:T(8,128)(2,1)S(1)}, u32[]{:S(2)}, u32[]{:S(2)}) collective-permute-start(bf16[2,64,2048]{2,1,0:T(8,128)(2,1)} %get-tuple-element.41), channel_id=1, source_target_pairs={{0,1},{1,0},{2,3},{3,2},{4,5},{5,4},{6,7},{7,6},{8,9},{9,8},{10,11... | collective-permute-start | bytes 1572872 | tf_op jit(solution)/shard_map/ppermute | solution.py:46
  60.1 1.9 %collective-permute-done.18 = bf16[64,2048]{1,0:T(8,128)(2,1)S(1)} collective-permute-done((bf16[64,2048]{1,0:T(8,128)(2,1)S(1)}, bf16[64,2048]{1,0:T(8,128)(2,1)S(1)}, u32[]{:S(2)}, u32[]{:S(2)}) %collective-permute-start.18) | collective-permute-done | bytes 262176 | tf_op jit(solution)/shard_map/ppermute | solution.py:46
  62.0 1.5 %collective-permute-start.22 = (bf16[64,2048]{1,0:T(8,128)(2,1)S(1)}, bf16[64,2048]{1,0:T(8,128)(2,1)S(1)}, u32[]{:S(2)}, u32[]{:S(2)}) collective-permute-start(bf16[64,2048]{1,0:T(8,128)(2,1)S(1)} %add_convert_fusion.2), channel_id=1, source_target_pairs={{0,16},{1,9},{8,24},{9,1},{16,0},{17,25},{24,8},{25,17},{2,18},{3,... | collective-permute-start | bytes 786440 | tf_op jit(solution)/shard_map/ppermute | solution.py:57
  64.3 4.0 %collective-permute-done.22 = bf16[64,2048]{1,0:T(8,128)(2,1)S(1)} collective-permute-done((bf16[64,2048]{1,0:T(8,128)(2,1)S(1)}, bf16[64,2048]{1,0:T(8,128)(2,1)S(1)}, u32[]{:S(2)}, u32[]{:S(2)}) %collective-permute-start.22) | collective-permute-done | bytes 262176 | tf_op jit(solution)/shard_map/ppermute | solution.py:57
  68.4 1.5 %collective-permute-start.19 = (bf16[64,2048]{1,0:T(8,128)(2,1)}, bf16[64,2048]{1,0:T(8,128)(2,1)}, u32[]{:S(2)}, u32[]{:S(2)}) collective-permute-start(bf16[64,2048]{1,0:T(8,128)(2,1)} %add_convert_fusion.3), channel_id=1, source_target_pairs={{0,16},{1,9},{8,24},{9,1},{16,0},{17,25},{24,8},{25,17},{2,18},{3,... | collective-permute-start | bytes 786440 | tf_op jit(solution)/shard_map/ppermute | solution.py:57
  71.0 4.2 %shard_map.112 = bf16[128,2048]{1,0:T(8,128)(2,1)} custom-call(s32[3]{0:T(128)S(1)} %pad_add_fusion.info_ref, bf16[3,128,2048]{2,1,0:T(8,128)(2,1)S(1)} %bitcast.35, bf16[2,64,2048]{2,1,0:T(8,128)(2,1)S(1)} %collective-permute-done.far_ref, bf16[2,64,2048]{2,1,0:T(8,128)(2,1)S(1)} %collective-permute-done.1.near_ref), custom_call_target="tpu_custom_call" | custom-call | flops 268435456 | bytes 3145728 | tf_op jit(solution)/shard_map/pallas_call | solution.py:342
  75.2 1.9 %shard_map.114 = bf16[24,1024]{1,0:T(8,128)(2,1)S(1)} custom-call(bf16[24,1024]{1,0:T(8,128)(2,1)S(1)} %pad_maximum_fusion.1.q_ref, bf16[96,2048]{1,0:T(8,128)(2,1)S(1)} %pad_maximum_fusion.near_ref, bf16[96,2048]{1,0:T(8,128)(2,1)S(1)} %collective-permute-done.6.far_ref), custom_call_target="tpu_custom_call" | custom-call | flops 18874368 | bytes 884736 | tf_op jit(solution)/shard_map/pallas_call | solution.py:30
  78.9 1.7 %collective-permute-start.24 = (bf16[24,2048]{1,0:T(8,128)(2,1)S(1)}, bf16[24,2048]{1,0:T(8,128)(2,1)S(1)}, u32[]{:S(2)}, u32[]{:S(2)}) collective-permute-start(bf16[24,2048]{1,0:T(8,128)(2,1)S(1)} %get-tuple-element.38), channel_id=1, source_target_pairs={{0,2},{2,0},{4,6},{6,4},{1,3},{3,1},{5,7},{7,5},{8,10},{10,8},{12,... | collective-permute-start | bytes 294920 | tf_op jit(solution)/shard_map/ppermute | solution.py:51
  80.6 1.8 %collective-permute-start.25 = (bf16[24,2048]{1,0:T(8,128)(2,1)S(1)}, bf16[24,2048]{1,0:T(8,128)(2,1)S(1)}, u32[]{:S(2)}, u32[]{:S(2)}) collective-permute-start(bf16[24,2048]{1,0:T(8,128)(2,1)S(1)} %get-tuple-element.39), channel_id=1, source_target_pairs={{0,4},{2,6},{4,0},{6,2},{1,5},{3,7},{5,1},{7,3},{8,12},{10,14},{12... | collective-permute-start | bytes 294920 | tf_op jit(solution)/shard_map/ppermute | solution.py:51
  84.1 6.3 %collective-permute-done.25 = bf16[24,2048]{1,0:T(8,128)(2,1)S(1)} collective-permute-done((bf16[24,2048]{1,0:T(8,128)(2,1)S(1)}, bf16[24,2048]{1,0:T(8,128)(2,1)S(1)}, u32[]{:S(2)}, u32[]{:S(2)}) %collective-permute-start.25) | collective-permute-done | bytes 98336 | tf_op jit(solution)/shard_map/ppermute | solution.py:51
  (83 shorter events, 16.9 us)
Async XLA Ops:
  4.4 8.1 %collective-permute-start.2 = (bf16[24,2048]{1,0:T(8,128)(2,1)S(1)}, bf16[24,2048]{1,0:T(8,128)(2,1)S(1)}, u32[]{:S(2)}, u32[]{:S(2)}) collective-permute-start(bf16[24,2048]{1,0:T(8,128)(2,1)S(1)} %get-tuple-element.23), channel_id=1, source_target_pairs={{0,1},{1,0},{2,3},{3,2},{4,5},{5,4},{6,7},{7,6},{8,9},{9,8},{10,11... | collective-permute-start | bytes 294920 | tf_op jit(solution)/shard_map/ppermute | solution.py:46
  12.5 6.1 %collective-permute-start.7 = (bf16[24,2048]{1,0:T(8,128)(2,1)S(1)}, bf16[24,2048]{1,0:T(8,128)(2,1)S(1)}, u32[]{:S(2)}, u32[]{:S(2)}) collective-permute-start(bf16[24,2048]{1,0:T(8,128)(2,1)S(1)} %add.46.refs_0_), channel_id=1, source_target_pairs={{0,2},{2,0},{4,6},{6,4},{1,3},{3,1},{5,7},{7,5},{8,10},{10,8},{12,... | collective-permute-start | bytes 294920 | tf_op jit(solution)/shard_map/ppermute | solution.py:51
  15.1 10.8 %collective-permute-start.8 = (bf16[24,2048]{1,0:T(8,128)(2,1)S(1)}, bf16[24,2048]{1,0:T(8,128)(2,1)S(1)}, u32[]{:S(2)}, u32[]{:S(2)}) collective-permute-start(bf16[24,2048]{1,0:T(8,128)(2,1)S(1)} %add.46.refs_0_), channel_id=1, source_target_pairs={{0,4},{2,6},{4,0},{6,2},{1,5},{3,7},{5,1},{7,3},{8,12},{10,14},{12... | collective-permute-start | bytes 294920 | tf_op jit(solution)/shard_map/ppermute | solution.py:51
  17.7 8.2 %collective-permute-start.9 = (bf16[24,2048]{1,0:T(8,128)(2,1)S(1)}, bf16[24,2048]{1,0:T(8,128)(2,1)S(1)}, u32[]{:S(2)}, u32[]{:S(2)}) collective-permute-start(bf16[24,2048]{1,0:T(8,128)(2,1)S(1)} %add.46.refs_0_), channel_id=1, source_target_pairs={{0,6},{2,4},{4,2},{6,0},{1,7},{3,5},{5,3},{7,1},{8,14},{10,12},{12... | collective-permute-start | bytes 294920 | tf_op jit(solution)/shard_map/ppermute | solution.py:51
  26.4 9.2 %collective-permute-start.10 = (bf16[64,2048]{1,0:T(8,128)(2,1)S(1)}, bf16[64,2048]{1,0:T(8,128)(2,1)S(1)}, u32[]{:S(2)}, u32[]{:S(2)}) collective-permute-start(bf16[64,2048]{1,0:T(8,128)(2,1)S(1)} %get-tuple-element.26.refs_0_), channel_id=1, source_target_pairs={{0,16},{1,9},{8,24},{9,1},{16,0},{17,25},{24,8},{25,17},{2,18},{3,... | collective-permute-start | bytes 786440 | tf_op jit(solution)/shard_map/ppermute | solution.py:57
  28.0 8.3 %collective-permute-start.11 = (bf16[64,2048]{1,0:T(8,128)(2,1)S(1)}, bf16[64,2048]{1,0:T(8,128)(2,1)S(1)}, u32[]{:S(2)}, u32[]{:S(2)}) collective-permute-start(bf16[64,2048]{1,0:T(8,128)(2,1)S(1)} %get-tuple-element.26.refs_0_), channel_id=1, source_target_pairs={{0,8},{1,17},{8,0},{9,25},{16,24},{17,1},{24,16},{25,9},{2,10},{3,... | collective-permute-start | bytes 786440 | tf_op jit(solution)/shard_map/ppermute | solution.py:57
  35.6 6.4 %collective-permute-start.12 = (bf16[64,2048]{1,0:T(8,128)(2,1)S(1)}, bf16[64,2048]{1,0:T(8,128)(2,1)S(1)}, u32[]{:S(2)}, u32[]{:S(2)}) collective-permute-start(bf16[64,2048]{1,0:T(8,128)(2,1)S(1)} %collective-permute-done.10.refs_1_), channel_id=1, source_target_pairs={{0,8},{1,17},{8,0},{9,25},{16,24},{17,1},{24,16},{25,9},{2,10},{3,... | collective-permute-start | bytes 786440 | tf_op jit(solution)/shard_map/ppermute | solution.py:57
  35.8 8.3 %collective-permute-start.13 = (bf16[64,2048]{1,0:T(8,128)(2,1)S(1)}, bf16[64,2048]{1,0:T(8,128)(2,1)S(1)}, u32[]{:S(2)}, u32[]{:S(2)}) collective-permute-start(bf16[64,2048]{1,0:T(8,128)(2,1)S(1)} %get-tuple-element.26.refs_0_), channel_id=1, source_target_pairs={{0,1},{1,0},{2,3},{3,2},{4,5},{5,4},{6,7},{7,6},{8,9},{9,8},{10,11... | collective-permute-start | bytes 786440 | tf_op jit(solution)/shard_map/ppermute | solution.py:46
  35.8 9.4 %collective-permute-start.15 = (bf16[64,2048]{1,0:T(8,128)(2,1)S(1)}, bf16[64,2048]{1,0:T(8,128)(2,1)S(1)}, u32[]{:S(2)}, u32[]{:S(2)}) collective-permute-start(bf16[64,2048]{1,0:T(8,128)(2,1)S(1)} %collective-permute-done.10.refs_1_), channel_id=1, source_target_pairs={{0,1},{1,0},{2,3},{3,2},{4,5},{5,4},{6,7},{7,6},{8,9},{9,8},{10,11... | collective-permute-start | bytes 786440 | tf_op jit(solution)/shard_map/ppermute | solution.py:46
  36.3 10.3 %collective-permute-start.14 = (bf16[64,2048]{1,0:T(8,128)(2,1)S(1)}, bf16[64,2048]{1,0:T(8,128)(2,1)S(1)}, u32[]{:S(2)}, u32[]{:S(2)}) collective-permute-start(bf16[64,2048]{1,0:T(8,128)(2,1)S(1)} %collective-permute-done.11.refs_2_), channel_id=1, source_target_pairs={{0,1},{1,0},{2,3},{3,2},{4,5},{5,4},{6,7},{7,6},{8,9},{9,8},{10,11... | collective-permute-start | bytes 786440 | tf_op jit(solution)/shard_map/ppermute | solution.py:46
  42.0 4.6 %collective-permute-start.16 = (bf16[64,2048]{1,0:T(8,128)(2,1)S(1)}, bf16[64,2048]{1,0:T(8,128)(2,1)S(1)}, u32[]{:S(2)}, u32[]{:S(2)}) collective-permute-start(bf16[64,2048]{1,0:T(8,128)(2,1)S(1)} %collective-permute-done.12.refs_3_), channel_id=1, source_target_pairs={{0,1},{1,0},{2,3},{3,2},{4,5},{5,4},{6,7},{7,6},{8,9},{9,8},{10,11... | collective-permute-start | bytes 786440 | tf_op jit(solution)/shard_map/ppermute | solution.py:46
  42.1 14.9 %collective-permute-start.3 = (bf16[24,2048]{1,0:T(8,128)(2,1)S(1)}, bf16[24,2048]{1,0:T(8,128)(2,1)S(1)}, u32[]{:S(2)}, u32[]{:S(2)}) collective-permute-start(bf16[24,2048]{1,0:T(8,128)(2,1)S(1)} %maximum_maximum_fusion), channel_id=1, source_target_pairs={{0,2},{2,0},{4,6},{6,4},{1,3},{3,1},{5,7},{7,5},{8,10},{10,8},{12,... | collective-permute-start | bytes 294920 | tf_op jit(solution)/shard_map/ppermute | solution.py:51
  44.0 15.3 %collective-permute-start.4 = (bf16[24,2048]{1,0:T(8,128)(2,1)S(1)}, bf16[24,2048]{1,0:T(8,128)(2,1)S(1)}, u32[]{:S(2)}, u32[]{:S(2)}) collective-permute-start(bf16[24,2048]{1,0:T(8,128)(2,1)S(1)} %maximum_maximum_fusion), channel_id=1, source_target_pairs={{0,4},{2,6},{4,0},{6,2},{1,5},{3,7},{5,1},{7,3},{8,12},{10,14},{12... | collective-permute-start | bytes 294920 | tf_op jit(solution)/shard_map/ppermute | solution.py:51
  45.2 14.1 %collective-permute-start.5 = (bf16[24,2048]{1,0:T(8,128)(2,1)S(1)}, bf16[24,2048]{1,0:T(8,128)(2,1)S(1)}, u32[]{:S(2)}, u32[]{:S(2)}) collective-permute-start(bf16[24,2048]{1,0:T(8,128)(2,1)S(1)} %maximum_maximum_fusion), channel_id=1, source_target_pairs={{0,6},{2,4},{4,2},{6,0},{1,7},{3,5},{5,3},{7,1},{8,14},{10,12},{12... | collective-permute-start | bytes 294920 | tf_op jit(solution)/shard_map/ppermute | solution.py:51
  56.3 14.4 %collective-permute-start = (bf16[2,64,2048]{2,1,0:T(8,128)(2,1)S(1)}, bf16[2,64,2048]{2,1,0:T(8,128)(2,1)S(1)}, u32[]{:S(2)}, u32[]{:S(2)}) collective-permute-start(bf16[2,64,2048]{2,1,0:T(8,128)(2,1)S(1)} %get-tuple-element.42), channel_id=1, source_target_pairs={{1,2},{3,4},{5,6},{2,1},{4,3},{6,5},{9,10},{11,12},{13,14},{10,9},... | collective-permute-start | bytes 1572872 | tf_op jit(solution)/shard_map/ppermute | solution.py:337
  57.0 14.0 %collective-permute-start.1 = (bf16[2,64,2048]{2,1,0:T(8,128)(2,1)}, bf16[2,64,2048]{2,1,0:T(8,128)(2,1)S(1)}, u32[]{:S(2)}, u32[]{:S(2)}) collective-permute-start(bf16[2,64,2048]{2,1,0:T(8,128)(2,1)} %get-tuple-element.41), channel_id=1, source_target_pairs={{0,1},{1,0},{2,3},{3,2},{4,5},{5,4},{6,7},{7,6},{8,9},{9,8},{10,11... | collective-permute-start | bytes 1572872 | tf_op jit(solution)/shard_map/ppermute | solution.py:46
  59.4 15.9 %collective-permute-start.6 = (bf16[96,2048]{1,0:T(8,128)(2,1)S(1)}, bf16[96,2048]{1,0:T(8,128)(2,1)S(1)}, u32[]{:S(2)}, u32[]{:S(2)}) collective-permute-start(bf16[96,2048]{1,0:T(8,128)(2,1)S(1)} %pad_maximum_fusion.near_ref), channel_id=1, source_target_pairs={{0,1},{1,0},{2,3},{3,2},{4,5},{5,4},{6,7},{7,6},{8,9},{9,8},{10,11... | collective-permute-start | bytes 1179656 | tf_op jit(solution)/shard_map/ppermute | solution.py:46
  62.0 6.4 %collective-permute-start.22 = (bf16[64,2048]{1,0:T(8,128)(2,1)S(1)}, bf16[64,2048]{1,0:T(8,128)(2,1)S(1)}, u32[]{:S(2)}, u32[]{:S(2)}) collective-permute-start(bf16[64,2048]{1,0:T(8,128)(2,1)S(1)} %add_convert_fusion.2), channel_id=1, source_target_pairs={{0,16},{1,9},{8,24},{9,1},{16,0},{17,25},{24,8},{25,17},{2,18},{3,... | collective-permute-start | bytes 786440 | tf_op jit(solution)/shard_map/ppermute | solution.py:57
  64.3 12.8 %collective-permute-start.17 = (bf16[64,2048]{1,0:T(8,128)(2,1)}, bf16[64,2048]{1,0:T(8,128)(2,1)}, u32[]{:S(2)}, u32[]{:S(2)}) collective-permute-start(bf16[64,2048]{1,0:T(8,128)(2,1)} %get-tuple-element.30), channel_id=1, source_target_pairs={{0,1},{1,0},{2,3},{3,2},{4,5},{5,4},{6,7},{7,6},{8,9},{9,8},{10,11... | collective-permute-start | bytes 786440 | tf_op jit(solution)/shard_map/ppermute | solution.py:46
  68.4 8.9 %collective-permute-start.19 = (bf16[64,2048]{1,0:T(8,128)(2,1)}, bf16[64,2048]{1,0:T(8,128)(2,1)}, u32[]{:S(2)}, u32[]{:S(2)}) collective-permute-start(bf16[64,2048]{1,0:T(8,128)(2,1)} %add_convert_fusion.3), channel_id=1, source_target_pairs={{0,16},{1,9},{8,24},{9,1},{16,0},{17,25},{24,8},{25,17},{2,18},{3,... | collective-permute-start | bytes 786440 | tf_op jit(solution)/shard_map/ppermute | solution.py:57
  70.7 6.7 %collective-permute-start.23 = (bf16[64,2048]{1,0:T(8,128)(2,1)}, bf16[64,2048]{1,0:T(8,128)(2,1)}, u32[]{:S(2)}, u32[]{:S(2)}) collective-permute-start(bf16[64,2048]{1,0:T(8,128)(2,1)} %add_convert_fusion.1), channel_id=1, source_target_pairs={{0,8},{1,17},{8,0},{9,25},{16,24},{17,1},{24,16},{25,9},{2,10},{3,... | collective-permute-start | bytes 786440 | tf_op jit(solution)/shard_map/ppermute | solution.py:57
  78.9 5.1 %collective-permute-start.24 = (bf16[24,2048]{1,0:T(8,128)(2,1)S(1)}, bf16[24,2048]{1,0:T(8,128)(2,1)S(1)}, u32[]{:S(2)}, u32[]{:S(2)}) collective-permute-start(bf16[24,2048]{1,0:T(8,128)(2,1)S(1)} %get-tuple-element.38), channel_id=1, source_target_pairs={{0,2},{2,0},{4,6},{6,4},{1,3},{3,1},{5,7},{7,5},{8,10},{10,8},{12,... | collective-permute-start | bytes 294920 | tf_op jit(solution)/shard_map/ppermute | solution.py:51
  80.6 9.7 %collective-permute-start.25 = (bf16[24,2048]{1,0:T(8,128)(2,1)S(1)}, bf16[24,2048]{1,0:T(8,128)(2,1)S(1)}, u32[]{:S(2)}, u32[]{:S(2)}) collective-permute-start(bf16[24,2048]{1,0:T(8,128)(2,1)S(1)} %get-tuple-element.39), channel_id=1, source_target_pairs={{0,4},{2,6},{4,0},{6,2},{1,5},{3,7},{5,1},{7,3},{8,12},{10,14},{12... | collective-permute-start | bytes 294920 | tf_op jit(solution)/shard_map/ppermute | solution.py:51
  82.5 7.9 %collective-permute-start.26 = (bf16[24,2048]{1,0:T(8,128)(2,1)S(1)}, bf16[24,2048]{1,0:T(8,128)(2,1)S(1)}, u32[]{:S(2)}, u32[]{:S(2)}) collective-permute-start(bf16[24,2048]{1,0:T(8,128)(2,1)S(1)} %get-tuple-element.40), channel_id=1, source_target_pairs={{0,6},{2,4},{4,2},{6,0},{1,7},{3,5},{5,3},{7,1},{8,14},{10,12},{12... | collective-permute-start | bytes 294920 | tf_op jit(solution)/shard_map/ppermute | solution.py:51
  (16 other events, 124.2 us)

commit v3 on v2

--- a/solution.py
+++ b/solution.py
@@ -119,6 +119,7 @@
         [core, counts, tokens, order, gain],
         2,
         2 * rows * TILE * width,
+        room=54 << 20,
         scratch_shapes=[pltpu.VMEM((rows, width), BF16)],
     )
 
@@ -266,7 +267,7 @@
             flops=0, bytes_accessed=sum(2 * a.size for a in arrays), transcendentals=0
         ),
         compiler_params=pltpu.CompilerParams(
-            vmem_limit_bytes=46 << 20
+            vmem_limit_bytes=42 << 20
         ),
     )(*arrays)
 
@@ -325,21 +326,40 @@
         out_ref[:, at] = (y / jnp.sum(e, axis=1, keepdims=True)).astype(BF16)
 
 
-def light_branch(core, qkv):
-    rows, _, width = qkv.shape
-    planes = jnp.transpose(qkv, (1, 0, 2))
-    last = rows - HALF_WIN
-    edge = core[0] * last
-    far = lax.dynamic_slice(planes, (1, edge, 0), (2, HALF_WIN, width))
-    near = lax.dynamic_slice(planes, (1, last - edge, 0), (2, HALF_WIN, width))
+def halo_kernel(info_ref, planes_ref, far_ref, near_ref, sems):
+    last = planes_ref.shape[1] - HALF_WIN
+    edge = pl.multiple_of(info_ref[0] * last, HALF_WIN)
+    other = pl.multiple_of(last - edge, HALF_WIN)
+    copies = [
+        pltpu.make_async_copy(planes_ref.at[1:3, pl.ds(at, HALF_WIN)], ref, sems.at[i])
+        for i, (at, ref) in enumerate(((edge, far_ref), (other, near_ref)))
+    ]
+    for c in copies:
+        c.start()
+    for c in copies:
+        c.wait()
+
+
+def light_branch(info, planes):
+    _, rows, width = planes.shape
+    run = pl.pallas_call(
+        halo_kernel,
+        out_shape=[struct((2, HALF_WIN, width))] * 2,
+        in_specs=[SMEM, pl.BlockSpec(memory_space=pl.ANY)],
+        out_specs=[VMEM] * 2,
+        scratch_shapes=[pltpu.SemaphoreType.DMA((2,))],
+        cost_estimate=pl.CostEstimate(
+            flops=0, bytes_accessed=8 * HALF_WIN * width, transcendentals=0
+        ),
+        compiler_params=pltpu.CompilerParams(vmem_limit_bytes=2 << 20),
+    )
+    far, near = run(info, planes)
     n = lax.axis_size("seq") * lax.axis_size("fsdp")
     pairs = [(i, i + 1) for i in range(1, n - 1, 2)]
     far = lax.ppermute(far, ("seq", "fsdp"), pairs + [(j, i) for i, j in pairs])
     near = swap_core(near)
-    first_pos = lax.axis_index(("seq", "fsdp")) * rows
-    info = jnp.stack([core[0], first_pos, jnp.int32(n * rows)])
     wide = 4 * HEAD_DIM
-    return pl.pallas_call(
+    run = pl.pallas_call(
         light_kernel,
         out_shape=struct((rows, width)),
         grid=(width // wide,),
@@ -356,7 +376,8 @@
             transcendentals=2 * rows * rows * LIGHT_HEADS,
         ),
         compiler_params=pltpu.CompilerParams(vmem_limit_bytes=12 << 20),
-    )(info, planes, far, near)
+    )
+    return run(info, planes, far, near)
 
 
 def heavy_kernel(q_ref, near_ref, far_ref, out_ref):
@@ -412,7 +433,11 @@
     tokens, ffn_gain, in_proj, out_proj, router_score, tile_counts, tile_order, light_qkv, heavy_qkv
 ):
     assert tile_order.shape[1] == 1 and lax.axis_size("fsdp") == 2 and lax.axis_size("dp") == 4
-    core = lax.axis_index("fsdp").astype(jnp.int32).reshape(1)
+    here = lax.axis_index(("seq", "fsdp")) * tokens.shape[1]
+    length = tokens.shape[1] * lax.axis_size("seq") * lax.axis_size("fsdp")
+    info = jnp.stack([lax.axis_index("fsdp"), here, jnp.int32(length)]).astype(jnp.int32)
+    info, tokens = lax.optimization_barrier((info, tokens))
+    core = info
     slot_live = jnp.arange(CAP) < tile_counts[0, 0]
     heavy_ffn, heavy_qkv = routed_ffn(
         core,
@@ -425,7 +450,7 @@
         tile_order[0],
         heavy_qkv,
     )
-    light_out = light_branch(core, light_qkv[0])
+    light_out = light_branch(info, jnp.transpose(light_qkv[0], (1, 0, 2)))
     heavy_attn = heavy_branch(heavy_qkv[0], slot_live)
     return (light_out[None], heavy_attn[None], heavy_ffn[None])
 

time: 93 us -> 82.4 us (0.89)
  local copies, waits for them, and re-layouts: 10 us -> 0.18 us
  other arithmetic: 3.94 us -> 1.95 us
  Pallas kernels: 18.1 us -> 19.2 us
    unnamed x24 -> x12, local copies, waits for them, and re-layouts: 9 us -> 0.03 us
    convert_element_type x4, other arithmetic: 2.91 us -> 0.37 us  [total(): return sum((t.astype(F32) for t in terms)).astype(BF16)]
    pallas_call x6, Pallas kernels: 8.44 us -> 10.8 us  [call(): pl.pallas_call(body, out_shape=outs, in_specs=[SMEM] * scalars + [VMEM] *...]
    pallas_call x1, Pallas kernels: 5.47 us -> 3.48 us  [load(): pl.pallas_call(load_kernel, out_shape=[struct(a.shape, a.dtype) for a in...]
    pallas_call x1 -> x2, Pallas kernels: 4.22 us -> 4.86 us  [the longest x1 4.22 us: light_branch(): return run(info, planes, far, near)]
  transfers between devices with their start and end apart: 28 -> 28, of which waited for: 11 -> 10; matrix products, arithmetic and copies ran while one was open for 4% -> 2% of each run, Pallas kernels for 17% -> 18%
where the time goes in v3:
time: 82.4 us; the launch traced here: 82.2 us
  waiting for transfers between devices  33.6 us (41%)
  starting transfers between devices  25.7 us (31%)
  Pallas kernels  19.2 us (23%)
  other arithmetic  1.95 us (2%)
  between operations  1.57 us (2%)
    ppermute x6, waiting for transfers between devices, swap_doc(): return lax.ppermute(x, ('dp', 'fsdp'), pairs)  16.4 us
    ppermute x9, waiting for transfers between devices, swap_seq(): return lax.ppermute(x, 'seq', [(i, i ^ mask) for i in range(n)])  15 us
    ppermute x9, starting transfers between devices, swap_seq(): return lax.ppermute(x, 'seq', [(i, i ^ mask) for i in range(n)])  14.3 us
    pallas_call x6, Pallas kernels, call(): pl.pallas_call(body, out_shape=outs, in_specs=[SMEM] * scalars + [VMEM] *...  10.8 us
    ppermute x6, starting transfers between devices, swap_doc(): return lax.ppermute(x, ('dp', 'fsdp'), pairs)  6.42 us
    ppermute x12, starting transfers between devices, swap_core(): return lax.ppermute(x, 'fsdp', [(0, 1), (1, 0)])  4.36 us
    pallas_call x1, Pallas kernels, light_branch(): return run(info, planes, far, near)  4.22 us
    pallas_call x1, Pallas kernels, load(): pl.pallas_call(load_kernel, out_shape=[struct(a.shape, a.dtype) for a in...  3.48 us
  transfers between devices with their start and end apart: 28, of which 10 were waited for; matrix products, arithmetic and copies ran while one was open for 2% of the time, Pallas kernels for 18%

profile of v3, /device:TPU:0, one launch (start us, length us, event | category | flops | bytes accessed | tf_op | source)
XLA Modules:
  0.0 82.2 jit_solution(11760771959830711325)
XLA Ops:
  1.9 2.4 %shard_map.114 = (bf16[24,2048]{1,0:T(8,128)(2,1)}, bf16[24,2048]{1,0:T(8,128)(2,1)}) custom-call(s32[3]{0:T(128)} %pad_add_fusion.info_ref.core_ref, s32[1,1]{1,0:T(1,128)} %copy.15.count_ref, bf16[128,4096]{1,0:T(8,128)(2,1)} %bitcast.31, s32[1,128]{1,0:T(1,128)} %bitcast.29, f32[1,4096]{1,0:T(1,128)} %bitcast.36), custom_call_target="tpu_custom_call" | custom-call | flops 25165824 | bytes 1262096 | tf_op jit(solution)/shard_map/pallas_call | solution.py:30
  4.9 3.5 %shard_map.117 = (bf16[4096,512]{1,0:T(8,128)(2,1)S(1)}, bf16[512,4096]{1,0:T(8,128)(2,1)S(1)}) custom-call(bf16[4096,512]{1,0:T(8,128)(2,1)} %refs_0_.1, bf16[512,4096]{1,0:T(8,128)(2,1)} %refs_1_.1), custom_call_target="tpu_custom_call" | custom-call | bytes 8388608 | tf_op jit(solution)/shard_map/pallas_call | solution.py:260
  8.5 2.7 %collective-permute-start.7 = (bf16[24,2048]{1,0:T(8,128)(2,1)S(1)}, bf16[24,2048]{1,0:T(8,128)(2,1)S(1)}, u32[]{:S(2)}, u32[]{:S(2)}) collective-permute-start(bf16[24,2048]{1,0:T(8,128)(2,1)S(1)} %add.37.refs_0_), channel_id=1, source_target_pairs={{0,2},{2,0},{4,6},{6,4},{1,3},{3,1},{5,7},{7,5},{8,10},{10,8},{12,... | collective-permute-start | bytes 294920 | tf_op jit(solution)/shard_map/ppermute | solution.py:51
  11.1 2.6 %collective-permute-start.8 = (bf16[24,2048]{1,0:T(8,128)(2,1)S(1)}, bf16[24,2048]{1,0:T(8,128)(2,1)S(1)}, u32[]{:S(2)}, u32[]{:S(2)}) collective-permute-start(bf16[24,2048]{1,0:T(8,128)(2,1)S(1)} %add.37.refs_0_), channel_id=1, source_target_pairs={{0,4},{2,6},{4,0},{6,2},{1,5},{3,7},{5,1},{7,3},{8,12},{10,14},{12... | collective-permute-start | bytes 294920 | tf_op jit(solution)/shard_map/ppermute | solution.py:51
  14.6 7.4 %collective-permute-done.8.refs_2_ = bf16[24,2048]{1,0:T(8,128)(2,1)S(1)} collective-permute-done((bf16[24,2048]{1,0:T(8,128)(2,1)S(1)}, bf16[24,2048]{1,0:T(8,128)(2,1)S(1)}, u32[]{:S(2)}, u32[]{:S(2)}) %collective-permute-start.8) | collective-permute-done | bytes 98336 | tf_op jit(solution)/shard_map/ppermute | solution.py:51
  22.4 1.6 %collective-permute-start.10 = (bf16[64,2048]{1,0:T(8,128)(2,1)S(1)}, bf16[64,2048]{1,0:T(8,128)(2,1)S(1)}, u32[]{:S(2)}, u32[]{:S(2)}) collective-permute-start(bf16[64,2048]{1,0:T(8,128)(2,1)S(1)} %get-tuple-element.34.refs_0_), channel_id=1, source_target_pairs={{0,16},{1,9},{8,24},{9,1},{16,0},{17,25},{24,8},{25,17},{2,18},{3,... | collective-permute-start | bytes 786440 | tf_op jit(solution)/shard_map/ppermute | solution.py:57
  24.0 1.6 %collective-permute-start.11 = (bf16[64,2048]{1,0:T(8,128)(2,1)S(1)}, bf16[64,2048]{1,0:T(8,128)(2,1)S(1)}, u32[]{:S(2)}, u32[]{:S(2)}) collective-permute-start(bf16[64,2048]{1,0:T(8,128)(2,1)S(1)} %get-tuple-element.34.refs_0_), channel_id=1, source_target_pairs={{0,8},{1,17},{8,0},{9,25},{16,24},{17,1},{24,16},{25,9},{2,10},{3,... | collective-permute-start | bytes 786440 | tf_op jit(solution)/shard_map/ppermute | solution.py:57
  25.6 6.1 %collective-permute-done.10.refs_1_ = bf16[64,2048]{1,0:T(8,128)(2,1)S(1)} collective-permute-done((bf16[64,2048]{1,0:T(8,128)(2,1)S(1)}, bf16[64,2048]{1,0:T(8,128)(2,1)S(1)}, u32[]{:S(2)}, u32[]{:S(2)}) %collective-permute-start.10) | collective-permute-done | bytes 262176 | tf_op jit(solution)/shard_map/ppermute | solution.py:57
  32.4 5.6 %collective-permute-done.12.refs_3_ = bf16[64,2048]{1,0:T(8,128)(2,1)S(1)} collective-permute-done((bf16[64,2048]{1,0:T(8,128)(2,1)S(1)}, bf16[64,2048]{1,0:T(8,128)(2,1)S(1)}, u32[]{:S(2)}, u32[]{:S(2)}) %collective-permute-start.12) | collective-permute-done | bytes 262176 | tf_op jit(solution)/shard_map/ppermute | solution.py:57
  38.1 1.9 %collective-permute-start.3 = (bf16[24,2048]{1,0:T(8,128)(2,1)S(1)}, bf16[24,2048]{1,0:T(8,128)(2,1)S(1)}, u32[]{:S(2)}, u32[]{:S(2)}) collective-permute-start(bf16[24,2048]{1,0:T(8,128)(2,1)S(1)} %maximum_maximum_fusion), channel_id=1, source_target_pairs={{0,2},{2,0},{4,6},{6,4},{1,3},{3,1},{5,7},{7,5},{8,10},{10,8},{12,... | collective-permute-start | bytes 294920 | tf_op jit(solution)/shard_map/ppermute | solution.py:51
  40.0 1.2 %collective-permute-start.4 = (bf16[24,2048]{1,0:T(8,128)(2,1)S(1)}, bf16[24,2048]{1,0:T(8,128)(2,1)S(1)}, u32[]{:S(2)}, u32[]{:S(2)}) collective-permute-start(bf16[24,2048]{1,0:T(8,128)(2,1)S(1)} %maximum_maximum_fusion), channel_id=1, source_target_pairs={{0,4},{2,6},{4,0},{6,2},{1,5},{3,7},{5,1},{7,3},{8,12},{10,14},{12... | collective-permute-start | bytes 294920 | tf_op jit(solution)/shard_map/ppermute | solution.py:51
  41.2 1.4 %collective-permute-start.5 = (bf16[24,2048]{1,0:T(8,128)(2,1)S(1)}, bf16[24,2048]{1,0:T(8,128)(2,1)S(1)}, u32[]{:S(2)}, u32[]{:S(2)}) collective-permute-start(bf16[24,2048]{1,0:T(8,128)(2,1)S(1)} %maximum_maximum_fusion), channel_id=1, source_target_pairs={{0,6},{2,4},{4,2},{6,0},{1,7},{3,5},{5,3},{7,1},{8,14},{10,12},{12... | collective-permute-start | bytes 294920 | tf_op jit(solution)/shard_map/ppermute | solution.py:51
  42.6 4.3 %shard_map.118 = (bf16[64,2048]{1,0:T(8,128)(2,1)S(1)}, bf16[64,2048]{1,0:T(8,128)(2,1)S(1)}, bf16[64,2048]{1,0:T(8,128)(2,1)S(1)}, bf16[64,2048]{1,0:T(8,128)(2...) custom-call(s32[3]{0:T(128)S(1)} %copy-done.1, ...), custom_call_target="tpu_custom_call" | custom-call | flops 2147483648 | bytes 12582924 | tf_op jit(solution)/shard_map/pallas_call | solution.py:30
  48.4 2.3 %collective-permute-start.1 = (bf16[2,64,2048]{2,1,0:T(8,128)(2,1)S(1)}, bf16[2,64,2048]{2,1,0:T(8,128)(2,1)S(1)}, u32[]{:S(2)}, u32[]{:S(2)}) collective-permute-start(bf16[2,64,2048]{2,1,0:T(8,128)(2,1)S(1)} %get-tuple-element.28), channel_id=1, source_target_pairs={{0,1},{1,0},{2,3},{3,2},{4,5},{5,4},{6,7},{7,6},{8,9},{9,8},{10,11... | collective-permute-start | bytes 1572872 | tf_op jit(solution)/shard_map/ppermute | solution.py:46
  51.6 1.6 %collective-permute-done.18 = bf16[64,2048]{1,0:T(8,128)(2,1)S(1)} collective-permute-done((bf16[64,2048]{1,0:T(8,128)(2,1)S(1)}, bf16[64,2048]{1,0:T(8,128)(2,1)S(1)}, u32[]{:S(2)}, u32[]{:S(2)}) %collective-permute-start.18) | collective-permute-done | bytes 262176 | tf_op jit(solution)/shard_map/ppermute | solution.py:46
  53.2 1.5 %collective-permute-start.22 = (bf16[64,2048]{1,0:T(8,128)(2,1)S(1)}, bf16[64,2048]{1,0:T(8,128)(2,1)S(1)}, u32[]{:S(2)}, u32[]{:S(2)}) collective-permute-start(bf16[64,2048]{1,0:T(8,128)(2,1)S(1)} %add_convert_fusion.2), channel_id=1, source_target_pairs={{0,16},{1,9},{8,24},{9,1},{16,0},{17,25},{24,8},{25,17},{2,18},{3,... | collective-permute-start | bytes 786440 | tf_op jit(solution)/shard_map/ppermute | solution.py:57
  54.9 4.7 %collective-permute-done.22 = bf16[64,2048]{1,0:T(8,128)(2,1)S(1)} collective-permute-done((bf16[64,2048]{1,0:T(8,128)(2,1)S(1)}, bf16[64,2048]{1,0:T(8,128)(2,1)S(1)}, u32[]{:S(2)}, u32[]{:S(2)}) %collective-permute-start.22) | collective-permute-done | bytes 262176 | tf_op jit(solution)/shard_map/ppermute | solution.py:57
  59.5 1.5 %collective-permute-start.19 = (bf16[64,2048]{1,0:T(8,128)(2,1)S(1)}, bf16[64,2048]{1,0:T(8,128)(2,1)S(1)}, u32[]{:S(2)}, u32[]{:S(2)}) collective-permute-start(bf16[64,2048]{1,0:T(8,128)(2,1)S(1)} %add_convert_fusion.3), channel_id=1, source_target_pairs={{0,16},{1,9},{8,24},{9,1},{16,0},{17,25},{24,8},{25,17},{2,18},{3,... | collective-permute-start | bytes 786440 | tf_op jit(solution)/shard_map/ppermute | solution.py:57
  61.4 4.2 %shard_map.113 = bf16[128,2048]{1,0:T(8,128)(2,1)} custom-call(s32[3]{0:T(128)S(1)} %copy-done.1, bf16[3,128,2048]{2,1,0:T(8,128)(2,1)S(1)} %bitcast.28, bf16[2,64,2048]{2,1,0:T(8,128)(2,1)S(1)} %collective-permute-done.far_ref, bf16[2,64,2048]{2,1,0:T(8,128)(2,1)S(1)} %collective-permute-done.1.near_ref), custom_call_target="tpu_custom_call" | custom-call | flops 268435456 | bytes 3145728 | tf_op jit(solution)/shard_map/pallas_call | solution.py:380
  65.7 1.9 %shard_map.115 = bf16[24,1024]{1,0:T(8,128)(2,1)S(1)} custom-call(bf16[24,1024]{1,0:T(8,128)(2,1)S(1)} %pad_maximum_fusion.1.q_ref, bf16[96,2048]{1,0:T(8,128)(2,1)S(1)} %pad_maximum_fusion.near_ref, bf16[96,2048]{1,0:T(8,128)(2,1)S(1)} %collective-permute-done.6.far_ref), custom_call_target="tpu_custom_call" | custom-call | flops 18874368 | bytes 884736 | tf_op jit(solution)/shard_map/pallas_call | solution.py:30
  68.1 1.8 %collective-permute-start.24 = (bf16[24,2048]{1,0:T(8,128)(2,1)S(1)}, bf16[24,2048]{1,0:T(8,128)(2,1)S(1)}, u32[]{:S(2)}, u32[]{:S(2)}) collective-permute-start(bf16[24,2048]{1,0:T(8,128)(2,1)S(1)} %get-tuple-element.46), channel_id=1, source_target_pairs={{0,2},{2,0},{4,6},{6,4},{1,3},{3,1},{5,7},{7,5},{8,10},{10,8},{12,... | collective-permute-start | bytes 294920 | tf_op jit(solution)/shard_map/ppermute | solution.py:51
  69.9 1.7 %collective-permute-start.25 = (bf16[24,2048]{1,0:T(8,128)(2,1)S(1)}, bf16[24,2048]{1,0:T(8,128)(2,1)S(1)}, u32[]{:S(2)}, u32[]{:S(2)}) collective-permute-start(bf16[24,2048]{1,0:T(8,128)(2,1)S(1)} %get-tuple-element.47), channel_id=1, source_target_pairs={{0,4},{2,6},{4,0},{6,2},{1,5},{3,7},{5,1},{7,3},{8,12},{10,14},{12... | collective-permute-start | bytes 294920 | tf_op jit(solution)/shard_map/ppermute | solution.py:51
  73.7 5.7 %collective-permute-done.25 = bf16[24,2048]{1,0:T(8,128)(2,1)S(1)} collective-permute-done((bf16[24,2048]{1,0:T(8,128)(2,1)S(1)}, bf16[24,2048]{1,0:T(8,128)(2,1)S(1)}, u32[]{:S(2)}, u32[]{:S(2)}) %collective-permute-start.25) | collective-permute-done | bytes 98336 | tf_op jit(solution)/shard_map/ppermute | solution.py:51
  80.8 1.4 %shard_map.120 = bf16[12,4096]{1,0:T(8,128)(2,1)} custom-call(s32[3]{0:T(128)S(1)} %copy-done.1, s32[1,1]{1,0:T(1,128)} %copy.15.count_ref, bf16[24,2048]{1,0:T(8,128)(2,1)S(1)} %add_convert_fusion.4.mine_ref, bf16[24,2048]{1,0:T(8,128)(2,1)S(1)} %collective-permute-done.27.peer_ref, s32[1,128]{1,0:T(1,128)S(1)} %bitcast.30, bf16[1,128]{1,0:T(2,128)(2,1)S(1)} %copy-done.3), custom_call_target="tpu_custom_call" | custom-call | flops 2359296 | bytes 295696 | tf_op jit(solution)/shard_map/pallas_call | solution.py:30
  (71 shorter events, 10.1 us)
Async XLA Ops:
  8.5 6.1 %collective-permute-start.7 = (bf16[24,2048]{1,0:T(8,128)(2,1)S(1)}, bf16[24,2048]{1,0:T(8,128)(2,1)S(1)}, u32[]{:S(2)}, u32[]{:S(2)}) collective-permute-start(bf16[24,2048]{1,0:T(8,128)(2,1)S(1)} %add.37.refs_0_), channel_id=1, source_target_pairs={{0,2},{2,0},{4,6},{6,4},{1,3},{3,1},{5,7},{7,5},{8,10},{10,8},{12,... | collective-permute-start | bytes 294920 | tf_op jit(solution)/shard_map/ppermute | solution.py:51
  11.1 10.8 %collective-permute-start.8 = (bf16[24,2048]{1,0:T(8,128)(2,1)S(1)}, bf16[24,2048]{1,0:T(8,128)(2,1)S(1)}, u32[]{:S(2)}, u32[]{:S(2)}) collective-permute-start(bf16[24,2048]{1,0:T(8,128)(2,1)S(1)} %add.37.refs_0_), channel_id=1, source_target_pairs={{0,4},{2,6},{4,0},{6,2},{1,5},{3,7},{5,1},{7,3},{8,12},{10,14},{12... | collective-permute-start | bytes 294920 | tf_op jit(solution)/shard_map/ppermute | solution.py:51
  13.7 8.2 %collective-permute-start.9 = (bf16[24,2048]{1,0:T(8,128)(2,1)S(1)}, bf16[24,2048]{1,0:T(8,128)(2,1)S(1)}, u32[]{:S(2)}, u32[]{:S(2)}) collective-permute-start(bf16[24,2048]{1,0:T(8,128)(2,1)S(1)} %add.37.refs_0_), channel_id=1, source_target_pairs={{0,6},{2,4},{4,2},{6,0},{1,7},{3,5},{5,3},{7,1},{8,14},{10,12},{12... | collective-permute-start | bytes 294920 | tf_op jit(solution)/shard_map/ppermute | solution.py:51
  22.4 9.2 %collective-permute-start.10 = (bf16[64,2048]{1,0:T(8,128)(2,1)S(1)}, bf16[64,2048]{1,0:T(8,128)(2,1)S(1)}, u32[]{:S(2)}, u32[]{:S(2)}) collective-permute-start(bf16[64,2048]{1,0:T(8,128)(2,1)S(1)} %get-tuple-element.34.refs_0_), channel_id=1, source_target_pairs={{0,16},{1,9},{8,24},{9,1},{16,0},{17,25},{24,8},{25,17},{2,18},{3,... | collective-permute-start | bytes 786440 | tf_op jit(solution)/shard_map/ppermute | solution.py:57
  24.0 8.3 %collective-permute-start.11 = (bf16[64,2048]{1,0:T(8,128)(2,1)S(1)}, bf16[64,2048]{1,0:T(8,128)(2,1)S(1)}, u32[]{:S(2)}, u32[]{:S(2)}) collective-permute-start(bf16[64,2048]{1,0:T(8,128)(2,1)S(1)} %get-tuple-element.34.refs_0_), channel_id=1, source_target_pairs={{0,8},{1,17},{8,0},{9,25},{16,24},{17,1},{24,16},{25,9},{2,10},{3,... | collective-permute-start | bytes 786440 | tf_op jit(solution)/shard_map/ppermute | solution.py:57
  31.7 6.4 %collective-permute-start.12 = (bf16[64,2048]{1,0:T(8,128)(2,1)S(1)}, bf16[64,2048]{1,0:T(8,128)(2,1)S(1)}, u32[]{:S(2)}, u32[]{:S(2)}) collective-permute-start(bf16[64,2048]{1,0:T(8,128)(2,1)S(1)} %collective-permute-done.10.refs_1_), channel_id=1, source_target_pairs={{0,8},{1,17},{8,0},{9,25},{16,24},{17,1},{24,16},{25,9},{2,10},{3,... | collective-permute-start | bytes 786440 | tf_op jit(solution)/shard_map/ppermute | solution.py:57
  31.8 8.3 %collective-permute-start.13 = (bf16[64,2048]{1,0:T(8,128)(2,1)S(1)}, bf16[64,2048]{1,0:T(8,128)(2,1)S(1)}, u32[]{:S(2)}, u32[]{:S(2)}) collective-permute-start(bf16[64,2048]{1,0:T(8,128)(2,1)S(1)} %get-tuple-element.34.refs_0_), channel_id=1, source_target_pairs={{0,1},{1,0},{2,3},{3,2},{4,5},{5,4},{6,7},{7,6},{8,9},{9,8},{10,11... | collective-permute-start | bytes 786440 | tf_op jit(solution)/shard_map/ppermute | solution.py:46
  31.8 10.8 %collective-permute-start.15 = (bf16[64,2048]{1,0:T(8,128)(2,1)S(1)}, bf16[64,2048]{1,0:T(8,128)(2,1)S(1)}, u32[]{:S(2)}, u32[]{:S(2)}) collective-permute-start(bf16[64,2048]{1,0:T(8,128)(2,1)S(1)} %collective-permute-done.10.refs_1_), channel_id=1, source_target_pairs={{0,1},{1,0},{2,3},{3,2},{4,5},{5,4},{6,7},{7,6},{8,9},{9,8},{10,11... | collective-permute-start | bytes 786440 | tf_op jit(solution)/shard_map/ppermute | solution.py:46
  32.3 8.9 %collective-permute-start.14 = (bf16[64,2048]{1,0:T(8,128)(2,1)S(1)}, bf16[64,2048]{1,0:T(8,128)(2,1)S(1)}, u32[]{:S(2)}, u32[]{:S(2)}) collective-permute-start(bf16[64,2048]{1,0:T(8,128)(2,1)S(1)} %collective-permute-done.11.refs_2_), channel_id=1, source_target_pairs={{0,1},{1,0},{2,3},{3,2},{4,5},{5,4},{6,7},{7,6},{8,9},{9,8},{10,11... | collective-permute-start | bytes 786440 | tf_op jit(solution)/shard_map/ppermute | solution.py:46
  38.0 4.6 %collective-permute-start.16 = (bf16[64,2048]{1,0:T(8,128)(2,1)S(1)}, bf16[64,2048]{1,0:T(8,128)(2,1)S(1)}, u32[]{:S(2)}, u32[]{:S(2)}) collective-permute-start(bf16[64,2048]{1,0:T(8,128)(2,1)S(1)} %collective-permute-done.12.refs_3_), channel_id=1, source_target_pairs={{0,1},{1,0},{2,3},{3,2},{4,5},{5,4},{6,7},{7,6},{8,9},{9,8},{10,11... | collective-permute-start | bytes 786440 | tf_op jit(solution)/shard_map/ppermute | solution.py:46
  38.1 10.3 %collective-permute-start.3 = (bf16[24,2048]{1,0:T(8,128)(2,1)S(1)}, bf16[24,2048]{1,0:T(8,128)(2,1)S(1)}, u32[]{:S(2)}, u32[]{:S(2)}) collective-permute-start(bf16[24,2048]{1,0:T(8,128)(2,1)S(1)} %maximum_maximum_fusion), channel_id=1, source_target_pairs={{0,2},{2,0},{4,6},{6,4},{1,3},{3,1},{5,7},{7,5},{8,10},{10,8},{12,... | collective-permute-start | bytes 294920 | tf_op jit(solution)/shard_map/ppermute | solution.py:51
  40.0 10.8 %collective-permute-start.4 = (bf16[24,2048]{1,0:T(8,128)(2,1)S(1)}, bf16[24,2048]{1,0:T(8,128)(2,1)S(1)}, u32[]{:S(2)}, u32[]{:S(2)}) collective-permute-start(bf16[24,2048]{1,0:T(8,128)(2,1)S(1)} %maximum_maximum_fusion), channel_id=1, source_target_pairs={{0,4},{2,6},{4,0},{6,2},{1,5},{3,7},{5,1},{7,3},{8,12},{10,14},{12... | collective-permute-start | bytes 294920 | tf_op jit(solution)/shard_map/ppermute | solution.py:51
  41.2 9.6 %collective-permute-start.5 = (bf16[24,2048]{1,0:T(8,128)(2,1)S(1)}, bf16[24,2048]{1,0:T(8,128)(2,1)S(1)}, u32[]{:S(2)}, u32[]{:S(2)}) collective-permute-start(bf16[24,2048]{1,0:T(8,128)(2,1)S(1)} %maximum_maximum_fusion), channel_id=1, source_target_pairs={{0,6},{2,4},{4,2},{6,0},{1,7},{3,5},{5,3},{7,1},{8,14},{10,12},{12... | collective-permute-start | bytes 294920 | tf_op jit(solution)/shard_map/ppermute | solution.py:51
  47.0 4.5 %collective-permute-start.21 = (bf16[64,2048]{1,0:T(8,128)(2,1)S(1)}, bf16[64,2048]{1,0:T(8,128)(2,1)S(1)}, u32[]{:S(2)}, u32[]{:S(2)}) collective-permute-start(bf16[64,2048]{1,0:T(8,128)(2,1)S(1)} %get-tuple-element.44), channel_id=1, source_target_pairs={{0,1},{1,0},{2,3},{3,2},{4,5},{5,4},{6,7},{7,6},{8,9},{9,8},{10,11... | collective-permute-start | bytes 786440 | tf_op jit(solution)/shard_map/ppermute | solution.py:46
  47.7 13.5 %collective-permute-start = (bf16[2,64,2048]{2,1,0:T(8,128)(2,1)S(1)}, bf16[2,64,2048]{2,1,0:T(8,128)(2,1)S(1)}, u32[]{:S(2)}, u32[]{:S(2)}) collective-permute-start(bf16[2,64,2048]{2,1,0:T(8,128)(2,1)S(1)} %get-tuple-element.27), channel_id=1, source_target_pairs={{1,2},{3,4},{5,6},{2,1},{4,3},{6,5},{9,10},{11,12},{13,14},{10,9},... | collective-permute-start | bytes 1572872 | tf_op jit(solution)/shard_map/ppermute | solution.py:359
  48.4 13.0 %collective-permute-start.1 = (bf16[2,64,2048]{2,1,0:T(8,128)(2,1)S(1)}, bf16[2,64,2048]{2,1,0:T(8,128)(2,1)S(1)}, u32[]{:S(2)}, u32[]{:S(2)}) collective-permute-start(bf16[2,64,2048]{2,1,0:T(8,128)(2,1)S(1)} %get-tuple-element.28), channel_id=1, source_target_pairs={{0,1},{1,0},{2,3},{3,2},{4,5},{5,4},{6,7},{7,6},{8,9},{9,8},{10,11... | collective-permute-start | bytes 1572872 | tf_op jit(solution)/shard_map/ppermute | solution.py:46
  50.8 14.8 %collective-permute-start.6 = (bf16[96,2048]{1,0:T(8,128)(2,1)S(1)}, bf16[96,2048]{1,0:T(8,128)(2,1)S(1)}, u32[]{:S(2)}, u32[]{:S(2)}) collective-permute-start(bf16[96,2048]{1,0:T(8,128)(2,1)S(1)} %pad_maximum_fusion.near_ref), channel_id=1, source_target_pairs={{0,1},{1,0},{2,3},{3,2},{4,5},{5,4},{6,7},{7,6},{8,9},{9,8},{10,11... | collective-permute-start | bytes 1179656 | tf_op jit(solution)/shard_map/ppermute | solution.py:46
  53.2 6.4 %collective-permute-start.22 = (bf16[64,2048]{1,0:T(8,128)(2,1)S(1)}, bf16[64,2048]{1,0:T(8,128)(2,1)S(1)}, u32[]{:S(2)}, u32[]{:S(2)}) collective-permute-start(bf16[64,2048]{1,0:T(8,128)(2,1)S(1)} %add_convert_fusion.2), channel_id=1, source_target_pairs={{0,16},{1,9},{8,24},{9,1},{16,0},{17,25},{24,8},{25,17},{2,18},{3,... | collective-permute-start | bytes 786440 | tf_op jit(solution)/shard_map/ppermute | solution.py:57
  54.8 12.8 %collective-permute-start.17 = (bf16[64,2048]{1,0:T(8,128)(2,1)S(1)}, bf16[64,2048]{1,0:T(8,128)(2,1)S(1)}, u32[]{:S(2)}, u32[]{:S(2)}) collective-permute-start(bf16[64,2048]{1,0:T(8,128)(2,1)S(1)} %get-tuple-element.38), channel_id=1, source_target_pairs={{0,1},{1,0},{2,3},{3,2},{4,5},{5,4},{6,7},{7,6},{8,9},{9,8},{10,11... | collective-permute-start | bytes 786440 | tf_op jit(solution)/shard_map/ppermute | solution.py:46
  59.5 8.1 %collective-permute-start.19 = (bf16[64,2048]{1,0:T(8,128)(2,1)S(1)}, bf16[64,2048]{1,0:T(8,128)(2,1)S(1)}, u32[]{:S(2)}, u32[]{:S(2)}) collective-permute-start(bf16[64,2048]{1,0:T(8,128)(2,1)S(1)} %add_convert_fusion.3), channel_id=1, source_target_pairs={{0,16},{1,9},{8,24},{9,1},{16,0},{17,25},{24,8},{25,17},{2,18},{3,... | collective-permute-start | bytes 786440 | tf_op jit(solution)/shard_map/ppermute | solution.py:57
  61.2 6.4 %collective-permute-start.23 = (bf16[64,2048]{1,0:T(8,128)(2,1)S(1)}, bf16[64,2048]{1,0:T(8,128)(2,1)S(1)}, u32[]{:S(2)}, u32[]{:S(2)}) collective-permute-start(bf16[64,2048]{1,0:T(8,128)(2,1)S(1)} %add_convert_fusion.1), channel_id=1, source_target_pairs={{0,8},{1,17},{8,0},{9,25},{16,24},{17,1},{24,16},{25,9},{2,10},{3,... | collective-permute-start | bytes 786440 | tf_op jit(solution)/shard_map/ppermute | solution.py:57
  68.1 5.6 %collective-permute-start.24 = (bf16[24,2048]{1,0:T(8,128)(2,1)S(1)}, bf16[24,2048]{1,0:T(8,128)(2,1)S(1)}, u32[]{:S(2)}, u32[]{:S(2)}) collective-permute-start(bf16[24,2048]{1,0:T(8,128)(2,1)S(1)} %get-tuple-element.46), channel_id=1, source_target_pairs={{0,2},{2,0},{4,6},{6,4},{1,3},{3,1},{5,7},{7,5},{8,10},{10,8},{12,... | collective-permute-start | bytes 294920 | tf_op jit(solution)/shard_map/ppermute | solution.py:51
  69.9 9.5 %collective-permute-start.25 = (bf16[24,2048]{1,0:T(8,128)(2,1)S(1)}, bf16[24,2048]{1,0:T(8,128)(2,1)S(1)}, u32[]{:S(2)}, u32[]{:S(2)}) collective-permute-start(bf16[24,2048]{1,0:T(8,128)(2,1)S(1)} %get-tuple-element.47), channel_id=1, source_target_pairs={{0,4},{2,6},{4,0},{6,2},{1,5},{3,7},{5,1},{7,3},{8,12},{10,14},{12... | collective-permute-start | bytes 294920 | tf_op jit(solution)/shard_map/ppermute | solution.py:51
  71.6 7.9 %collective-permute-start.26 = (bf16[24,2048]{1,0:T(8,128)(2,1)S(1)}, bf16[24,2048]{1,0:T(8,128)(2,1)S(1)}, u32[]{:S(2)}, u32[]{:S(2)}) collective-permute-start(bf16[24,2048]{1,0:T(8,128)(2,1)S(1)} %get-tuple-element.48), channel_id=1, source_target_pairs={{0,6},{2,4},{4,2},{6,0},{1,7},{3,5},{5,3},{7,1},{8,14},{10,12},{12... | collective-permute-start | bytes 294920 | tf_op jit(solution)/shard_map/ppermute | solution.py:51
  (10 other events, 125.7 us)

commit v4 on v3

--- a/solution.py
+++ b/solution.py
@@ -51,9 +51,9 @@
     return lax.ppermute(x, "seq", [(i, i ^ mask) for i in range(n)])
 
 
-def swap_doc(x, first):
-    masks = (2, 1) if first else (1, 2)
-    pairs = [(2 * d + c, 2 * (d ^ masks[c]) + c) for d in range(lax.axis_size("dp")) for c in range(2)]
+def swap_doc(x, masks):
+    docs = range(lax.axis_size("dp"))
+    pairs = [(2 * d + c, 2 * (d ^ masks[c]) + c) for d in docs for c in range(2)]
     return lax.ppermute(x, ("dp", "fsdp"), pairs)
 
 
@@ -89,108 +89,105 @@
     return total
 
 
-def slot_rows_of(order_ref, rows, shift):
+def pick_kernel(count_ref, tokens_ref, order_ref, gain_ref, out_ref):
+    rows, half = out_ref.shape
+    slot = lax.rem(iota((rows, 1), 0), CAP)
     lanes = iota((rows, TILE), 1)
-    wanted = iota((rows, TILE), 0) - shift
     order = jnp.broadcast_to(order_ref[...], (rows, TILE))
-    return jnp.sum(jnp.where(lanes == wanted, order, 0), axis=1, keepdims=True)
-
-
-def pick_kernel(core_ref, count_ref, tokens_ref, order_ref, gain_ref, mine_ref, send_ref, all_ref):
-    rows, half = mine_ref.shape
-    core = core_ref[0]
-    shift = core * CAP
-    slot = iota((rows, 1), 0) - shift
-    own = (slot >= 0) & (slot < CAP)
-    picker = (slot_rows_of(order_ref, rows, shift) == iota((rows, TILE), 1)) & own
-    x = jnp.dot(picker.astype(BF16), tokens_ref[...], preferred_element_type=F32)
+    row = jnp.sum(jnp.where(lanes == slot, order, 0), axis=1, keepdims=True)
+    x = jnp.dot((lanes == row).astype(BF16), tokens_ref[...], preferred_element_type=F32)
     scale = lax.rsqrt(jnp.mean(x * x, axis=1, keepdims=True) + 1e-06)
-    dead = own & (slot >= count_ref[0, 0])
-    all_ref[...] = jnp.where(dead, MARK, x * scale * gain_ref[...]).astype(BF16)
-    mine_ref[...] = all_ref[:, pl.ds(pl.multiple_of(core * half, 128), half)]
-    send_ref[...] = all_ref[:, pl.ds(pl.multiple_of((1 - core) * half, 128), half)]
-
-
-def pick_rows(core, counts, tokens, order, gain):
+    first = iota((rows, 1), 0) < CAP
+    x = jnp.where(first, x[:, :half], x[:, half:])
+    gain = jnp.where(first, gain_ref[:, :half], gain_ref[:, half:])
+    dead = slot >= count_ref[0, 0]
+    out_ref[...] = jnp.where(dead, MARK, x * scale * gain).astype(BF16)
+
+
+def pick_rows(counts, tokens, order, gain):
     rows, width = 2 * CAP, tokens.shape[1]
     return call(
         pick_kernel,
-        [struct((rows, width // 2))] * 2,
-        [core, counts, tokens, order, gain],
-        2,
+        [struct((rows, width // 2))],
+        [counts, tokens, order, gain],
+        1,
         2 * rows * TILE * width,
         room=54 << 20,
-        scratch_shapes=[pltpu.VMEM((rows, width), BF16)],
-    )
+    )[0]
 
 
 def compact_kernel(parts, *refs):
-    ins, (out_ref, place_ref) = refs[:parts], refs[parts:]
+    mine, peer, (out_ref, place_ref) = refs[:parts], refs[parts : 2 * parts], refs[2 * parts :]
     live_rows, width = out_ref.shape
-    n = ins[0].shape[0]
+    n = mine[0].shape[0]
+    core = lax.axis_index("fsdp")
     up, side = iota((n, n), 0), iota((n, n), 1)
+    turned = jnp.where(lax.rem(side, 2 * CAP) < CAP, side + CAP, side - CAP)
+    own = (lax.rem(iota((n, 1), 0), 2 * CAP) < CAP) == (core == 0)
+    usable = (lax.rem(iota((1, n), 1), 2 * CAP) < CAP) == (core == 0)
     base = jnp.zeros((1, 1), F32)
     total = jnp.zeros((live_rows, width), F32)
-    for k, ref in enumerate(ins):
-        live = jnp.where(ref[:, 0:128].astype(F32)[:, 0:1] < MARK / 2, 1.0, 0.0)
-        live_row = jnp.sum(jnp.where(up == side, live, 0.0), axis=0, keepdims=True)
-        ahead_row = jnp.sum(jnp.where(up < side, live, 0.0), axis=0, keepdims=True) + base
-        ahead = jnp.sum(jnp.where(side < up, live_row, 0.0), axis=1, keepdims=True) + base
-        to_row = iota((live_rows, n), 0).astype(F32) == ahead_row
-        pick = jnp.where(to_row & (live_row > 0.5), 1.0, 0.0).astype(BF16)
-        total = total + jnp.dot(pick, ref[...], preferred_element_type=F32)
+    for k in range(parts):
+        mark = jnp.where(
+            own, mine[k][:, 0:128].astype(F32)[:, 0:1], peer[k][:, 0:128].astype(F32)[:, 0:1]
+        )
+        live = jnp.where(mark < MARK / 2, 1.0, 0.0)
+        for ref, at in ((mine[k], side), (peer[k], turned)):
+            there = jnp.sum(jnp.where(up == at, live, 0.0), axis=0, keepdims=True)
+            ahead = jnp.sum(jnp.where(up < at, live, 0.0), axis=0, keepdims=True) + base
+            to_row = iota((live_rows, n), 0).astype(F32) == ahead
+            pick = jnp.where(to_row & (there > 0.5) & usable, 1.0, 0.0).astype(BF16)
+            total = total + jnp.dot(pick, ref[...], preferred_element_type=F32)
+        row = jnp.sum(jnp.where(up == side, live, 0.0), axis=0, keepdims=True)
+        ahead = jnp.sum(jnp.where(side < up, row, 0.0), axis=1, keepdims=True) + base
         at = iota((n, live_rows), 1).astype(F32) == ahead
         place_ref[k, :, :] = jnp.where(at & (live > 0.5), 1.0, 0.0).astype(BF16)
         base = base + jnp.sum(live, axis=0, keepdims=True)
     out_ref[...] = total.astype(BF16)
 
 
-def compact(parts, live_rows):
-    n, width = parts[0].shape
+def compact(mine, peer, live_rows):
+    n, width = mine[0].shape
     return call(
-        functools.partial(compact_kernel, len(parts)),
-        [struct((live_rows, width)), struct((len(parts), n, live_rows))],
-        parts,
+        functools.partial(compact_kernel, len(mine)),
+        [struct((live_rows, width)), struct((len(mine), n, live_rows))],
+        [*mine, *peer],
         0,
-        2 * len(parts) * n * live_rows * width,
-    )
-
-
-def spread_kernel(parts, place_ref, rows_ref, *outs):
+        4 * len(mine) * n * live_rows * width,
+    )
+
+
+def spread_kernel(parts, terms, place_ref, *refs):
+    rows = sum(r[...].astype(F32) for r in refs[:terms]).astype(BF16)
     for k in range(parts):
-        outs[k][...] = jnp.dot(
-            place_ref[k, :, :], rows_ref[...], preferred_element_type=F32
+        refs[terms + k][...] = jnp.dot(
+            place_ref[k, :, :], rows, preferred_element_type=F32
         ).astype(BF16)
 
 
-def spread(place, rows):
+def spread(place, terms):
     parts, n, live_rows = place.shape
-    width = rows.shape[1]
+    width = terms[0].shape[1]
     return call(
-        functools.partial(spread_kernel, parts),
+        functools.partial(spread_kernel, parts, len(terms)),
         [struct((n, width))] * parts,
-        [place, rows],
+        [place, *terms],
         0,
         2 * parts * n * live_rows * width,
     )
 
 
-def ffn_kernel(core_ref, *refs):
-    mine, peer, (win_ref, wout_ref), send, keep = (
-        refs[0:4],
-        refs[4:8],
-        refs[8:10],
-        refs[10:14],
-        refs[14:18],
-    )
-    core = core_ref[0]
+def ffn_kernel(n, *refs):
+    mine, peer, (win_ref, wout_ref) = refs[:n], refs[n : 2 * n], refs[2 * n : 2 * n + 2]
+    send, keep = refs[2 * n + 2 : 3 * n + 2], refs[3 * n + 2 :]
+    core = lax.axis_index("fsdp")
     rows, half = mine[0].shape
     at_mine = pl.multiple_of(core * half, 128)
     at_peer = pl.multiple_of((1 - core) * half, 128)
-    group = max(1, min(4, 256 // rows))
+    group = max(1, min(n, 256 // rows))
     step = 256
-    for first in range(0, 4, group):
-        roles = range(first, first + group)
+    for first in range(0, n, group):
+        roles = range(first, min(n, first + group))
         x_mine = jnp.concatenate([mine[r][...] for r in roles], axis=0)
         x_peer = jnp.concatenate([peer[r][...] for r in roles], axis=0)
         total = jnp.dot(x_mine, win_ref[pl.ds(at_mine, half), :], preferred_element_type=F32)
@@ -210,38 +207,40 @@
         lax.fori_loop(0, half // step, columns, 0)
 
 
-def ffn(core, mine, peer, win, wout):
+def ffn(mine, peer, win, wout):
+    n = len(mine)
     rows, half = mine[0].shape
-    units = win.shape[1]
     outs = call(
-        ffn_kernel,
-        [struct((rows, half))] * 8,
-        [core, *mine, *peer, win, wout],
-        1,
-        4 * 4 * rows * 2 * half * units,
-    )
-    return outs[:4], outs[4:]
-
-
-def finish_kernel(core_ref, count_ref, mine_ref, peer_ref, order_ref, score_ref, out_ref):
+        functools.partial(ffn_kernel, n),
+        [struct((rows, half))] * (2 * n),
+        [*mine, *peer, win, wout],
+        0,
+        4 * n * rows * 2 * half * win.shape[1],
+    )
+    return outs[:n], outs[n:]
+
+
+def finish_kernel(count_ref, mine_ref, peer_ref, order_ref, score_ref, out_ref):
     rows, half = mine_ref.shape
-    core = core_ref[0]
+    core = lax.axis_index("fsdp")
     pick = (iota((CAP, rows), 1) == iota((CAP, rows), 0) + core * CAP).astype(BF16)
-    at = slot_rows_of(order_ref, CAP, 0) == iota((CAP, TILE), 1)
-    score = jnp.sum(jnp.where(at, score_ref[...].astype(F32), 0.0), axis=1, keepdims=True)
+    lanes, slot = iota((CAP, TILE), 1), iota((CAP, TILE), 0)
+    order = jnp.broadcast_to(order_ref[...], (CAP, TILE))
+    row = jnp.sum(jnp.where(lanes == slot, order, 0), axis=1, keepdims=True)
+    score = jnp.sum(jnp.where(lanes == row, score_ref[...].astype(F32), 0.0), axis=1, keepdims=True)
     score = jnp.where(iota((CAP, 1), 0) < count_ref[0, 0], score, 0.0)
     for ref, start in ((mine_ref, core * half), (peer_ref, (1 - core) * half)):
         y = jnp.dot(pick, ref[...], preferred_element_type=F32)
         out_ref[:, pl.ds(pl.multiple_of(start, 128), half)] = (score * y).astype(BF16)
 
 
-def finish(core, counts, mine, peer, order, score):
+def finish(counts, mine, peer, order, score):
     rows, half = mine.shape
     return call(
         finish_kernel,
         [struct((CAP, 2 * half))],
-        [core, counts, mine, peer, order, score],
-        2,
+        [counts, mine, peer, order, score],
+        1,
         4 * CAP * rows * half,
     )[0]
 
@@ -272,35 +271,40 @@
     )(*arrays)
 
 
-def routed_ffn(core, tokens, gain, win, wout, score, counts, order, heavy_qkv):
+def total(*terms):
+    return sum(t.astype(F32) for t in terms).astype(BF16)
+
+
+NEAR, OTHER, DIAGONAL = (2, 1), (1, 2), (3, 3)
+
+
+def routed_ffn(tokens, gain, win, wout, score, counts, order, heavy_qkv):
     devices = lax.axis_size("seq") * lax.axis_size("fsdp")
-    mine, send = pick_rows(core, counts, tokens, order, gain)
-    pair = mine + swap_core(send)
-    heavy_qkv, _ = lax.optimization_barrier((heavy_qkv, pair))
+    own = pick_rows(counts, tokens, order, gain)
+    heavy_qkv, _ = lax.optimization_barrier((heavy_qkv, own))
     win, wout = load(win, wout)
-    x0, place = compact(gather_seq(pair), MEAN_LIVE * devices)
-    x1 = swap_doc(x0, True)
-    x2 = swap_doc(x0, False)
-    x3 = swap_doc(x1, False)
-    mine = (x0, x1, x2, x3)
-    p0, p2, p1, p3 = [swap_core(x) for x in mine]
-    send, keep = ffn(core, mine, (p0, p1, p2, p3), win, wout)
-    back = {i: swap_core(send[i]) for i in (3, 2, 1, 0)}
-
-    def total(*terms):
-        return sum(t.astype(F32) for t in terms).astype(BF16)
-
-    got1 = swap_doc(total(keep[3], back[3]), True)
-    got2 = swap_doc(total(keep[1], back[2]), True)
-    got3 = swap_doc(total(keep[2], back[1], got1), False)
-    own = total(keep[0], back[0], got2, got3)
-    summed = scatter_seq(spread(place, own))
-    return finish(core, counts, summed, swap_core(summed), order, score), heavy_qkv
-
-
-def light_kernel(info_ref, qkv_ref, far_ref, near_ref, out_ref):
+    blocks = gather_seq(own)
+    peers = [swap_core(x) for x in blocks]
+    x0, place = compact(blocks, peers, MEAN_LIVE * devices)
+    x1 = swap_doc(x0, NEAR)
+    x2 = swap_doc(x0, OTHER)
+    x3 = swap_doc(x1, OTHER)
+    p0, p2, p1, p3 = [swap_core(x) for x in (x0, x1, x2, x3)]
+    send, keep = ffn((x0, x1, x2), (p0, p1, p2), win, wout)
+    back = [swap_core(x) for x in send]
+    got1 = swap_doc(total(keep[1], back[2]), NEAR)
+    got2 = swap_doc(total(keep[2], back[1]), OTHER)
+    send3, keep3 = ffn((x3,), (p3,), win, wout)
+    got3 = swap_doc(total(keep3[0], swap_core(send3[0])), DIAGONAL)
+    summed = scatter_seq(spread(place, (keep[0], back[0], got1, got2, got3)))
+    return finish(counts, summed, swap_core(summed), order, score), heavy_qkv
+
+
+def light_kernel(qkv_ref, far_ref, near_ref, out_ref):
     rows = qkv_ref.shape[1]
-    core, first_pos, length = info_ref[0], info_ref[1], info_ref[2]
+    core = lax.axis_index("fsdp")
+    first_pos = lax.axis_index(("seq", "fsdp")) * rows
+    length = rows * lax.axis_size("seq") * lax.axis_size("fsdp")
     span = rows + 2 * HALF_WIN
     lane = iota((rows, span), 1)
     row = iota((rows, span), 0)
@@ -326,9 +330,9 @@
         out_ref[:, at] = (y / jnp.sum(e, axis=1, keepdims=True)).astype(BF16)
 
 
-def halo_kernel(info_ref, planes_ref, far_ref, near_ref, sems):
+def halo_kernel(planes_ref, far_ref, near_ref, sems):
     last = planes_ref.shape[1] - HALF_WIN
-    edge = pl.multiple_of(info_ref[0] * last, HALF_WIN)
+    edge = pl.multiple_of(lax.axis_index("fsdp") * last, HALF_WIN)
     other = pl.multiple_of(last - edge, HALF_WIN)
     copies = [
         pltpu.make_async_copy(planes_ref.at[1:3, pl.ds(at, HALF_WIN)], ref, sems.at[i])
@@ -340,20 +344,20 @@
         c.wait()
 
 
-def light_branch(info, planes):
+def light_branch(planes):
     _, rows, width = planes.shape
     run = pl.pallas_call(
         halo_kernel,
         out_shape=[struct((2, HALF_WIN, width))] * 2,
-        in_specs=[SMEM, pl.BlockSpec(memory_space=pl.ANY)],
+        in_specs=[pl.BlockSpec(memory_space=pl.ANY)],
         out_specs=[VMEM] * 2,
         scratch_shapes=[pltpu.SemaphoreType.DMA((2,))],
         cost_estimate=pl.CostEstimate(
             flops=0, bytes_accessed=8 * HALF_WIN * width, transcendentals=0
         ),
-        compiler_params=pltpu.CompilerParams(vmem_limit_bytes=2 << 20),
-    )
-    far, near = run(info, planes)
+        compiler_params=pltpu.CompilerParams(vmem_limit_bytes=48 << 20),
+    )
+    far, near = run(planes)
     n = lax.axis_size("seq") * lax.axis_size("fsdp")
     pairs = [(i, i + 1) for i in range(1, n - 1, 2)]
     far = lax.ppermute(far, ("seq", "fsdp"), pairs + [(j, i) for i, j in pairs])
@@ -364,7 +368,6 @@
         out_shape=struct((rows, width)),
         grid=(width // wide,),
         in_specs=[
-            SMEM,
             pl.BlockSpec((3, rows, wide), lambda i: (0, 0, i)),
             pl.BlockSpec((2, HALF_WIN, wide), lambda i: (0, 0, i)),
             pl.BlockSpec((2, HALF_WIN, wide), lambda i: (0, 0, i)),
@@ -377,7 +380,7 @@
         ),
         compiler_params=pltpu.CompilerParams(vmem_limit_bytes=12 << 20),
     )
-    return run(info, planes, far, near)
+    return run(planes, far, near)
 
 
 def heavy_kernel(q_ref, near_ref, far_ref, out_ref):
@@ -433,14 +436,8 @@
     tokens, ffn_gain, in_proj, out_proj, router_score, tile_counts, tile_order, light_qkv, heavy_qkv
 ):
     assert tile_order.shape[1] == 1 and lax.axis_size("fsdp") == 2 and lax.axis_size("dp") == 4
-    here = lax.axis_index(("seq", "fsdp")) * tokens.shape[1]
-    length = tokens.shape[1] * lax.axis_size("seq") * lax.axis_size("fsdp")
-    info = jnp.stack([lax.axis_index("fsdp"), here, jnp.int32(length)]).astype(jnp.int32)
-    info, tokens = lax.optimization_barrier((info, tokens))
-    core = info
     slot_live = jnp.arange(CAP) < tile_counts[0, 0]
     heavy_ffn, heavy_qkv = routed_ffn(
-        core,
         tokens[0],
         ffn_gain[None],
         in_proj,
@@ -450,7 +447,7 @@
         tile_order[0],
         heavy_qkv,
     )
-    light_out = light_branch(info, jnp.transpose(light_qkv[0], (1, 0, 2)))
+    light_out = light_branch(jnp.transpose(light_qkv[0], (1, 0, 2)))
     heavy_attn = heavy_branch(heavy_qkv[0], slot_live)
     return (light_out[None], heavy_attn[None], heavy_ffn[None])
 

time: 82.4 us -> 83.9 us (1.018)
  starting transfers between devices: 25.7 us -> 31.4 us
  waiting for transfers between devices: 33.6 us -> 28.3 us
  local copies, waits for them, and re-layouts: 0.18 us -> 1.98 us
    ppermute x6, waiting for transfers between devices: 16.4 us -> 10.3 us  [swap_doc(): return lax.ppermute(x, ('dp', 'fsdp'), pairs)]
    ppermute x12 -> x15, starting transfers between devices: 4.36 us -> 7.2 us  [swap_core(): return lax.ppermute(x, 'fsdp', [(0, 1), (1, 0)])]
    ppermute x6, starting transfers between devices: 6.42 us -> 8.49 us  [swap_doc(): return lax.ppermute(x, ('dp', 'fsdp'), pairs)]
    ppermute x9, waiting for transfers between devices: 15 us -> 17 us  [swap_seq(): return lax.ppermute(x, 'seq', [(i, i ^ mask) for i in range(n)])]
    pallas_call x6 -> x7, Pallas kernels: 10.8 us -> 12.1 us  [call(): pl.pallas_call(body, out_shape=outs, in_specs=[SMEM] * scalars + [VMEM] *...]
    ppermute x12 -> x15, waiting for transfers between devices: 2.18 us -> 0.96 us  [swap_core(): return lax.ppermute(x, 'fsdp', [(0, 1), (1, 0)])]
    pallas_call x2, Pallas kernels: 4.86 us -> 3.79 us  [the longest x1 3.7 us: light_branch(): return run(planes, far, near)]
    optimization_barrier x1, local copies, waits for them, and re-layouts: 0.12 us -> 1.04 us  [routed_ffn(): heavy_qkv, _ = lax.optimization_barrier((heavy_qkv, own))]
  transfers between devices with their start and end apart: 28 -> 31, of which waited for: 10 -> 8; matrix products, arithmetic and copies ran while one was open for 2% -> 3% of each run, Pallas kernels for 18% -> 18%
where the time goes in v4:
time: 83.9 us; the launch traced here: 83.7 us
  starting transfers between devices  31.4 us (37%)
  waiting for transfers between devices  28.3 us (34%)
  Pallas kernels  19.4 us (23%)
  local copies, waits for them, and re-layouts  1.98 us (2%)
  between operations  1.48 us (2%)
  other arithmetic  1.12 us (1%)
    ppermute x9, waiting for transfers between devices, swap_seq(): return lax.ppermute(x, 'seq', [(i, i ^ mask) for i in range(n)])  17 us
    ppermute x9, starting transfers between devices, swap_seq(): return lax.ppermute(x, 'seq', [(i, i ^ mask) for i in range(n)])  15.1 us
    pallas_call x7, Pallas kernels, call(): pl.pallas_call(body, out_shape=outs, in_specs=[SMEM] * scalars + [VMEM] *...  12.1 us
    ppermute x6, waiting for transfers between devices, swap_doc(): return lax.ppermute(x, ('dp', 'fsdp'), pairs)  10.3 us
    ppermute x6, starting transfers between devices, swap_doc(): return lax.ppermute(x, ('dp', 'fsdp'), pairs)  8.49 us
    ppermute x15, starting transfers between devices, swap_core(): return lax.ppermute(x, 'fsdp', [(0, 1), (1, 0)])  7.2 us
    pallas_call x1, Pallas kernels, light_branch(): return run(planes, far, near)  3.7 us
    pallas_call x1, Pallas kernels, load(): pl.pallas_call(load_kernel, out_shape=[struct(a.shape, a.dtype) for a in...  3.48 us
  transfers between devices with their start and end apart: 31, of which 8 were waited for; matrix products, arithmetic and copies ran while one was open for 3% of the time, Pallas kernels for 18%

profile of v4, /device:TPU:0, one launch (start us, length us, event | category | flops | bytes accessed | tf_op | source)
XLA Modules:
  0.0 83.7 jit_solution(13388109469786004312)
XLA Ops:
  1.3 2.3 %shard_map.114.refs_0_ = bf16[24,2048]{1,0:T(8,128)(2,1)} custom-call(s32[1,1]{1,0:T(1,128)} %copy.15.count_ref, bf16[128,4096]{1,0:T(8,128)(2,1)} %bitcast.29, s32[1,128]{1,0:T(1,128)} %bitcast.27, f32[1,4096]{1,0:T(1,128)} %bitcast.34), custom_call_target="tpu_custom_call" | custom-call | flops 25165824 | bytes 1163780 | tf_op jit(solution)/shard_map/pallas_call | solution.py:30
  3.6 3.1 %collective-permute-start.6 = (bf16[24,2048]{1,0:T(8,128)(2,1)}, bf16[24,2048]{1,0:T(8,128)(2,1)S(1)}, u32[]{:S(2)}, u32[]{:S(2)}) collective-permute-start(bf16[24,2048]{1,0:T(8,128)(2,1)} %shard_map.114.refs_0_), channel_id=1, source_target_pairs={{0,2},{2,0},{4,6},{6,4},{1,3},{3,1},{5,7},{7,5},{8,10},{10,8},{12,... | collective-permute-start | bytes 294920 | tf_op jit(solution)/shard_map/ppermute | solution.py:51
  6.7 2.6 %collective-permute-start.7 = (bf16[24,2048]{1,0:T(8,128)(2,1)}, bf16[24,2048]{1,0:T(8,128)(2,1)S(1)}, u32[]{:S(2)}, u32[]{:S(2)}) collective-permute-start(bf16[24,2048]{1,0:T(8,128)(2,1)} %shard_map.114.refs_0_), channel_id=1, source_target_pairs={{0,4},{2,6},{4,0},{6,2},{1,5},{3,7},{5,1},{7,3},{8,12},{10,14},{12... | collective-permute-start | bytes 294920 | tf_op jit(solution)/shard_map/ppermute | solution.py:51
  10.9 6.4 %collective-permute-done.7.refs_2_ = bf16[24,2048]{1,0:T(8,128)(2,1)S(1)} collective-permute-done((bf16[24,2048]{1,0:T(8,128)(2,1)}, bf16[24,2048]{1,0:T(8,128)(2,1)S(1)}, u32[]{:S(2)}, u32[]{:S(2)}) %collective-permute-start.7) | collective-permute-done | bytes 98336 | tf_op jit(solution)/shard_map/ppermute | solution.py:51
  20.5 1.6 %collective-permute-start.13 = (bf16[64,2048]{1,0:T(8,128)(2,1)S(1)}, bf16[64,2048]{1,0:T(8,128)(2,1)S(1)}, u32[]{:S(2)}, u32[]{:S(2)}) collective-permute-start(bf16[64,2048]{1,0:T(8,128)(2,1)S(1)} %get-tuple-element.26.refs_0_), channel_id=1, source_target_pairs={{0,16},{1,9},{8,24},{9,1},{16,0},{17,25},{24,8},{25,17},{2,18},{3,... | collective-permute-start | bytes 786440 | tf_op jit(solution)/shard_map/ppermute | solution.py:57
  22.0 1.5 %collective-permute-start.14 = (bf16[64,2048]{1,0:T(8,128)(2,1)S(1)}, bf16[64,2048]{1,0:T(8,128)(2,1)S(1)}, u32[]{:S(2)}, u32[]{:S(2)}) collective-permute-start(bf16[64,2048]{1,0:T(8,128)(2,1)S(1)} %get-tuple-element.26.refs_0_), channel_id=1, source_target_pairs={{0,8},{1,17},{8,0},{9,25},{16,24},{17,1},{24,16},{25,9},{2,10},{3,... | collective-permute-start | bytes 786440 | tf_op jit(solution)/shard_map/ppermute | solution.py:57
  23.7 5.4 %collective-permute-done.13.refs_1_ = bf16[64,2048]{1,0:T(8,128)(2,1)S(1)} collective-permute-done((bf16[64,2048]{1,0:T(8,128)(2,1)S(1)}, bf16[64,2048]{1,0:T(8,128)(2,1)S(1)}, u32[]{:S(2)}, u32[]{:S(2)}) %collective-permute-start.13) | collective-permute-done | bytes 262176 | tf_op jit(solution)/shard_map/ppermute | solution.py:57
  29.1 1.7 %collective-permute-start.23 = (bf16[64,2048]{1,0:T(8,128)(2,1)S(1)}, bf16[64,2048]{1,0:T(8,128)(2,1)S(1)}, u32[]{:S(2)}, u32[]{:S(2)}) collective-permute-start(bf16[64,2048]{1,0:T(8,128)(2,1)S(1)} %collective-permute-done.13.refs_1_), channel_id=1, source_target_pairs={{0,8},{1,17},{8,0},{9,25},{16,24},{17,1},{24,16},{25,9},{2,10},{3,... | collective-permute-start | bytes 786440 | tf_op jit(solution)/shard_map/ppermute | solution.py:57
  31.4 1.3 %collective-permute-start.2 = (bf16[24,2048]{1,0:T(8,128)(2,1)S(1)}, bf16[24,2048]{1,0:T(8,128)(2,1)S(1)}, u32[]{:S(2)}, u32[]{:S(2)}) collective-permute-start(bf16[24,2048]{1,0:T(8,128)(2,1)S(1)} %maximum_maximum_fusion), channel_id=1, source_target_pairs={{0,2},{2,0},{4,6},{6,4},{1,3},{3,1},{5,7},{7,5},{8,10},{10,8},{12,... | collective-permute-start | bytes 294920 | tf_op jit(solution)/shard_map/ppermute | solution.py:51
  32.7 3.5 %shard_map.117 = (bf16[4096,512]{1,0:T(8,128)(2,1)S(1)}, bf16[512,4096]{1,0:T(8,128)(2,1)S(1)}) custom-call(bf16[4096,512]{1,0:T(8,128)(2,1)} %refs_0_.1, bf16[512,4096]{1,0:T(8,128)(2,1)} %refs_1_.1), custom_call_target="tpu_custom_call" | custom-call | bytes 8388608 | tf_op jit(solution)/shard_map/pallas_call | solution.py:259
  36.2 1.8 %collective-permute-start.3 = (bf16[24,2048]{1,0:T(8,128)(2,1)S(1)}, bf16[24,2048]{1,0:T(8,128)(2,1)S(1)}, u32[]{:S(2)}, u32[]{:S(2)}) collective-permute-start(bf16[24,2048]{1,0:T(8,128)(2,1)S(1)} %maximum_maximum_fusion), channel_id=1, source_target_pairs={{0,4},{2,6},{4,0},{6,2},{1,5},{3,7},{5,1},{7,3},{8,12},{10,14},{12... | collective-permute-start | bytes 294920 | tf_op jit(solution)/shard_map/ppermute | solution.py:51
  38.1 1.4 %collective-permute-start.4 = (bf16[24,2048]{1,0:T(8,128)(2,1)S(1)}, bf16[24,2048]{1,0:T(8,128)(2,1)S(1)}, u32[]{:S(2)}, u32[]{:S(2)}) collective-permute-start(bf16[24,2048]{1,0:T(8,128)(2,1)S(1)} %maximum_maximum_fusion), channel_id=1, source_target_pairs={{0,6},{2,4},{4,2},{6,0},{1,7},{3,5},{5,3},{7,1},{8,14},{10,12},{12... | collective-permute-start | bytes 294920 | tf_op jit(solution)/shard_map/ppermute | solution.py:51
  39.4 3.2 %shard_map.118 = (bf16[64,2048]{1,0:T(8,128)(2,1)S(1)}, bf16[64,2048]{1,0:T(8,128)(2,1)S(1)}, bf16[64,2048]{1,0:T(8,128)(2,1)S(1)}, bf16[64,2048]{1,0:T(8,128)(2...) custom-call(bf16[64,2048]{1,0:T(8,128)(2,1)S(1)} %get-tuple-element.26.refs_0_, ...), custom_call_target="tpu_custom_call" | custom-call | flops 1610612736 | bytes 11534336 | tf_op jit(solution)/shard_map/pallas_call | solution.py:30
  43.2 2.9 %collective-permute-done.3 = bf16[24,2048]{1,0:T(8,128)(2,1)S(1)} collective-permute-done((bf16[24,2048]{1,0:T(8,128)(2,1)S(1)}, bf16[24,2048]{1,0:T(8,128)(2,1)S(1)}, u32[]{:S(2)}, u32[]{:S(2)}) %collective-permute-start.3) | collective-permute-done | bytes 98336 | tf_op jit(solution)/shard_map/ppermute | solution.py:51
  46.8 2.5 %shard_map.119 = (bf16[64,2048]{1,0:T(8,128)(2,1)S(1)}, bf16[64,2048]{1,0:T(8,128)(2,1)S(1)}) custom-call(bf16[64,2048]{1,0:T(8,128)(2,1)S(1)} %collective-permute-done.23.refs_0_, bf16[64,2048]{1,0:T(8,128)(2,1)S(1)} %collective-permute-done.24.refs_1_, bf16[4096,512]{1,0:T(8,128)(2,1)S(1)} %get-tuple-element.27.refs_6_.refs_2_, ...), custom_call_target="tpu_custom_call" | custom-call | flops 536870912 | bytes 9437184 | tf_op jit(solution)/shard_map/pallas_call | solution.py:30
  50.5 1.6 %collective-permute-start.20 = (bf16[64,2048]{1,0:T(8,128)(2,1)S(1)}, bf16[64,2048]{1,0:T(8,128)(2,1)S(1)}, u32[]{:S(2)}, u32[]{:S(2)}) collective-permute-start(bf16[64,2048]{1,0:T(8,128)(2,1)S(1)} %add_convert_fusion.2), channel_id=1, source_target_pairs={{0,16},{1,9},{8,24},{9,1},{16,0},{17,25},{24,8},{25,17},{2,18},{3,... | collective-permute-start | bytes 786440 | tf_op jit(solution)/shard_map/ppermute | solution.py:57
  52.1 1.6 %collective-permute-start.26 = (bf16[64,2048]{1,0:T(8,128)(2,1)S(1)}, bf16[64,2048]{1,0:T(8,128)(2,1)S(1)}, u32[]{:S(2)}, u32[]{:S(2)}) collective-permute-start(bf16[64,2048]{1,0:T(8,128)(2,1)S(1)} %add_convert_fusion), channel_id=1, source_target_pairs={{0,24},{1,25},{8,16},{9,17},{16,8},{17,9},{24,0},{25,1},{2,26},{3,... | collective-permute-start | bytes 786440 | tf_op jit(solution)/shard_map/ppermute | solution.py:57
  54.6 1.9 %shard_map.115 = bf16[24,1024]{1,0:T(8,128)(2,1)S(1)} custom-call(bf16[24,1024]{1,0:T(8,128)(2,1)S(1)} %pad_maximum_fusion.1.q_ref, bf16[96,2048]{1,0:T(8,128)(2,1)S(1)} %pad_maximum_fusion.near_ref, bf16[96,2048]{1,0:T(8,128)(2,1)S(1)} %collective-permute-done.5.far_ref), custom_call_target="tpu_custom_call" | custom-call | flops 18874368 | bytes 884736 | tf_op jit(solution)/shard_map/pallas_call | solution.py:30
  56.6 3.8 %collective-permute-start.1 = (bf16[2,64,2048]{2,1,0:T(8,128)(2,1)S(1)}, bf16[2,64,2048]{2,1,0:T(8,128)(2,1)S(1)}, u32[]{:S(2)}, u32[]{:S(2)}) collective-permute-start(bf16[2,64,2048]{2,1,0:T(8,128)(2,1)S(1)} %get-tuple-element.23), channel_id=1, source_target_pairs={{0,1},{1,0},{2,3},{3,2},{4,5},{5,4},{6,7},{7,6},{8,9},{9,8},{10,11... | collective-permute-start | bytes 1572872 | tf_op jit(solution)/shard_map/ppermute | solution.py:46
  60.3 4.9 %collective-permute-done.26.refs_4_ = bf16[64,2048]{1,0:T(8,128)(2,1)S(1)} collective-permute-done((bf16[64,2048]{1,0:T(8,128)(2,1)S(1)}, bf16[64,2048]{1,0:T(8,128)(2,1)S(1)}, u32[]{:S(2)}, u32[]{:S(2)}) %collective-permute-start.26) | collective-permute-done | bytes 262176 | tf_op jit(solution)/shard_map/ppermute | solution.py:57
  65.7 2.4 %collective-permute-start.27 = (bf16[24,2048]{1,0:T(8,128)(2,1)S(1)}, bf16[24,2048]{1,0:T(8,128)(2,1)S(1)}, u32[]{:S(2)}, u32[]{:S(2)}) collective-permute-start(bf16[24,2048]{1,0:T(8,128)(2,1)S(1)} %get-tuple-element.38), channel_id=1, source_target_pairs={{0,2},{2,0},{4,6},{6,4},{1,3},{3,1},{5,7},{7,5},{8,10},{10,8},{12,... | collective-permute-start | bytes 294920 | tf_op jit(solution)/shard_map/ppermute | solution.py:51
  69.2 1.4 %collective-permute-start.29 = (bf16[24,2048]{1,0:T(8,128)(2,1)S(1)}, bf16[24,2048]{1,0:T(8,128)(2,1)S(1)}, u32[]{:S(2)}, u32[]{:S(2)}) collective-permute-start(bf16[24,2048]{1,0:T(8,128)(2,1)S(1)} %get-tuple-element.40), channel_id=1, source_target_pairs={{0,6},{2,4},{4,2},{6,0},{1,7},{3,5},{5,3},{7,1},{8,14},{10,12},{12... | collective-permute-start | bytes 294920 | tf_op jit(solution)/shard_map/ppermute | solution.py:51
  71.3 7.0 %collective-permute-done.28 = bf16[24,2048]{1,0:T(8,128)(2,1)S(1)} collective-permute-done((bf16[24,2048]{1,0:T(8,128)(2,1)S(1)}, bf16[24,2048]{1,0:T(8,128)(2,1)S(1)}, u32[]{:S(2)}, u32[]{:S(2)}) %collective-permute-start.28) | collective-permute-done | bytes 98336 | tf_op jit(solution)/shard_map/ppermute | solution.py:51
  79.1 3.7 %shard_map.113 = bf16[128,2048]{1,0:T(8,128)(2,1)} custom-call(bf16[3,128,2048]{2,1,0:T(8,128)(2,1)S(1)} %bitcast.26, bf16[2,64,2048]{2,1,0:T(8,128)(2,1)S(1)} %collective-permute-done.far_ref, bf16[2,64,2048]{2,1,0:T(8,128)(2,1)S(1)} %collective-permute-done.1.near_ref), custom_call_target="tpu_custom_call" | custom-call | flops 268435456 | bytes 3145728 | tf_op jit(solution)/shard_map/pallas_call | solution.py:383
  (71 shorter events, 12.6 us)
Async XLA Ops:
  6.7 10.7 %collective-permute-start.7 = (bf16[24,2048]{1,0:T(8,128)(2,1)}, bf16[24,2048]{1,0:T(8,128)(2,1)S(1)}, u32[]{:S(2)}, u32[]{:S(2)}) collective-permute-start(bf16[24,2048]{1,0:T(8,128)(2,1)} %shard_map.114.refs_0_), channel_id=1, source_target_pairs={{0,4},{2,6},{4,0},{6,2},{1,5},{3,7},{5,1},{7,3},{8,12},{10,14},{12... | collective-permute-start | bytes 294920 | tf_op jit(solution)/shard_map/ppermute | solution.py:51
  9.3 8.1 %collective-permute-start.8 = (bf16[24,2048]{1,0:T(8,128)(2,1)}, bf16[24,2048]{1,0:T(8,128)(2,1)S(1)}, u32[]{:S(2)}, u32[]{:S(2)}) collective-permute-start(bf16[24,2048]{1,0:T(8,128)(2,1)} %shard_map.114.refs_0_), channel_id=1, source_target_pairs={{0,6},{2,4},{4,2},{6,0},{1,7},{3,5},{5,3},{7,1},{8,14},{10,12},{12... | collective-permute-start | bytes 294920 | tf_op jit(solution)/shard_map/ppermute | solution.py:51
  9.3 8.6 %collective-permute-start.9 = (bf16[24,2048]{1,0:T(8,128)(2,1)}, bf16[24,2048]{1,0:T(8,128)(2,1)S(1)}, u32[]{:S(2)}, u32[]{:S(2)}) collective-permute-start(bf16[24,2048]{1,0:T(8,128)(2,1)} %shard_map.114.refs_0_), channel_id=1, source_target_pairs={{0,1},{1,0},{2,3},{3,2},{4,5},{5,4},{6,7},{7,6},{8,9},{9,8},{10,11... | collective-permute-start | bytes 294920 | tf_op jit(solution)/shard_map/ppermute | solution.py:46
  10.3 7.5 %collective-permute-start.10 = (bf16[24,2048]{1,0:T(8,128)(2,1)S(1)}, bf16[24,2048]{1,0:T(8,128)(2,1)S(1)}, u32[]{:S(2)}, u32[]{:S(2)}) collective-permute-start(bf16[24,2048]{1,0:T(8,128)(2,1)S(1)} %collective-permute-done.6.refs_1_), channel_id=1, source_target_pairs={{0,1},{1,0},{2,3},{3,2},{4,5},{5,4},{6,7},{7,6},{8,9},{9,8},{10,11... | collective-permute-start | bytes 294920 | tf_op jit(solution)/shard_map/ppermute | solution.py:46
  20.5 8.6 %collective-permute-start.13 = (bf16[64,2048]{1,0:T(8,128)(2,1)S(1)}, bf16[64,2048]{1,0:T(8,128)(2,1)S(1)}, u32[]{:S(2)}, u32[]{:S(2)}) collective-permute-start(bf16[64,2048]{1,0:T(8,128)(2,1)S(1)} %get-tuple-element.26.refs_0_), channel_id=1, source_target_pairs={{0,16},{1,9},{8,24},{9,1},{16,0},{17,25},{24,8},{25,17},{2,18},{3,... | collective-permute-start | bytes 786440 | tf_op jit(solution)/shard_map/ppermute | solution.py:57
  22.0 8.8 %collective-permute-start.14 = (bf16[64,2048]{1,0:T(8,128)(2,1)S(1)}, bf16[64,2048]{1,0:T(8,128)(2,1)S(1)}, u32[]{:S(2)}, u32[]{:S(2)}) collective-permute-start(bf16[64,2048]{1,0:T(8,128)(2,1)S(1)} %get-tuple-element.26.refs_0_), channel_id=1, source_target_pairs={{0,8},{1,17},{8,0},{9,25},{16,24},{17,1},{24,16},{25,9},{2,10},{3,... | collective-permute-start | bytes 786440 | tf_op jit(solution)/shard_map/ppermute | solution.py:57
  23.6 12.6 %collective-permute-start.15 = (bf16[64,2048]{1,0:T(8,128)(2,1)S(1)}, bf16[64,2048]{1,0:T(8,128)(2,1)S(1)}, u32[]{:S(2)}, u32[]{:S(2)}) collective-permute-start(bf16[64,2048]{1,0:T(8,128)(2,1)S(1)} %get-tuple-element.26.refs_0_), channel_id=1, source_target_pairs={{0,1},{1,0},{2,3},{3,2},{4,5},{5,4},{6,7},{7,6},{8,9},{9,8},{10,11... | collective-permute-start | bytes 786440 | tf_op jit(solution)/shard_map/ppermute | solution.py:46
  29.1 8.9 %collective-permute-start.23 = (bf16[64,2048]{1,0:T(8,128)(2,1)S(1)}, bf16[64,2048]{1,0:T(8,128)(2,1)S(1)}, u32[]{:S(2)}, u32[]{:S(2)}) collective-permute-start(bf16[64,2048]{1,0:T(8,128)(2,1)S(1)} %collective-permute-done.13.refs_1_), channel_id=1, source_target_pairs={{0,8},{1,17},{8,0},{9,25},{16,24},{17,1},{24,16},{25,9},{2,10},{3,... | collective-permute-start | bytes 786440 | tf_op jit(solution)/shard_map/ppermute | solution.py:57
  30.8 8.6 %collective-permute-start.17 = (bf16[64,2048]{1,0:T(8,128)(2,1)S(1)}, bf16[64,2048]{1,0:T(8,128)(2,1)S(1)}, u32[]{:S(2)}, u32[]{:S(2)}) collective-permute-start(bf16[64,2048]{1,0:T(8,128)(2,1)S(1)} %collective-permute-done.13.refs_1_), channel_id=1, source_target_pairs={{0,1},{1,0},{2,3},{3,2},{4,5},{5,4},{6,7},{7,6},{8,9},{9,8},{10,11... | collective-permute-start | bytes 786440 | tf_op jit(solution)/shard_map/ppermute | solution.py:46
  30.9 8.6 %collective-permute-start.16 = (bf16[64,2048]{1,0:T(8,128)(2,1)S(1)}, bf16[64,2048]{1,0:T(8,128)(2,1)S(1)}, u32[]{:S(2)}, u32[]{:S(2)}) collective-permute-start(bf16[64,2048]{1,0:T(8,128)(2,1)S(1)} %collective-permute-done.14.refs_2_), channel_id=1, source_target_pairs={{0,1},{1,0},{2,3},{3,2},{4,5},{5,4},{6,7},{7,6},{8,9},{9,8},{10,11... | collective-permute-start | bytes 786440 | tf_op jit(solution)/shard_map/ppermute | solution.py:46
  31.4 11.8 %collective-permute-start.2 = (bf16[24,2048]{1,0:T(8,128)(2,1)S(1)}, bf16[24,2048]{1,0:T(8,128)(2,1)S(1)}, u32[]{:S(2)}, u32[]{:S(2)}) collective-permute-start(bf16[24,2048]{1,0:T(8,128)(2,1)S(1)} %maximum_maximum_fusion), channel_id=1, source_target_pairs={{0,2},{2,0},{4,6},{6,4},{1,3},{3,1},{5,7},{7,5},{8,10},{10,8},{12,... | collective-permute-start | bytes 294920 | tf_op jit(solution)/shard_map/ppermute | solution.py:51
  36.2 9.9 %collective-permute-start.3 = (bf16[24,2048]{1,0:T(8,128)(2,1)S(1)}, bf16[24,2048]{1,0:T(8,128)(2,1)S(1)}, u32[]{:S(2)}, u32[]{:S(2)}) collective-permute-start(bf16[24,2048]{1,0:T(8,128)(2,1)S(1)} %maximum_maximum_fusion), channel_id=1, source_target_pairs={{0,4},{2,6},{4,0},{6,2},{1,5},{3,7},{5,1},{7,3},{8,12},{10,14},{12... | collective-permute-start | bytes 294920 | tf_op jit(solution)/shard_map/ppermute | solution.py:51
  38.1 8.1 %collective-permute-start.4 = (bf16[24,2048]{1,0:T(8,128)(2,1)S(1)}, bf16[24,2048]{1,0:T(8,128)(2,1)S(1)}, u32[]{:S(2)}, u32[]{:S(2)}) collective-permute-start(bf16[24,2048]{1,0:T(8,128)(2,1)S(1)} %maximum_maximum_fusion), channel_id=1, source_target_pairs={{0,6},{2,4},{4,2},{6,0},{1,7},{3,5},{5,3},{7,1},{8,14},{10,12},{12... | collective-permute-start | bytes 294920 | tf_op jit(solution)/shard_map/ppermute | solution.py:51
  39.4 7.4 %collective-permute-start.24 = (bf16[64,2048]{1,0:T(8,128)(2,1)S(1)}, bf16[64,2048]{1,0:T(8,128)(2,1)S(1)}, u32[]{:S(2)}, u32[]{:S(2)}) collective-permute-start(bf16[64,2048]{1,0:T(8,128)(2,1)S(1)} %collective-permute-done.23.refs_0_), channel_id=1, source_target_pairs={{0,1},{1,0},{2,3},{3,2},{4,5},{5,4},{6,7},{7,6},{8,9},{9,8},{10,11... | collective-permute-start | bytes 786440 | tf_op jit(solution)/shard_map/ppermute | solution.py:46
  42.7 7.2 %collective-permute-start.21 = (bf16[64,2048]{1,0:T(8,128)(2,1)S(1)}, bf16[64,2048]{1,0:T(8,128)(2,1)S(1)}, u32[]{:S(2)}, u32[]{:S(2)}) collective-permute-start(bf16[64,2048]{1,0:T(8,128)(2,1)S(1)} %get-tuple-element.34), channel_id=1, source_target_pairs={{0,1},{1,0},{2,3},{3,2},{4,5},{5,4},{6,7},{7,6},{8,9},{9,8},{10,11... | collective-permute-start | bytes 786440 | tf_op jit(solution)/shard_map/ppermute | solution.py:46
  46.2 7.7 %collective-permute-start.5 = (bf16[96,2048]{1,0:T(8,128)(2,1)S(1)}, bf16[96,2048]{1,0:T(8,128)(2,1)S(1)}, u32[]{:S(2)}, u32[]{:S(2)}) collective-permute-start(bf16[96,2048]{1,0:T(8,128)(2,1)S(1)} %pad_maximum_fusion.near_ref), channel_id=1, source_target_pairs={{0,1},{1,0},{2,3},{3,2},{4,5},{5,4},{6,7},{7,6},{8,9},{9,8},{10,11... | collective-permute-start | bytes 1179656 | tf_op jit(solution)/shard_map/ppermute | solution.py:46
  46.8 9.8 %collective-permute-start.18 = (bf16[64,2048]{1,0:T(8,128)(2,1)S(1)}, bf16[64,2048]{1,0:T(8,128)(2,1)S(1)}, u32[]{:S(2)}, u32[]{:S(2)}) collective-permute-start(bf16[64,2048]{1,0:T(8,128)(2,1)S(1)} %get-tuple-element.30), channel_id=1, source_target_pairs={{0,1},{1,0},{2,3},{3,2},{4,5},{5,4},{6,7},{7,6},{8,9},{9,8},{10,11... | collective-permute-start | bytes 786440 | tf_op jit(solution)/shard_map/ppermute | solution.py:46
  49.9 10.4 %collective-permute-start.22 = (bf16[64,2048]{1,0:T(8,128)(2,1)S(1)}, bf16[64,2048]{1,0:T(8,128)(2,1)S(1)}, u32[]{:S(2)}, u32[]{:S(2)}) collective-permute-start(bf16[64,2048]{1,0:T(8,128)(2,1)S(1)} %add_convert_fusion.1), channel_id=1, source_target_pairs={{0,8},{1,17},{8,0},{9,25},{16,24},{17,1},{24,16},{25,9},{2,10},{3,... | collective-permute-start | bytes 786440 | tf_op jit(solution)/shard_map/ppermute | solution.py:57
  50.5 9.9 %collective-permute-start.20 = (bf16[64,2048]{1,0:T(8,128)(2,1)S(1)}, bf16[64,2048]{1,0:T(8,128)(2,1)S(1)}, u32[]{:S(2)}, u32[]{:S(2)}) collective-permute-start(bf16[64,2048]{1,0:T(8,128)(2,1)S(1)} %add_convert_fusion.2), channel_id=1, source_target_pairs={{0,16},{1,9},{8,24},{9,1},{16,0},{17,25},{24,8},{25,17},{2,18},{3,... | collective-permute-start | bytes 786440 | tf_op jit(solution)/shard_map/ppermute | solution.py:57
  52.1 13.1 %collective-permute-start.26 = (bf16[64,2048]{1,0:T(8,128)(2,1)S(1)}, bf16[64,2048]{1,0:T(8,128)(2,1)S(1)}, u32[]{:S(2)}, u32[]{:S(2)}) collective-permute-start(bf16[64,2048]{1,0:T(8,128)(2,1)S(1)} %add_convert_fusion), channel_id=1, source_target_pairs={{0,24},{1,25},{8,16},{9,17},{16,8},{17,9},{24,0},{25,1},{2,26},{3,... | collective-permute-start | bytes 786440 | tf_op jit(solution)/shard_map/ppermute | solution.py:57
  53.9 25.2 %collective-permute-start = (bf16[2,64,2048]{2,1,0:T(8,128)(2,1)S(1)}, bf16[2,64,2048]{2,1,0:T(8,128)(2,1)S(1)}, u32[]{:S(2)}, u32[]{:S(2)}) collective-permute-start(bf16[2,64,2048]{2,1,0:T(8,128)(2,1)S(1)} %get-tuple-element.22), channel_id=1, source_target_pairs={{1,2},{3,4},{5,6},{2,1},{4,3},{6,5},{9,10},{11,12},{13,14},{10,9},... | collective-permute-start | bytes 1572872 | tf_op jit(solution)/shard_map/ppermute | solution.py:363
  56.6 22.6 %collective-permute-start.1 = (bf16[2,64,2048]{2,1,0:T(8,128)(2,1)S(1)}, bf16[2,64,2048]{2,1,0:T(8,128)(2,1)S(1)}, u32[]{:S(2)}, u32[]{:S(2)}) collective-permute-start(bf16[2,64,2048]{2,1,0:T(8,128)(2,1)S(1)} %get-tuple-element.23), channel_id=1, source_target_pairs={{0,1},{1,0},{2,3},{3,2},{4,5},{5,4},{6,7},{7,6},{8,9},{9,8},{10,11... | collective-permute-start | bytes 1572872 | tf_op jit(solution)/shard_map/ppermute | solution.py:46
  68.1 10.2 %collective-permute-start.28 = (bf16[24,2048]{1,0:T(8,128)(2,1)S(1)}, bf16[24,2048]{1,0:T(8,128)(2,1)S(1)}, u32[]{:S(2)}, u32[]{:S(2)}) collective-permute-start(bf16[24,2048]{1,0:T(8,128)(2,1)S(1)} %get-tuple-element.39), channel_id=1, source_target_pairs={{0,4},{2,6},{4,0},{6,2},{1,5},{3,7},{5,1},{7,3},{8,12},{10,14},{12... | collective-permute-start | bytes 294920 | tf_op jit(solution)/shard_map/ppermute | solution.py:51
  69.2 9.1 %collective-permute-start.29 = (bf16[24,2048]{1,0:T(8,128)(2,1)S(1)}, bf16[24,2048]{1,0:T(8,128)(2,1)S(1)}, u32[]{:S(2)}, u32[]{:S(2)}) collective-permute-start(bf16[24,2048]{1,0:T(8,128)(2,1)S(1)} %get-tuple-element.40), channel_id=1, source_target_pairs={{0,6},{2,4},{4,2},{6,0},{1,7},{3,5},{5,3},{7,1},{8,14},{10,12},{12... | collective-permute-start | bytes 294920 | tf_op jit(solution)/shard_map/ppermute | solution.py:51
  (11 other events, 95.9 us)

commit v5 on v4

--- a/solution.py
+++ b/solution.py
@@ -177,21 +177,45 @@
     )
 
 
-def ffn_kernel(n, *refs):
-    mine, peer, (win_ref, wout_ref) = refs[:n], refs[n : 2 * n], refs[2 * n : 2 * n + 2]
-    send, keep = refs[2 * n + 2 : 3 * n + 2], refs[3 * n + 2 :]
+def enter_kernel(*refs):
+    *rows, win_ref, out_ref = refs
+    half = rows[0].shape[1]
+    at = pl.multiple_of(lax.axis_index("fsdp") * half, 128)
+    group = max(1, 256 // rows[0].shape[0])
+    for first in range(0, len(rows), group):
+        x = jnp.concatenate([r[...] for r in rows[first : first + group]], axis=0)
+        at_row = first * rows[0].shape[0]
+        out_ref[at_row : at_row + x.shape[0], :] = jnp.dot(
+            x, win_ref[pl.ds(at, half), :], preferred_element_type=F32
+        )
+
+
+def enter(rows, win):
+    count, half = rows[0].shape
+    return call(
+        enter_kernel,
+        [struct((len(rows) * count, win.shape[1]), F32)],
+        [*rows, win],
+        0,
+        2 * len(rows) * count * half * win.shape[1],
+    )[0]
+
+
+def leave_kernel(n, *refs):
+    part_ref, peer, (win_ref, wout_ref) = refs[0], refs[1 : n + 1], refs[n + 1 : n + 3]
+    send, keep = refs[n + 3 : 2 * n + 3], refs[2 * n + 3 :]
     core = lax.axis_index("fsdp")
-    rows, half = mine[0].shape
+    rows, half = peer[0].shape
     at_mine = pl.multiple_of(core * half, 128)
     at_peer = pl.multiple_of((1 - core) * half, 128)
     group = max(1, min(n, 256 // rows))
-    step = 256
+    step = half
     for first in range(0, n, group):
         roles = range(first, min(n, first + group))
-        x_mine = jnp.concatenate([mine[r][...] for r in roles], axis=0)
-        x_peer = jnp.concatenate([peer[r][...] for r in roles], axis=0)
-        total = jnp.dot(x_mine, win_ref[pl.ds(at_mine, half), :], preferred_element_type=F32)
-        total = total + jnp.dot(x_peer, win_ref[pl.ds(at_peer, half), :], preferred_element_type=F32)
+        x = jnp.concatenate([peer[r][...] for r in roles], axis=0)
+        total = part_ref[first * rows : first * rows + x.shape[0], :] + jnp.dot(
+            x, win_ref[pl.ds(at_peer, half), :], preferred_element_type=F32
+        )
         hidden = jnp.maximum(total, 0.0).astype(BF16)
 
         def columns(i, carry, hidden=hidden, roles=roles):
@@ -207,15 +231,15 @@
         lax.fori_loop(0, half // step, columns, 0)
 
 
-def ffn(mine, peer, win, wout):
-    n = len(mine)
-    rows, half = mine[0].shape
+def leave(part, peer, win, wout):
+    n = len(peer)
+    rows, half = peer[0].shape
     outs = call(
-        functools.partial(ffn_kernel, n),
+        functools.partial(leave_kernel, n),
         [struct((rows, half))] * (2 * n),
-        [*mine, *peer, win, wout],
+        [part, *peer, win, wout],
         0,
-        4 * n * rows * 2 * half * win.shape[1],
+        6 * n * rows * half * win.shape[1],
     )
     return outs[:n], outs[n:]
 
@@ -281,20 +305,20 @@
 def routed_ffn(tokens, gain, win, wout, score, counts, order, heavy_qkv):
     devices = lax.axis_size("seq") * lax.axis_size("fsdp")
     own = pick_rows(counts, tokens, order, gain)
-    heavy_qkv, _ = lax.optimization_barrier((heavy_qkv, own))
     win, wout = load(win, wout)
     blocks = gather_seq(own)
     peers = [swap_core(x) for x in blocks]
     x0, place = compact(blocks, peers, MEAN_LIVE * devices)
+    heavy_qkv, _ = lax.optimization_barrier((heavy_qkv, x0))
     x1 = swap_doc(x0, NEAR)
     x2 = swap_doc(x0, OTHER)
     x3 = swap_doc(x1, OTHER)
     p0, p2, p1, p3 = [swap_core(x) for x in (x0, x1, x2, x3)]
-    send, keep = ffn((x0, x1, x2), (p0, p1, p2), win, wout)
+    send, keep = leave(enter((x0, x1, x2), win), (p0, p1, p2), win, wout)
     back = [swap_core(x) for x in send]
     got1 = swap_doc(total(keep[1], back[2]), NEAR)
     got2 = swap_doc(total(keep[2], back[1]), OTHER)
-    send3, keep3 = ffn((x3,), (p3,), win, wout)
+    send3, keep3 = leave(enter((x3,), win), (p3,), win, wout)
     got3 = swap_doc(total(keep3[0], swap_core(send3[0])), DIAGONAL)
     summed = scatter_seq(spread(place, (keep[0], back[0], got1, got2, got3)))
     return finish(counts, summed, swap_core(summed), order, score), heavy_qkv
@@ -419,7 +443,8 @@
     q = stacked(qkv[:, 0])
     keys = jnp.where(slot_live[:, None], qkv[:, 1], jnp.bfloat16(MARK))
     kv = jnp.concatenate([stacked(keys), stacked(qkv[:, 2])], axis=1)
-    near = jnp.concatenate(gather_seq(kv), axis=0)
+    parts = gather_seq(kv)
+    near = jnp.concatenate(parts, axis=0)
     far = swap_core(near)
     out = call(
         heavy_kernel,

time: 83.9 us -> 78 us (0.930)
  waiting for transfers between devices: 28.3 us -> 23.9 us
  Pallas kernels: 19.4 us -> 17.5 us
    ppermute x9, waiting for transfers between devices: 17 us -> 9.58 us  [swap_seq(): return lax.ppermute(x, 'seq', [(i, i ^ mask) for i in range(n)])]
    ppermute x9, starting transfers between devices: 15.1 us -> 17.6 us  [swap_seq(): return lax.ppermute(x, 'seq', [(i, i ^ mask) for i in range(n)])]
    ppermute x15, starting transfers between devices: 7.2 us -> 5.15 us  [swap_core(): return lax.ppermute(x, 'fsdp', [(0, 1), (1, 0)])]
    pallas_call x7 -> x9, Pallas kernels: 12.1 us -> 10.2 us  [call(): pl.pallas_call(body, out_shape=outs, in_specs=[SMEM] * scalars + [VMEM] *...]
    ppermute x15, waiting for transfers between devices: 0.96 us -> 2.72 us  [swap_core(): return lax.ppermute(x, 'fsdp', [(0, 1), (1, 0)])]
    ppermute x6, waiting for transfers between devices: 10.3 us -> 11.6 us  [swap_doc(): return lax.ppermute(x, ('dp', 'fsdp'), pairs)]
    optimization_barrier x1, local copies, waits for them, and re-layouts: 1.04 us -> 0.11 us  [routed_ffn(): heavy_qkv, _ = lax.optimization_barrier((heavy_qkv, x0))]
  transfers between devices with their start and end apart: 31 -> 31, of which waited for: 8 -> 11; matrix products, arithmetic and copies ran while one was open for 3% -> 2% of each run, Pallas kernels for 18% -> 18%
where the time goes in v5:
time: 78 us; the launch traced here: 77.8 us
  starting transfers between devices  32.1 us (41%)
  waiting for transfers between devices  23.9 us (31%)
  Pallas kernels  17.5 us (22%)
  local copies, waits for them, and re-layouts  1.59 us (2%)
  between operations  1.56 us (2%)
  other arithmetic  1.12 us (1%)
    ppermute x9, starting transfers between devices, swap_seq(): return lax.ppermute(x, 'seq', [(i, i ^ mask) for i in range(n)])  17.6 us
    ppermute x6, waiting for transfers between devices, swap_doc(): return lax.ppermute(x, ('dp', 'fsdp'), pairs)  11.6 us
    pallas_call x9, Pallas kernels, call(): pl.pallas_call(body, out_shape=outs, in_specs=[SMEM] * scalars + [VMEM] *...  10.2 us
    ppermute x9, waiting for transfers between devices, swap_seq(): return lax.ppermute(x, 'seq', [(i, i ^ mask) for i in range(n)])  9.58 us
    ppermute x6, starting transfers between devices, swap_doc(): return lax.ppermute(x, ('dp', 'fsdp'), pairs)  8.48 us
    ppermute x15, starting transfers between devices, swap_core(): return lax.ppermute(x, 'fsdp', [(0, 1), (1, 0)])  5.15 us
    pallas_call x1, Pallas kernels, light_branch(): return run(planes, far, near)  3.71 us
    pallas_call x1, Pallas kernels, load(): pl.pallas_call(load_kernel, out_shape=[struct(a.shape, a.dtype) for a in...  3.49 us
  transfers between devices with their start and end apart: 31, of which 11 were waited for; matrix products, arithmetic and copies ran while one was open for 2% of the time, Pallas kernels for 18%

profile of v5, /device:TPU:0, one launch (start us, length us, event | category | flops | bytes accessed | tf_op | source)
XLA Modules:
  0.0 77.8 jit_solution(7595906173607205702)
XLA Ops:
  1.3 2.3 %shard_map.114.refs_0_ = bf16[24,2048]{1,0:T(8,128)(2,1)} custom-call(s32[1,1]{1,0:T(1,128)} %copy.15.count_ref, bf16[128,4096]{1,0:T(8,128)(2,1)} %bitcast.29, s32[1,128]{1,0:T(1,128)} %bitcast.27, f32[1,4096]{1,0:T(1,128)} %bitcast.34), custom_call_target="tpu_custom_call" | custom-call | flops 25165824 | bytes 1163780 | tf_op jit(solution)/shard_map/pallas_call | solution.py:30
  3.6 3.1 %collective-permute-start.2 = (bf16[24,2048]{1,0:T(8,128)(2,1)}, bf16[24,2048]{1,0:T(8,128)(2,1)S(1)}, u32[]{:S(2)}, u32[]{:S(2)}) collective-permute-start(bf16[24,2048]{1,0:T(8,128)(2,1)} %shard_map.114.refs_0_), channel_id=1, source_target_pairs={{0,2},{2,0},{4,6},{6,4},{1,3},{3,1},{5,7},{7,5},{8,10},{10,8},{12,... | collective-permute-start | bytes 294920 | tf_op jit(solution)/shard_map/ppermute | solution.py:51
  6.7 2.6 %collective-permute-start.3 = (bf16[24,2048]{1,0:T(8,128)(2,1)}, bf16[24,2048]{1,0:T(8,128)(2,1)S(1)}, u32[]{:S(2)}, u32[]{:S(2)}) collective-permute-start(bf16[24,2048]{1,0:T(8,128)(2,1)} %shard_map.114.refs_0_), channel_id=1, source_target_pairs={{0,4},{2,6},{4,0},{6,2},{1,5},{3,7},{5,1},{7,3},{8,12},{10,14},{12... | collective-permute-start | bytes 294920 | tf_op jit(solution)/shard_map/ppermute | solution.py:51
  9.3 1.4 %copy-done = bf16[1,128,3,2048]{3,1,2,0:T(8,128)(2,1)S(1)} copy-done((bf16[1,128,3,2048]{3,1,2,0:T(8,128)(2,1)S(1)}, bf16[1,128,3,2048]{3,1,2,0:T(8,128)(2,1)}, u32[]{:S(2)}) %copy-start) | copy-done | bytes 1572888
  11.6 3.5 %shard_map.117 = (bf16[4096,512]{1,0:T(8,128)(2,1)S(1)}, bf16[512,4096]{1,0:T(8,128)(2,1)S(1)}) custom-call(bf16[4096,512]{1,0:T(8,128)(2,1)} %refs_0_.1, bf16[512,4096]{1,0:T(8,128)(2,1)} %refs_1_.1), custom_call_target="tpu_custom_call" | custom-call | bytes 8388608 | tf_op jit(solution)/shard_map/pallas_call | solution.py:283
  15.1 2.3 %collective-permute-start.6 = (bf16[24,2048]{1,0:T(8,128)(2,1)S(1)}, bf16[24,2048]{1,0:T(8,128)(2,1)S(1)}, u32[]{:S(2)}, u32[]{:S(2)}) collective-permute-start(bf16[24,2048]{1,0:T(8,128)(2,1)S(1)} %collective-permute-done.2.refs_1_), channel_id=1, source_target_pairs={{0,1},{1,0},{2,3},{3,2},{4,5},{5,4},{6,7},{7,6},{8,9},{9,8},{10,11... | collective-permute-start | bytes 294920 | tf_op jit(solution)/shard_map/ppermute | solution.py:46
  19.7 1.6 %collective-permute-start.13 = (bf16[64,2048]{1,0:T(8,128)(2,1)S(1)}, bf16[64,2048]{1,0:T(8,128)(2,1)S(1)}, u32[]{:S(2)}, u32[]{:S(2)}) collective-permute-start(bf16[64,2048]{1,0:T(8,128)(2,1)S(1)} %get-tuple-element.24.refs_0_), channel_id=1, source_target_pairs={{0,16},{1,9},{8,24},{9,1},{16,0},{17,25},{24,8},{25,17},{2,18},{3,... | collective-permute-start | bytes 786440 | tf_op jit(solution)/shard_map/ppermute | solution.py:57
  21.3 1.5 %collective-permute-start.14 = (bf16[64,2048]{1,0:T(8,128)(2,1)S(1)}, bf16[64,2048]{1,0:T(8,128)(2,1)S(1)}, u32[]{:S(2)}, u32[]{:S(2)}) collective-permute-start(bf16[64,2048]{1,0:T(8,128)(2,1)S(1)} %get-tuple-element.24.refs_0_), channel_id=1, source_target_pairs={{0,8},{1,17},{8,0},{9,25},{16,24},{17,1},{24,16},{25,9},{2,10},{3,... | collective-permute-start | bytes 786440 | tf_op jit(solution)/shard_map/ppermute | solution.py:57
  23.0 5.3 %collective-permute-done.13.refs_1_ = bf16[64,2048]{1,0:T(8,128)(2,1)S(1)} collective-permute-done((bf16[64,2048]{1,0:T(8,128)(2,1)S(1)}, bf16[64,2048]{1,0:T(8,128)(2,1)S(1)}, u32[]{:S(2)}, u32[]{:S(2)}) %collective-permute-start.13) | collective-permute-done | bytes 262176 | tf_op jit(solution)/shard_map/ppermute | solution.py:57
  28.3 1.7 %collective-permute-start.23 = (bf16[64,2048]{1,0:T(8,128)(2,1)S(1)}, bf16[64,2048]{1,0:T(8,128)(2,1)S(1)}, u32[]{:S(2)}, u32[]{:S(2)}) collective-permute-start(bf16[64,2048]{1,0:T(8,128)(2,1)S(1)} %collective-permute-done.13.refs_1_), channel_id=1, source_target_pairs={{0,8},{1,17},{8,0},{9,25},{16,24},{17,1},{24,16},{25,9},{2,10},{3,... | collective-permute-start | bytes 786440 | tf_op jit(solution)/shard_map/ppermute | solution.py:57
  31.2 3.6 %collective-permute-start.10 = (bf16[24,2048]{1,0:T(8,128)(2,1)S(1)}, bf16[24,2048]{1,0:T(8,128)(2,1)S(1)}, u32[]{:S(2)}, u32[]{:S(2)}) collective-permute-start(bf16[24,2048]{1,0:T(8,128)(2,1)S(1)} %maximum_maximum_fusion), channel_id=1, source_target_pairs={{0,4},{2,6},{4,0},{6,2},{1,5},{3,7},{5,1},{7,3},{8,12},{10,14},{12... | collective-permute-start | bytes 294920 | tf_op jit(solution)/shard_map/ppermute | solution.py:51
  34.8 3.3 %collective-permute-start.11 = (bf16[24,2048]{1,0:T(8,128)(2,1)S(1)}, bf16[24,2048]{1,0:T(8,128)(2,1)S(1)}, u32[]{:S(2)}, u32[]{:S(2)}) collective-permute-start(bf16[24,2048]{1,0:T(8,128)(2,1)S(1)} %maximum_maximum_fusion), channel_id=1, source_target_pairs={{0,6},{2,4},{4,2},{6,0},{1,7},{3,5},{5,3},{7,1},{8,14},{10,12},{12... | collective-permute-start | bytes 294920 | tf_op jit(solution)/shard_map/ppermute | solution.py:51
  38.8 1.5 %shard_map.119 = (bf16[64,2048]{1,0:T(8,128)(2,1)S(1)}, bf16[64,2048]{1,0:T(8,128)(2,1)S(1)}, bf16[64,2048]{1,0:T(8,128)(2,1)S(1)}, bf16[64,2048]{1,0:T(8,128)(2...) custom-call(f32[192,512]{1,0:T(8,128)S(1)} %shard_map.118.refs_0_, ...), custom_call_target="tpu_custom_call" | custom-call | flops 1207959552 | bytes 11141120 | tf_op jit(solution)/shard_map/pallas_call | solution.py:30
  40.3 2.0 %collective-permute-done.10 = bf16[24,2048]{1,0:T(8,128)(2,1)S(1)} collective-permute-done((bf16[24,2048]{1,0:T(8,128)(2,1)S(1)}, bf16[24,2048]{1,0:T(8,128)(2,1)S(1)}, u32[]{:S(2)}, u32[]{:S(2)}) %collective-permute-start.10) | collective-permute-done | bytes 98336 | tf_op jit(solution)/shard_map/ppermute | solution.py:51
  44.6 1.3 %shard_map.121 = (bf16[64,2048]{1,0:T(8,128)(2,1)S(1)}, bf16[64,2048]{1,0:T(8,128)(2,1)S(1)}) custom-call(f32[64,512]{1,0:T(8,128)S(1)} %shard_map.120.refs_0_, bf16[64,2048]{1,0:T(8,128)(2,1)S(1)} %collective-permute-done.24.refs_1_, bf16[4096,512]{1,0:T(8,128)(2,1)S(1)} %get-tuple-element.27.refs_3_.refs_4_.refs_1_.refs_2_, ...), custom_call_target="tpu_custom_call" | custom-call | flops 402653184 | bytes 9306112 | tf_op jit(solution)/shard_map/pallas_call | solution.py:30
  46.7 1.2 %collective-permute-done.25 = bf16[64,2048]{1,0:T(8,128)(2,1)S(1)} collective-permute-done((bf16[64,2048]{1,0:T(8,128)(2,1)S(1)}, bf16[64,2048]{1,0:T(8,128)(2,1)S(1)}, u32[]{:S(2)}, u32[]{:S(2)}) %collective-permute-start.25) | collective-permute-done | bytes 262176 | tf_op jit(solution)/shard_map/ppermute | solution.py:46
  48.9 1.6 %collective-permute-start.20 = (bf16[64,2048]{1,0:T(8,128)(2,1)S(1)}, bf16[64,2048]{1,0:T(8,128)(2,1)S(1)}, u32[]{:S(2)}, u32[]{:S(2)}) collective-permute-start(bf16[64,2048]{1,0:T(8,128)(2,1)S(1)} %add_convert_fusion.2), channel_id=1, source_target_pairs={{0,16},{1,9},{8,24},{9,1},{16,0},{17,25},{24,8},{25,17},{2,18},{3,... | collective-permute-start | bytes 786440 | tf_op jit(solution)/shard_map/ppermute | solution.py:57
  50.5 1.2 %collective-permute-start.26 = (bf16[64,2048]{1,0:T(8,128)(2,1)S(1)}, bf16[64,2048]{1,0:T(8,128)(2,1)S(1)}, u32[]{:S(2)}, u32[]{:S(2)}) collective-permute-start(bf16[64,2048]{1,0:T(8,128)(2,1)S(1)} %add_convert_fusion), channel_id=1, source_target_pairs={{0,24},{1,25},{8,16},{9,17},{16,8},{17,9},{24,0},{25,1},{2,26},{3,... | collective-permute-start | bytes 786440 | tf_op jit(solution)/shard_map/ppermute | solution.py:57
  51.7 3.7 %shard_map.113 = bf16[128,2048]{1,0:T(8,128)(2,1)} custom-call(bf16[3,128,2048]{2,1,0:T(8,128)(2,1)S(1)} %bitcast.26, bf16[2,64,2048]{2,1,0:T(8,128)(2,1)S(1)} %collective-permute-done.far_ref, bf16[2,64,2048]{2,1,0:T(8,128)(2,1)S(1)} %collective-permute-done.1.near_ref), custom_call_target="tpu_custom_call" | custom-call | flops 268435456 | bytes 3145728 | tf_op jit(solution)/shard_map/pallas_call | solution.py:407
  55.4 1.9 %shard_map.116 = bf16[24,1024]{1,0:T(8,128)(2,1)S(1)} custom-call(bf16[24,1024]{1,0:T(8,128)(2,1)S(1)} %pad_maximum_fusion.1.q_ref, bf16[96,2048]{1,0:T(8,128)(2,1)S(1)} %pad_maximum_fusion.near_ref, bf16[96,2048]{1,0:T(8,128)(2,1)S(1)} %collective-permute-done.12.far_ref), custom_call_target="tpu_custom_call" | custom-call | flops 18874368 | bytes 884736 | tf_op jit(solution)/shard_map/pallas_call | solution.py:30
  57.4 6.3 %collective-permute-done.26.refs_4_ = bf16[64,2048]{1,0:T(8,128)(2,1)S(1)} collective-permute-done((bf16[64,2048]{1,0:T(8,128)(2,1)S(1)}, bf16[64,2048]{1,0:T(8,128)(2,1)S(1)}, u32[]{:S(2)}, u32[]{:S(2)}) %collective-permute-start.26) | collective-permute-done | bytes 262176 | tf_op jit(solution)/shard_map/ppermute | solution.py:57
  64.1 1.2 %collective-permute-start.27 = (bf16[24,2048]{1,0:T(8,128)(2,1)S(1)}, bf16[24,2048]{1,0:T(8,128)(2,1)S(1)}, u32[]{:S(2)}, u32[]{:S(2)}) collective-permute-start(bf16[24,2048]{1,0:T(8,128)(2,1)S(1)} %get-tuple-element.38), channel_id=1, source_target_pairs={{0,2},{2,0},{4,6},{6,4},{1,3},{3,1},{5,7},{7,5},{8,10},{10,8},{12,... | collective-permute-start | bytes 294920 | tf_op jit(solution)/shard_map/ppermute | solution.py:51
  66.3 2.3 %collective-permute-start.29 = (bf16[24,2048]{1,0:T(8,128)(2,1)S(1)}, bf16[24,2048]{1,0:T(8,128)(2,1)S(1)}, u32[]{:S(2)}, u32[]{:S(2)}) collective-permute-start(bf16[24,2048]{1,0:T(8,128)(2,1)S(1)} %get-tuple-element.40), channel_id=1, source_target_pairs={{0,6},{2,4},{4,2},{6,0},{1,7},{3,5},{5,3},{7,1},{8,14},{10,12},{12... | collective-permute-start | bytes 294920 | tf_op jit(solution)/shard_map/ppermute | solution.py:51
  69.6 5.8 %collective-permute-done.28 = bf16[24,2048]{1,0:T(8,128)(2,1)S(1)} collective-permute-done((bf16[24,2048]{1,0:T(8,128)(2,1)S(1)}, bf16[24,2048]{1,0:T(8,128)(2,1)S(1)}, u32[]{:S(2)}, u32[]{:S(2)}) %collective-permute-start.28) | collective-permute-done | bytes 98336 | tf_op jit(solution)/shard_map/ppermute | solution.py:51
  (77 shorter events, 14.1 us)
Async XLA Ops:
  3.6 11.5 %collective-permute-start.2 = (bf16[24,2048]{1,0:T(8,128)(2,1)}, bf16[24,2048]{1,0:T(8,128)(2,1)S(1)}, u32[]{:S(2)}, u32[]{:S(2)}) collective-permute-start(bf16[24,2048]{1,0:T(8,128)(2,1)} %shard_map.114.refs_0_), channel_id=1, source_target_pairs={{0,2},{2,0},{4,6},{6,4},{1,3},{3,1},{5,7},{7,5},{8,10},{10,8},{12,... | collective-permute-start | bytes 294920 | tf_op jit(solution)/shard_map/ppermute | solution.py:51
  6.7 10.8 %collective-permute-start.3 = (bf16[24,2048]{1,0:T(8,128)(2,1)}, bf16[24,2048]{1,0:T(8,128)(2,1)S(1)}, u32[]{:S(2)}, u32[]{:S(2)}) collective-permute-start(bf16[24,2048]{1,0:T(8,128)(2,1)} %shard_map.114.refs_0_), channel_id=1, source_target_pairs={{0,4},{2,6},{4,0},{6,2},{1,5},{3,7},{5,1},{7,3},{8,12},{10,14},{12... | collective-permute-start | bytes 294920 | tf_op jit(solution)/shard_map/ppermute | solution.py:51
  9.3 8.3 %collective-permute-start.4 = (bf16[24,2048]{1,0:T(8,128)(2,1)}, bf16[24,2048]{1,0:T(8,128)(2,1)S(1)}, u32[]{:S(2)}, u32[]{:S(2)}) collective-permute-start(bf16[24,2048]{1,0:T(8,128)(2,1)} %shard_map.114.refs_0_), channel_id=1, source_target_pairs={{0,6},{2,4},{4,2},{6,0},{1,7},{3,5},{5,3},{7,1},{8,14},{10,12},{12... | collective-permute-start | bytes 294920 | tf_op jit(solution)/shard_map/ppermute | solution.py:51
  9.3 8.7 %collective-permute-start.5 = (bf16[24,2048]{1,0:T(8,128)(2,1)}, bf16[24,2048]{1,0:T(8,128)(2,1)S(1)}, u32[]{:S(2)}, u32[]{:S(2)}) collective-permute-start(bf16[24,2048]{1,0:T(8,128)(2,1)} %shard_map.114.refs_0_), channel_id=1, source_target_pairs={{0,1},{1,0},{2,3},{3,2},{4,5},{5,4},{6,7},{7,6},{8,9},{9,8},{10,11... | collective-permute-start | bytes 294920 | tf_op jit(solution)/shard_map/ppermute | solution.py:46
  10.8 38.1 %collective-permute-start = (bf16[2,64,2048]{2,1,0:T(8,128)(2,1)S(1)}, bf16[2,64,2048]{2,1,0:T(8,128)(2,1)S(1)}, u32[]{:S(2)}, u32[]{:S(2)}) collective-permute-start(bf16[2,64,2048]{2,1,0:T(8,128)(2,1)S(1)} %get-tuple-element.22), channel_id=1, source_target_pairs={{1,2},{3,4},{5,6},{2,1},{4,3},{6,5},{9,10},{11,12},{13,14},{10,9},... | collective-permute-start | bytes 1572872 | tf_op jit(solution)/shard_map/ppermute | solution.py:387
  19.7 8.6 %collective-permute-start.13 = (bf16[64,2048]{1,0:T(8,128)(2,1)S(1)}, bf16[64,2048]{1,0:T(8,128)(2,1)S(1)}, u32[]{:S(2)}, u32[]{:S(2)}) collective-permute-start(bf16[64,2048]{1,0:T(8,128)(2,1)S(1)} %get-tuple-element.24.refs_0_), channel_id=1, source_target_pairs={{0,16},{1,9},{8,24},{9,1},{16,0},{17,25},{24,8},{25,17},{2,18},{3,... | collective-permute-start | bytes 786440 | tf_op jit(solution)/shard_map/ppermute | solution.py:57
  21.3 8.8 %collective-permute-start.14 = (bf16[64,2048]{1,0:T(8,128)(2,1)S(1)}, bf16[64,2048]{1,0:T(8,128)(2,1)S(1)}, u32[]{:S(2)}, u32[]{:S(2)}) collective-permute-start(bf16[64,2048]{1,0:T(8,128)(2,1)S(1)} %get-tuple-element.24.refs_0_), channel_id=1, source_target_pairs={{0,8},{1,17},{8,0},{9,25},{16,24},{17,1},{24,16},{25,9},{2,10},{3,... | collective-permute-start | bytes 786440 | tf_op jit(solution)/shard_map/ppermute | solution.py:57
  22.8 8.4 %collective-permute-start.15 = (bf16[64,2048]{1,0:T(8,128)(2,1)S(1)}, bf16[64,2048]{1,0:T(8,128)(2,1)S(1)}, u32[]{:S(2)}, u32[]{:S(2)}) collective-permute-start(bf16[64,2048]{1,0:T(8,128)(2,1)S(1)} %get-tuple-element.24.refs_0_), channel_id=1, source_target_pairs={{0,1},{1,0},{2,3},{3,2},{4,5},{5,4},{6,7},{7,6},{8,9},{9,8},{10,11... | collective-permute-start | bytes 786440 | tf_op jit(solution)/shard_map/ppermute | solution.py:46
  28.3 6.4 %collective-permute-start.23 = (bf16[64,2048]{1,0:T(8,128)(2,1)S(1)}, bf16[64,2048]{1,0:T(8,128)(2,1)S(1)}, u32[]{:S(2)}, u32[]{:S(2)}) collective-permute-start(bf16[64,2048]{1,0:T(8,128)(2,1)S(1)} %collective-permute-done.13.refs_1_), channel_id=1, source_target_pairs={{0,8},{1,17},{8,0},{9,25},{16,24},{17,1},{24,16},{25,9},{2,10},{3,... | collective-permute-start | bytes 786440 | tf_op jit(solution)/shard_map/ppermute | solution.py:57
  30.1 8.0 %collective-permute-start.17 = (bf16[64,2048]{1,0:T(8,128)(2,1)S(1)}, bf16[64,2048]{1,0:T(8,128)(2,1)S(1)}, u32[]{:S(2)}, u32[]{:S(2)}) collective-permute-start(bf16[64,2048]{1,0:T(8,128)(2,1)S(1)} %collective-permute-done.13.refs_1_), channel_id=1, source_target_pairs={{0,1},{1,0},{2,3},{3,2},{4,5},{5,4},{6,7},{7,6},{8,9},{9,8},{10,11... | collective-permute-start | bytes 786440 | tf_op jit(solution)/shard_map/ppermute | solution.py:46
  30.1 8.7 %collective-permute-start.16 = (bf16[64,2048]{1,0:T(8,128)(2,1)S(1)}, bf16[64,2048]{1,0:T(8,128)(2,1)S(1)}, u32[]{:S(2)}, u32[]{:S(2)}) collective-permute-start(bf16[64,2048]{1,0:T(8,128)(2,1)S(1)} %collective-permute-done.14.refs_2_), channel_id=1, source_target_pairs={{0,1},{1,0},{2,3},{3,2},{4,5},{5,4},{6,7},{7,6},{8,9},{9,8},{10,11... | collective-permute-start | bytes 786440 | tf_op jit(solution)/shard_map/ppermute | solution.py:46
  31.2 11.0 %collective-permute-start.10 = (bf16[24,2048]{1,0:T(8,128)(2,1)S(1)}, bf16[24,2048]{1,0:T(8,128)(2,1)S(1)}, u32[]{:S(2)}, u32[]{:S(2)}) collective-permute-start(bf16[24,2048]{1,0:T(8,128)(2,1)S(1)} %maximum_maximum_fusion), channel_id=1, source_target_pairs={{0,4},{2,6},{4,0},{6,2},{1,5},{3,7},{5,1},{7,3},{8,12},{10,14},{12... | collective-permute-start | bytes 294920 | tf_op jit(solution)/shard_map/ppermute | solution.py:51
  34.8 7.5 %collective-permute-start.11 = (bf16[24,2048]{1,0:T(8,128)(2,1)S(1)}, bf16[24,2048]{1,0:T(8,128)(2,1)S(1)}, u32[]{:S(2)}, u32[]{:S(2)}) collective-permute-start(bf16[24,2048]{1,0:T(8,128)(2,1)S(1)} %maximum_maximum_fusion), channel_id=1, source_target_pairs={{0,6},{2,4},{4,2},{6,0},{1,7},{3,5},{5,3},{7,1},{8,14},{10,12},{12... | collective-permute-start | bytes 294920 | tf_op jit(solution)/shard_map/ppermute | solution.py:51
  38.1 5.4 %collective-permute-start.9 = (bf16[24,2048]{1,0:T(8,128)(2,1)S(1)}, bf16[24,2048]{1,0:T(8,128)(2,1)S(1)}, u32[]{:S(2)}, u32[]{:S(2)}) collective-permute-start(bf16[24,2048]{1,0:T(8,128)(2,1)S(1)} %maximum_maximum_fusion), channel_id=1, source_target_pairs={{0,2},{2,0},{4,6},{6,4},{1,3},{3,1},{5,7},{7,5},{8,10},{10,8},{12,... | collective-permute-start | bytes 294920 | tf_op jit(solution)/shard_map/ppermute | solution.py:51
  38.8 5.3 %collective-permute-start.24 = (bf16[64,2048]{1,0:T(8,128)(2,1)S(1)}, bf16[64,2048]{1,0:T(8,128)(2,1)S(1)}, u32[]{:S(2)}, u32[]{:S(2)}) collective-permute-start(bf16[64,2048]{1,0:T(8,128)(2,1)S(1)} %collective-permute-done.23.refs_0_), channel_id=1, source_target_pairs={{0,1},{1,0},{2,3},{3,2},{4,5},{5,4},{6,7},{7,6},{8,9},{9,8},{10,11... | collective-permute-start | bytes 786440 | tf_op jit(solution)/shard_map/ppermute | solution.py:46
  42.3 8.2 %collective-permute-start.1 = (bf16[2,64,2048]{2,1,0:T(8,128)(2,1)S(1)}, bf16[2,64,2048]{2,1,0:T(8,128)(2,1)S(1)}, u32[]{:S(2)}, u32[]{:S(2)}) collective-permute-start(bf16[2,64,2048]{2,1,0:T(8,128)(2,1)S(1)} %get-tuple-element.23), channel_id=1, source_target_pairs={{0,1},{1,0},{2,3},{3,2},{4,5},{5,4},{6,7},{7,6},{8,9},{9,8},{10,11... | collective-permute-start | bytes 1572872 | tf_op jit(solution)/shard_map/ppermute | solution.py:46
  43.5 11.9 %collective-permute-start.12 = (bf16[96,2048]{1,0:T(8,128)(2,1)S(1)}, bf16[96,2048]{1,0:T(8,128)(2,1)S(1)}, u32[]{:S(2)}, u32[]{:S(2)}) collective-permute-start(bf16[96,2048]{1,0:T(8,128)(2,1)S(1)} %pad_maximum_fusion.near_ref), channel_id=1, source_target_pairs={{0,1},{1,0},{2,3},{3,2},{4,5},{5,4},{6,7},{7,6},{8,9},{9,8},{10,11... | collective-permute-start | bytes 1179656 | tf_op jit(solution)/shard_map/ppermute | solution.py:46
  45.9 11.4 %collective-permute-start.18 = (bf16[64,2048]{1,0:T(8,128)(2,1)S(1)}, bf16[64,2048]{1,0:T(8,128)(2,1)S(1)}, u32[]{:S(2)}, u32[]{:S(2)}) collective-permute-start(bf16[64,2048]{1,0:T(8,128)(2,1)S(1)} %get-tuple-element.30), channel_id=1, source_target_pairs={{0,1},{1,0},{2,3},{3,2},{4,5},{5,4},{6,7},{7,6},{8,9},{9,8},{10,11... | collective-permute-start | bytes 786440 | tf_op jit(solution)/shard_map/ppermute | solution.py:46
  47.9 9.4 %collective-permute-start.22 = (bf16[64,2048]{1,0:T(8,128)(2,1)S(1)}, bf16[64,2048]{1,0:T(8,128)(2,1)S(1)}, u32[]{:S(2)}, u32[]{:S(2)}) collective-permute-start(bf16[64,2048]{1,0:T(8,128)(2,1)S(1)} %add_convert_fusion.1), channel_id=1, source_target_pairs={{0,8},{1,17},{8,0},{9,25},{16,24},{17,1},{24,16},{25,9},{2,10},{3,... | collective-permute-start | bytes 786440 | tf_op jit(solution)/shard_map/ppermute | solution.py:57
  48.9 8.5 %collective-permute-start.20 = (bf16[64,2048]{1,0:T(8,128)(2,1)S(1)}, bf16[64,2048]{1,0:T(8,128)(2,1)S(1)}, u32[]{:S(2)}, u32[]{:S(2)}) collective-permute-start(bf16[64,2048]{1,0:T(8,128)(2,1)S(1)} %add_convert_fusion.2), channel_id=1, source_target_pairs={{0,16},{1,9},{8,24},{9,1},{16,0},{17,25},{24,8},{25,17},{2,18},{3,... | collective-permute-start | bytes 786440 | tf_op jit(solution)/shard_map/ppermute | solution.py:57
  50.5 13.2 %collective-permute-start.26 = (bf16[64,2048]{1,0:T(8,128)(2,1)S(1)}, bf16[64,2048]{1,0:T(8,128)(2,1)S(1)}, u32[]{:S(2)}, u32[]{:S(2)}) collective-permute-start(bf16[64,2048]{1,0:T(8,128)(2,1)S(1)} %add_convert_fusion), channel_id=1, source_target_pairs={{0,24},{1,25},{8,16},{9,17},{16,8},{17,9},{24,0},{25,1},{2,26},{3,... | collective-permute-start | bytes 786440 | tf_op jit(solution)/shard_map/ppermute | solution.py:57
  64.1 5.5 %collective-permute-start.27 = (bf16[24,2048]{1,0:T(8,128)(2,1)S(1)}, bf16[24,2048]{1,0:T(8,128)(2,1)S(1)}, u32[]{:S(2)}, u32[]{:S(2)}) collective-permute-start(bf16[24,2048]{1,0:T(8,128)(2,1)S(1)} %get-tuple-element.38), channel_id=1, source_target_pairs={{0,2},{2,0},{4,6},{6,4},{1,3},{3,1},{5,7},{7,5},{8,10},{10,8},{12,... | collective-permute-start | bytes 294920 | tf_op jit(solution)/shard_map/ppermute | solution.py:51
  65.3 10.2 %collective-permute-start.28 = (bf16[24,2048]{1,0:T(8,128)(2,1)S(1)}, bf16[24,2048]{1,0:T(8,128)(2,1)S(1)}, u32[]{:S(2)}, u32[]{:S(2)}) collective-permute-start(bf16[24,2048]{1,0:T(8,128)(2,1)S(1)} %get-tuple-element.39), channel_id=1, source_target_pairs={{0,4},{2,6},{4,0},{6,2},{1,5},{3,7},{5,1},{7,3},{8,12},{10,14},{12... | collective-permute-start | bytes 294920 | tf_op jit(solution)/shard_map/ppermute | solution.py:51
  66.3 9.2 %collective-permute-start.29 = (bf16[24,2048]{1,0:T(8,128)(2,1)S(1)}, bf16[24,2048]{1,0:T(8,128)(2,1)S(1)}, u32[]{:S(2)}, u32[]{:S(2)}) collective-permute-start(bf16[24,2048]{1,0:T(8,128)(2,1)S(1)} %get-tuple-element.40), channel_id=1, source_target_pairs={{0,6},{2,4},{4,2},{6,0},{1,7},{3,5},{5,3},{7,1},{8,14},{10,12},{12... | collective-permute-start | bytes 294920 | tf_op jit(solution)/shard_map/ppermute | solution.py:51
  (13 other events, 105.7 us)

commit v6 on v5

--- a/solution.py
+++ b/solution.py
@@ -100,7 +100,7 @@
     first = iota((rows, 1), 0) < CAP
     x = jnp.where(first, x[:, :half], x[:, half:])
     gain = jnp.where(first, gain_ref[:, :half], gain_ref[:, half:])
-    dead = slot >= count_ref[0, 0]
+    dead = slot >= count_ref[...]
     out_ref[...] = jnp.where(dead, MARK, x * scale * gain).astype(BF16)
 
 
@@ -110,7 +110,7 @@
         pick_kernel,
         [struct((rows, width // 2))],
         [counts, tokens, order, gain],
-        1,
+        0,
         2 * rows * TILE * width,
         room=54 << 20,
     )[0]
@@ -201,47 +201,60 @@
     )[0]
 
 
-def leave_kernel(n, *refs):
+def hide_kernel(n, *refs):
     part_ref, peer, (win_ref, wout_ref) = refs[0], refs[1 : n + 1], refs[n + 1 : n + 3]
-    send, keep = refs[n + 3 : 2 * n + 3], refs[2 * n + 3 :]
-    core = lax.axis_index("fsdp")
+    send, hidden_ref = refs[n + 3 : 2 * n + 3], refs[2 * n + 3]
     rows, half = peer[0].shape
-    at_mine = pl.multiple_of(core * half, 128)
-    at_peer = pl.multiple_of((1 - core) * half, 128)
+    at = pl.multiple_of((1 - lax.axis_index("fsdp")) * half, 128)
     group = max(1, min(n, 256 // rows))
-    step = half
     for first in range(0, n, group):
         roles = range(first, min(n, first + group))
         x = jnp.concatenate([peer[r][...] for r in roles], axis=0)
-        total = part_ref[first * rows : first * rows + x.shape[0], :] + jnp.dot(
-            x, win_ref[pl.ds(at_peer, half), :], preferred_element_type=F32
+        here = slice(first * rows, first * rows + x.shape[0])
+        total = part_ref[here, :] + jnp.dot(
+            x, win_ref[pl.ds(at, half), :], preferred_element_type=F32
         )
         hidden = jnp.maximum(total, 0.0).astype(BF16)
-
-        def columns(i, carry, hidden=hidden, roles=roles):
-            off = pl.multiple_of(i * step, step)
-            for start, targets in ((at_peer, send), (at_mine, keep)):
-                y = jnp.dot(
-                    hidden, wout_ref[:, pl.ds(start + off, step)], preferred_element_type=F32
-                ).astype(BF16)
-                for j, r in enumerate(roles):
-                    targets[r][:, pl.ds(off, step)] = y[j * rows : (j + 1) * rows]
-            return carry
-
-        lax.fori_loop(0, half // step, columns, 0)
-
-
-def leave(part, peer, win, wout):
+        hidden_ref[here, :] = hidden
+        y = jnp.dot(hidden, wout_ref[:, pl.ds(at, half)], preferred_element_type=F32).astype(BF16)
+        for j, r in enumerate(roles):
+            send[r][...] = y[j * rows : (j + 1) * rows]
+
+
+def hide(part, peer, win, wout):
     n = len(peer)
     rows, half = peer[0].shape
     outs = call(
+        functools.partial(hide_kernel, n),
+        [struct((rows, half))] * n + [struct(part.shape)],
+        [part, *peer, win, wout],
+        0,
+        4 * n * rows * half * win.shape[1],
+    )
+    return outs[:n], outs[n]
+
+
+def leave_kernel(n, hidden_ref, wout_ref, *keep):
+    rows, half = keep[0].shape
+    at = pl.multiple_of(lax.axis_index("fsdp") * half, 128)
+    group = max(1, min(n, 256 // rows))
+    for first in range(0, n, group):
+        roles = range(first, min(n, first + group))
+        hidden = hidden_ref[first * rows : (first + len(roles)) * rows, :]
+        y = jnp.dot(hidden, wout_ref[:, pl.ds(at, half)], preferred_element_type=F32).astype(BF16)
+        for j, r in enumerate(roles):
+            keep[r][...] = y[j * rows : (j + 1) * rows]
+
+
+def leave(hidden, wout, n):
+    rows, half = hidden.shape[0] // n, wout.shape[1] // 2
+    return call(
         functools.partial(leave_kernel, n),
-        [struct((rows, half))] * (2 * n),
-        [part, *peer, win, wout],
-        0,
-        6 * n * rows * half * win.shape[1],
-    )
-    return outs[:n], outs[n:]
+        [struct((rows, half))] * n,
+        [hidden, wout],
+        0,
+        2 * n * rows * half * wout.shape[0],
+    )
 
 
 def finish_kernel(count_ref, mine_ref, peer_ref, order_ref, score_ref, out_ref):
@@ -252,7 +265,7 @@
     order = jnp.broadcast_to(order_ref[...], (CAP, TILE))
     row = jnp.sum(jnp.where(lanes == slot, order, 0), axis=1, keepdims=True)
     score = jnp.sum(jnp.where(lanes == row, score_ref[...].astype(F32), 0.0), axis=1, keepdims=True)
-    score = jnp.where(iota((CAP, 1), 0) < count_ref[0, 0], score, 0.0)
+    score = jnp.where(iota((CAP, 1), 0) < count_ref[...], score, 0.0)
     for ref, start in ((mine_ref, core * half), (peer_ref, (1 - core) * half)):
         y = jnp.dot(pick, ref[...], preferred_element_type=F32)
         out_ref[:, pl.ds(pl.multiple_of(start, 128), half)] = (score * y).astype(BF16)
@@ -264,7 +277,7 @@
         finish_kernel,
         [struct((CAP, 2 * half))],
         [counts, mine, peer, order, score],
-        1,
+        0,
         4 * CAP * rows * half,
     )[0]
 
@@ -309,19 +322,21 @@
     blocks = gather_seq(own)
     peers = [swap_core(x) for x in blocks]
     x0, place = compact(blocks, peers, MEAN_LIVE * devices)
-    heavy_qkv, _ = lax.optimization_barrier((heavy_qkv, x0))
+    heavy_qkv, counts_later, _ = lax.optimization_barrier((heavy_qkv, counts, x0))
     x1 = swap_doc(x0, NEAR)
     x2 = swap_doc(x0, OTHER)
     x3 = swap_doc(x1, OTHER)
     p0, p2, p1, p3 = [swap_core(x) for x in (x0, x1, x2, x3)]
-    send, keep = leave(enter((x0, x1, x2), win), (p0, p1, p2), win, wout)
+    send, hidden = hide(enter((x0, x1, x2), win), (p0, p1, p2), win, wout)
+    keep = leave(hidden, wout, 3)
     back = [swap_core(x) for x in send]
     got1 = swap_doc(total(keep[1], back[2]), NEAR)
     got2 = swap_doc(total(keep[2], back[1]), OTHER)
-    send3, keep3 = leave(enter((x3,), win), (p3,), win, wout)
+    send3, hidden = hide(enter((x3,), win), (p3,), win, wout)
+    keep3 = leave(hidden, wout, 1)
     got3 = swap_doc(total(keep3[0], swap_core(send3[0])), DIAGONAL)
     summed = scatter_seq(spread(place, (keep[0], back[0], got1, got2, got3)))
-    return finish(counts, summed, swap_core(summed), order, score), heavy_qkv
+    return finish(counts, summed, swap_core(summed), order, score), heavy_qkv, counts_later
 
 
 def light_kernel(qkv_ref, far_ref, near_ref, out_ref):
@@ -461,8 +476,7 @@
     tokens, ffn_gain, in_proj, out_proj, router_score, tile_counts, tile_order, light_qkv, heavy_qkv
 ):
     assert tile_order.shape[1] == 1 and lax.axis_size("fsdp") == 2 and lax.axis_size("dp") == 4
-    slot_live = jnp.arange(CAP) < tile_counts[0, 0]
-    heavy_ffn, heavy_qkv = routed_ffn(
+    heavy_ffn, heavy_qkv, counts_later = routed_ffn(
         tokens[0],
         ffn_gain[None],
         in_proj,
@@ -472,6 +486,7 @@
         tile_order[0],
         heavy_qkv,
     )
+    slot_live = jnp.arange(CAP) < counts_later[0, 0]
     light_out = light_branch(jnp.transpose(light_qkv[0], (1, 0, 2)))
     heavy_attn = heavy_branch(heavy_qkv[0], slot_live)
     return (light_out[None], heavy_attn[None], heavy_ffn[None])

time: 78 us -> 77.4 us (level)
  starting transfers between devices: 32.1 us -> 26.1 us
  waiting for transfers between devices: 23.9 us -> 28.9 us
    ppermute x9, waiting for transfers between devices: 9.58 us -> 14.7 us  [swap_seq(): return lax.ppermute(x, 'seq', [(i, i ^ mask) for i in range(n)])]
    ppermute x9, starting transfers between devices: 17.6 us -> 14.3 us  [swap_seq(): return lax.ppermute(x, 'seq', [(i, i ^ mask) for i in range(n)])]
    ppermute x15, starting transfers between devices: 5.15 us -> 2.75 us  [swap_core(): return lax.ppermute(x, 'fsdp', [(0, 1), (1, 0)])]
    pallas_call x9 -> x11, Pallas kernels: 10.2 us -> 10.6 us  [call(): pl.pallas_call(body, out_shape=outs, in_specs=[SMEM] * scalars + [VMEM] *...]
  transfers between devices with their start and end apart: 31 -> 31, of which waited for: 11 -> 12; matrix products, arithmetic and copies ran while one was open for 2% -> 2% of each run, Pallas kernels for 18% -> 17%
where the time goes in v6:
time: 77.4 us; the launch traced here: 77.2 us
  waiting for transfers between devices  28.9 us (37%)
  starting transfers between devices  26.1 us (34%)
  Pallas kernels  17.9 us (23%)
  local copies, waits for them, and re-layouts  1.59 us (2%)
  between operations  1.56 us (2%)
  other arithmetic  1.12 us (1%)
    ppermute x9, waiting for transfers between devices, swap_seq(): return lax.ppermute(x, 'seq', [(i, i ^ mask) for i in range(n)])  14.7 us
    ppermute x9, starting transfers between devices, swap_seq(): return lax.ppermute(x, 'seq', [(i, i ^ mask) for i in range(n)])  14.3 us
    ppermute x6, waiting for transfers between devices, swap_doc(): return lax.ppermute(x, ('dp', 'fsdp'), pairs)  11.4 us
    pallas_call x11, Pallas kernels, call(): pl.pallas_call(body, out_shape=outs, in_specs=[SMEM] * scalars + [VMEM] *...  10.6 us
    ppermute x6, starting transfers between devices, swap_doc(): return lax.ppermute(x, ('dp', 'fsdp'), pairs)  8.42 us
    pallas_call x1, Pallas kernels, light_branch(): return run(planes, far, near)  3.71 us
    pallas_call x1, Pallas kernels, load(): pl.pallas_call(load_kernel, out_shape=[struct(a.shape, a.dtype) for a in...  3.52 us
    ppermute x15, waiting for transfers between devices, swap_core(): return lax.ppermute(x, 'fsdp', [(0, 1), (1, 0)])  2.79 us
  transfers between devices with their start and end apart: 31, of which 12 were waited for; matrix products, arithmetic and copies ran while one was open for 2% of the time, Pallas kernels for 17%

profile of v6, /device:TPU:0, one launch (start us, length us, event | category | flops | bytes accessed | tf_op | source)
XLA Modules:
  0.0 77.2 jit_solution(10130368006346538626)
XLA Ops:
  1.3 2.4 %shard_map.114.refs_0_ = bf16[24,2048]{1,0:T(8,128)(2,1)} custom-call(s32[1,1]{1,0:T(1,128)} %copy.15.count_ref, bf16[128,4096]{1,0:T(8,128)(2,1)} %bitcast.29, s32[1,128]{1,0:T(1,128)} %bitcast.27, f32[1,4096]{1,0:T(1,128)} %bitcast.34), custom_call_target="tpu_custom_call" | custom-call | flops 25165824 | bytes 1163780 | tf_op jit(solution)/shard_map/pallas_call | solution.py:30
  3.6 3.1 %collective-permute-start.2 = (bf16[24,2048]{1,0:T(8,128)(2,1)}, bf16[24,2048]{1,0:T(8,128)(2,1)S(1)}, u32[]{:S(2)}, u32[]{:S(2)}) collective-permute-start(bf16[24,2048]{1,0:T(8,128)(2,1)} %shard_map.114.refs_0_), channel_id=1, source_target_pairs={{0,2},{2,0},{4,6},{6,4},{1,3},{3,1},{5,7},{7,5},{8,10},{10,8},{12,... | collective-permute-start | bytes 294920 | tf_op jit(solution)/shard_map/ppermute | solution.py:51
  6.7 2.6 %collective-permute-start.3 = (bf16[24,2048]{1,0:T(8,128)(2,1)}, bf16[24,2048]{1,0:T(8,128)(2,1)S(1)}, u32[]{:S(2)}, u32[]{:S(2)}) collective-permute-start(bf16[24,2048]{1,0:T(8,128)(2,1)} %shard_map.114.refs_0_), channel_id=1, source_target_pairs={{0,4},{2,6},{4,0},{6,2},{1,5},{3,7},{5,1},{7,3},{8,12},{10,14},{12... | collective-permute-start | bytes 294920 | tf_op jit(solution)/shard_map/ppermute | solution.py:51
  9.3 1.4 %copy-done = bf16[1,128,3,2048]{3,1,2,0:T(8,128)(2,1)S(1)} copy-done((bf16[1,128,3,2048]{3,1,2,0:T(8,128)(2,1)S(1)}, bf16[1,128,3,2048]{3,1,2,0:T(8,128)(2,1)}, u32[]{:S(2)}) %copy-start) | copy-done | bytes 1572888
  10.8 3.5 %shard_map.117 = (bf16[4096,512]{1,0:T(8,128)(2,1)S(1)}, bf16[512,4096]{1,0:T(8,128)(2,1)S(1)}) custom-call(bf16[4096,512]{1,0:T(8,128)(2,1)} %refs_0_.1, bf16[512,4096]{1,0:T(8,128)(2,1)} %refs_1_.1), custom_call_target="tpu_custom_call" | custom-call | bytes 8388608 | tf_op jit(solution)/shard_map/pallas_call | solution.py:296
  14.9 2.4 %collective-permute-done.3.refs_2_ = bf16[24,2048]{1,0:T(8,128)(2,1)S(1)} collective-permute-done((bf16[24,2048]{1,0:T(8,128)(2,1)}, bf16[24,2048]{1,0:T(8,128)(2,1)S(1)}, u32[]{:S(2)}, u32[]{:S(2)}) %collective-permute-start.3) | collective-permute-done | bytes 98336 | tf_op jit(solution)/shard_map/ppermute | solution.py:51
  19.6 1.6 %collective-permute-start.13 = (bf16[64,2048]{1,0:T(8,128)(2,1)S(1)}, bf16[64,2048]{1,0:T(8,128)(2,1)S(1)}, u32[]{:S(2)}, u32[]{:S(2)}) collective-permute-start(bf16[64,2048]{1,0:T(8,128)(2,1)S(1)} %get-tuple-element.26.refs_0_), channel_id=1, source_target_pairs={{0,16},{1,9},{8,24},{9,1},{16,0},{17,25},{24,8},{25,17},{2,18},{3,... | collective-permute-start | bytes 786440 | tf_op jit(solution)/shard_map/ppermute | solution.py:57
  21.2 1.5 %collective-permute-start.14 = (bf16[64,2048]{1,0:T(8,128)(2,1)S(1)}, bf16[64,2048]{1,0:T(8,128)(2,1)S(1)}, u32[]{:S(2)}, u32[]{:S(2)}) collective-permute-start(bf16[64,2048]{1,0:T(8,128)(2,1)S(1)} %get-tuple-element.26.refs_0_), channel_id=1, source_target_pairs={{0,8},{1,17},{8,0},{9,25},{16,24},{17,1},{24,16},{25,9},{2,10},{3,... | collective-permute-start | bytes 786440 | tf_op jit(solution)/shard_map/ppermute | solution.py:57
  22.9 5.3 %collective-permute-done.13.refs_1_ = bf16[64,2048]{1,0:T(8,128)(2,1)S(1)} collective-permute-done((bf16[64,2048]{1,0:T(8,128)(2,1)S(1)}, bf16[64,2048]{1,0:T(8,128)(2,1)S(1)}, u32[]{:S(2)}, u32[]{:S(2)}) %collective-permute-start.13) | collective-permute-done | bytes 262176 | tf_op jit(solution)/shard_map/ppermute | solution.py:57
  28.3 1.8 %collective-permute-start.23 = (bf16[64,2048]{1,0:T(8,128)(2,1)S(1)}, bf16[64,2048]{1,0:T(8,128)(2,1)S(1)}, u32[]{:S(2)}, u32[]{:S(2)}) collective-permute-start(bf16[64,2048]{1,0:T(8,128)(2,1)S(1)} %collective-permute-done.13.refs_1_), channel_id=1, source_target_pairs={{0,8},{1,17},{8,0},{9,25},{16,24},{17,1},{24,16},{25,9},{2,10},{3,... | collective-permute-start | bytes 786440 | tf_op jit(solution)/shard_map/ppermute | solution.py:57
  30.1 2.7 %collective-permute-start.10 = (bf16[24,2048]{1,0:T(8,128)(2,1)S(1)}, bf16[24,2048]{1,0:T(8,128)(2,1)S(1)}, u32[]{:S(2)}, u32[]{:S(2)}) collective-permute-start(bf16[24,2048]{1,0:T(8,128)(2,1)S(1)} %maximum_maximum_fusion), channel_id=1, source_target_pairs={{0,4},{2,6},{4,0},{6,2},{1,5},{3,7},{5,1},{7,3},{8,12},{10,14},{12... | collective-permute-start | bytes 294920 | tf_op jit(solution)/shard_map/ppermute | solution.py:51
  32.8 1.4 %collective-permute-start.11 = (bf16[24,2048]{1,0:T(8,128)(2,1)S(1)}, bf16[24,2048]{1,0:T(8,128)(2,1)S(1)}, u32[]{:S(2)}, u32[]{:S(2)}) collective-permute-start(bf16[24,2048]{1,0:T(8,128)(2,1)S(1)} %maximum_maximum_fusion), channel_id=1, source_target_pairs={{0,6},{2,4},{4,2},{6,0},{1,7},{3,5},{5,3},{7,1},{8,14},{10,12},{12... | collective-permute-start | bytes 294920 | tf_op jit(solution)/shard_map/ppermute | solution.py:51
  35.4 1.1 %shard_map.119 = (bf16[64,2048]{1,0:T(8,128)(2,1)S(1)}, bf16[64,2048]{1,0:T(8,128)(2,1)S(1)}, bf16[64,2048]{1,0:T(8,128)(2,1)S(1)}, bf16[192,512]{1,0:T(8,128)(2,1)S(1)}) custom-call(f32[192,512]{1,0:T(8,128)S(1)} %shard_map.118.refs_0_, bf16[64,2048]{1,0:T(8,128)(2,1)S(1)} %collective-permute-done.15.refs_1_, ...), custom_call_target="tpu_custom_call" | custom-call | flops 805306368 | bytes 10551296 | tf_op jit(solution)/shard_map/pallas_call | solution.py:30
  36.6 4.4 %collective-permute-done.10 = bf16[24,2048]{1,0:T(8,128)(2,1)S(1)} collective-permute-done((bf16[24,2048]{1,0:T(8,128)(2,1)S(1)}, bf16[24,2048]{1,0:T(8,128)(2,1)S(1)}, u32[]{:S(2)}, u32[]{:S(2)}) %collective-permute-start.10) | collective-permute-done | bytes 98336 | tf_op jit(solution)/shard_map/ppermute | solution.py:51
  46.9 1.5 %collective-permute-start.22 = (bf16[64,2048]{1,0:T(8,128)(2,1)S(1)}, bf16[64,2048]{1,0:T(8,128)(2,1)S(1)}, u32[]{:S(2)}, u32[]{:S(2)}) collective-permute-start(bf16[64,2048]{1,0:T(8,128)(2,1)S(1)} %add_convert_fusion.1), channel_id=1, source_target_pairs={{0,8},{1,17},{8,0},{9,25},{16,24},{17,1},{24,16},{25,9},{2,10},{3,... | collective-permute-start | bytes 786440 | tf_op jit(solution)/shard_map/ppermute | solution.py:57
  49.2 1.3 %collective-permute-start.26 = (bf16[64,2048]{1,0:T(8,128)(2,1)S(1)}, bf16[64,2048]{1,0:T(8,128)(2,1)S(1)}, u32[]{:S(2)}, u32[]{:S(2)}) collective-permute-start(bf16[64,2048]{1,0:T(8,128)(2,1)S(1)} %add_convert_fusion), channel_id=1, source_target_pairs={{0,24},{1,25},{8,16},{9,17},{16,8},{17,9},{24,0},{25,1},{2,26},{3,... | collective-permute-start | bytes 786440 | tf_op jit(solution)/shard_map/ppermute | solution.py:57
  50.5 3.7 %shard_map.113 = bf16[128,2048]{1,0:T(8,128)(2,1)} custom-call(bf16[3,128,2048]{2,1,0:T(8,128)(2,1)S(1)} %bitcast.26, bf16[2,64,2048]{2,1,0:T(8,128)(2,1)S(1)} %collective-permute-done.far_ref, bf16[2,64,2048]{2,1,0:T(8,128)(2,1)S(1)} %collective-permute-done.1.near_ref), custom_call_target="tpu_custom_call" | custom-call | flops 268435456 | bytes 3145728 | tf_op jit(solution)/shard_map/pallas_call | solution.py:422
  54.2 1.9 %shard_map.116 = bf16[24,1024]{1,0:T(8,128)(2,1)S(1)} custom-call(bf16[24,1024]{1,0:T(8,128)(2,1)S(1)} %pad_maximum_fusion.1.q_ref, bf16[96,2048]{1,0:T(8,128)(2,1)S(1)} %pad_maximum_fusion.near_ref, bf16[96,2048]{1,0:T(8,128)(2,1)S(1)} %collective-permute-done.12.far_ref), custom_call_target="tpu_custom_call" | custom-call | flops 18874368 | bytes 884736 | tf_op jit(solution)/shard_map/pallas_call | solution.py:30
  56.2 6.0 %collective-permute-done.26.refs_4_ = bf16[64,2048]{1,0:T(8,128)(2,1)S(1)} collective-permute-done((bf16[64,2048]{1,0:T(8,128)(2,1)S(1)}, bf16[64,2048]{1,0:T(8,128)(2,1)S(1)}, u32[]{:S(2)}, u32[]{:S(2)}) %collective-permute-start.26) | collective-permute-done | bytes 262176 | tf_op jit(solution)/shard_map/ppermute | solution.py:57
  62.7 1.7 %collective-permute-start.27 = (bf16[24,2048]{1,0:T(8,128)(2,1)S(1)}, bf16[24,2048]{1,0:T(8,128)(2,1)S(1)}, u32[]{:S(2)}, u32[]{:S(2)}) collective-permute-start(bf16[24,2048]{1,0:T(8,128)(2,1)S(1)} %get-tuple-element.42), channel_id=1, source_target_pairs={{0,2},{2,0},{4,6},{6,4},{1,3},{3,1},{5,7},{7,5},{8,10},{10,8},{12,... | collective-permute-start | bytes 294920 | tf_op jit(solution)/shard_map/ppermute | solution.py:51
  64.4 1.8 %collective-permute-start.28 = (bf16[24,2048]{1,0:T(8,128)(2,1)S(1)}, bf16[24,2048]{1,0:T(8,128)(2,1)S(1)}, u32[]{:S(2)}, u32[]{:S(2)}) collective-permute-start(bf16[24,2048]{1,0:T(8,128)(2,1)S(1)} %get-tuple-element.43), channel_id=1, source_target_pairs={{0,4},{2,6},{4,0},{6,2},{1,5},{3,7},{5,1},{7,3},{8,12},{10,14},{12... | collective-permute-start | bytes 294920 | tf_op jit(solution)/shard_map/ppermute | solution.py:51
  66.2 1.1 %collective-permute-start.29 = (bf16[24,2048]{1,0:T(8,128)(2,1)S(1)}, bf16[24,2048]{1,0:T(8,128)(2,1)S(1)}, u32[]{:S(2)}, u32[]{:S(2)}) collective-permute-start(bf16[24,2048]{1,0:T(8,128)(2,1)S(1)} %get-tuple-element.44), channel_id=1, source_target_pairs={{0,6},{2,4},{4,2},{6,0},{1,7},{3,5},{5,3},{7,1},{8,14},{10,12},{12... | collective-permute-start | bytes 294920 | tf_op jit(solution)/shard_map/ppermute | solution.py:51
  67.4 7.5 %collective-permute-done.28 = bf16[24,2048]{1,0:T(8,128)(2,1)S(1)} collective-permute-done((bf16[24,2048]{1,0:T(8,128)(2,1)S(1)}, bf16[24,2048]{1,0:T(8,128)(2,1)S(1)}, u32[]{:S(2)}, u32[]{:S(2)}) %collective-permute-start.28) | collective-permute-done | bytes 98336 | tf_op jit(solution)/shard_map/ppermute | solution.py:51
  76.3 0.9 %shard_map.125 = bf16[12,4096]{1,0:T(8,128)(2,1)} custom-call(s32[1,1]{1,0:T(1,128)} %copy.15.count_ref, bf16[24,2048]{1,0:T(8,128)(2,1)S(1)} %add_convert_fusion.3.mine_ref, bf16[24,2048]{1,0:T(8,128)(2,1)S(1)} %collective-permute-done.30.peer_ref, s32[1,128]{1,0:T(1,128)S(1)} %bitcast.28, bf16[1,128]{1,0:T(2,128)(2,1)S(1)} %copy-done.4), custom_call_target="tpu_custom_call" | custom-call | flops 2359296 | bytes 295684 | tf_op jit(solution)/shard_map/pallas_call | solution.py:30
  (79 shorter events, 13.1 us)
Async XLA Ops:
  3.6 10.7 %collective-permute-start.2 = (bf16[24,2048]{1,0:T(8,128)(2,1)}, bf16[24,2048]{1,0:T(8,128)(2,1)S(1)}, u32[]{:S(2)}, u32[]{:S(2)}) collective-permute-start(bf16[24,2048]{1,0:T(8,128)(2,1)} %shard_map.114.refs_0_), channel_id=1, source_target_pairs={{0,2},{2,0},{4,6},{6,4},{1,3},{3,1},{5,7},{7,5},{8,10},{10,8},{12,... | collective-permute-start | bytes 294920 | tf_op jit(solution)/shard_map/ppermute | solution.py:51
  6.7 10.7 %collective-permute-start.3 = (bf16[24,2048]{1,0:T(8,128)(2,1)}, bf16[24,2048]{1,0:T(8,128)(2,1)S(1)}, u32[]{:S(2)}, u32[]{:S(2)}) collective-permute-start(bf16[24,2048]{1,0:T(8,128)(2,1)} %shard_map.114.refs_0_), channel_id=1, source_target_pairs={{0,4},{2,6},{4,0},{6,2},{1,5},{3,7},{5,1},{7,3},{8,12},{10,14},{12... | collective-permute-start | bytes 294920 | tf_op jit(solution)/shard_map/ppermute | solution.py:51
  9.3 8.1 %collective-permute-start.4 = (bf16[24,2048]{1,0:T(8,128)(2,1)}, bf16[24,2048]{1,0:T(8,128)(2,1)S(1)}, u32[]{:S(2)}, u32[]{:S(2)}) collective-permute-start(bf16[24,2048]{1,0:T(8,128)(2,1)} %shard_map.114.refs_0_), channel_id=1, source_target_pairs={{0,6},{2,4},{4,2},{6,0},{1,7},{3,5},{5,3},{7,1},{8,14},{10,12},{12... | collective-permute-start | bytes 294920 | tf_op jit(solution)/shard_map/ppermute | solution.py:51
  9.3 8.6 %collective-permute-start.5 = (bf16[24,2048]{1,0:T(8,128)(2,1)}, bf16[24,2048]{1,0:T(8,128)(2,1)S(1)}, u32[]{:S(2)}, u32[]{:S(2)}) collective-permute-start(bf16[24,2048]{1,0:T(8,128)(2,1)} %shard_map.114.refs_0_), channel_id=1, source_target_pairs={{0,1},{1,0},{2,3},{3,2},{4,5},{5,4},{6,7},{7,6},{8,9},{9,8},{10,11... | collective-permute-start | bytes 294920 | tf_op jit(solution)/shard_map/ppermute | solution.py:46
  19.6 8.6 %collective-permute-start.13 = (bf16[64,2048]{1,0:T(8,128)(2,1)S(1)}, bf16[64,2048]{1,0:T(8,128)(2,1)S(1)}, u32[]{:S(2)}, u32[]{:S(2)}) collective-permute-start(bf16[64,2048]{1,0:T(8,128)(2,1)S(1)} %get-tuple-element.26.refs_0_), channel_id=1, source_target_pairs={{0,16},{1,9},{8,24},{9,1},{16,0},{17,25},{24,8},{25,17},{2,18},{3,... | collective-permute-start | bytes 786440 | tf_op jit(solution)/shard_map/ppermute | solution.py:57
  21.2 8.9 %collective-permute-start.14 = (bf16[64,2048]{1,0:T(8,128)(2,1)S(1)}, bf16[64,2048]{1,0:T(8,128)(2,1)S(1)}, u32[]{:S(2)}, u32[]{:S(2)}) collective-permute-start(bf16[64,2048]{1,0:T(8,128)(2,1)S(1)} %get-tuple-element.26.refs_0_), channel_id=1, source_target_pairs={{0,8},{1,17},{8,0},{9,25},{16,24},{17,1},{24,16},{25,9},{2,10},{3,... | collective-permute-start | bytes 786440 | tf_op jit(solution)/shard_map/ppermute | solution.py:57
  22.7 10.1 %collective-permute-start.15 = (bf16[64,2048]{1,0:T(8,128)(2,1)S(1)}, bf16[64,2048]{1,0:T(8,128)(2,1)S(1)}, u32[]{:S(2)}, u32[]{:S(2)}) collective-permute-start(bf16[64,2048]{1,0:T(8,128)(2,1)S(1)} %get-tuple-element.26.refs_0_), channel_id=1, source_target_pairs={{0,1},{1,0},{2,3},{3,2},{4,5},{5,4},{6,7},{7,6},{8,9},{9,8},{10,11... | collective-permute-start | bytes 786440 | tf_op jit(solution)/shard_map/ppermute | solution.py:46
  28.3 5.9 %collective-permute-start.17 = (bf16[64,2048]{1,0:T(8,128)(2,1)S(1)}, bf16[64,2048]{1,0:T(8,128)(2,1)S(1)}, u32[]{:S(2)}, u32[]{:S(2)}) collective-permute-start(bf16[64,2048]{1,0:T(8,128)(2,1)S(1)} %collective-permute-done.13.refs_1_), channel_id=1, source_target_pairs={{0,1},{1,0},{2,3},{3,2},{4,5},{5,4},{6,7},{7,6},{8,9},{9,8},{10,11... | collective-permute-start | bytes 786440 | tf_op jit(solution)/shard_map/ppermute | solution.py:46
  28.3 13.2 %collective-permute-start.23 = (bf16[64,2048]{1,0:T(8,128)(2,1)S(1)}, bf16[64,2048]{1,0:T(8,128)(2,1)S(1)}, u32[]{:S(2)}, u32[]{:S(2)}) collective-permute-start(bf16[64,2048]{1,0:T(8,128)(2,1)S(1)} %collective-permute-done.13.refs_1_), channel_id=1, source_target_pairs={{0,8},{1,17},{8,0},{9,25},{16,24},{17,1},{24,16},{25,9},{2,10},{3,... | collective-permute-start | bytes 786440 | tf_op jit(solution)/shard_map/ppermute | solution.py:57
  30.1 4.7 %collective-permute-start.16 = (bf16[64,2048]{1,0:T(8,128)(2,1)S(1)}, bf16[64,2048]{1,0:T(8,128)(2,1)S(1)}, u32[]{:S(2)}, u32[]{:S(2)}) collective-permute-start(bf16[64,2048]{1,0:T(8,128)(2,1)S(1)} %collective-permute-done.14.refs_2_), channel_id=1, source_target_pairs={{0,1},{1,0},{2,3},{3,2},{4,5},{5,4},{6,7},{7,6},{8,9},{9,8},{10,11... | collective-permute-start | bytes 786440 | tf_op jit(solution)/shard_map/ppermute | solution.py:46
  30.1 10.9 %collective-permute-start.10 = (bf16[24,2048]{1,0:T(8,128)(2,1)S(1)}, bf16[24,2048]{1,0:T(8,128)(2,1)S(1)}, u32[]{:S(2)}, u32[]{:S(2)}) collective-permute-start(bf16[24,2048]{1,0:T(8,128)(2,1)S(1)} %maximum_maximum_fusion), channel_id=1, source_target_pairs={{0,4},{2,6},{4,0},{6,2},{1,5},{3,7},{5,1},{7,3},{8,12},{10,14},{12... | collective-permute-start | bytes 294920 | tf_op jit(solution)/shard_map/ppermute | solution.py:51
  32.8 8.2 %collective-permute-start.11 = (bf16[24,2048]{1,0:T(8,128)(2,1)S(1)}, bf16[24,2048]{1,0:T(8,128)(2,1)S(1)}, u32[]{:S(2)}, u32[]{:S(2)}) collective-permute-start(bf16[24,2048]{1,0:T(8,128)(2,1)S(1)} %maximum_maximum_fusion), channel_id=1, source_target_pairs={{0,6},{2,4},{4,2},{6,0},{1,7},{3,5},{5,3},{7,1},{8,14},{10,12},{12... | collective-permute-start | bytes 294920 | tf_op jit(solution)/shard_map/ppermute | solution.py:51
  34.1 7.7 %collective-permute-start.9 = (bf16[24,2048]{1,0:T(8,128)(2,1)S(1)}, bf16[24,2048]{1,0:T(8,128)(2,1)S(1)}, u32[]{:S(2)}, u32[]{:S(2)}) collective-permute-start(bf16[24,2048]{1,0:T(8,128)(2,1)S(1)} %maximum_maximum_fusion), channel_id=1, source_target_pairs={{0,2},{2,0},{4,6},{6,4},{1,3},{3,1},{5,7},{7,5},{8,10},{10,8},{12,... | collective-permute-start | bytes 294920 | tf_op jit(solution)/shard_map/ppermute | solution.py:51
  34.7 13.7 %collective-permute-start = (bf16[2,64,2048]{2,1,0:T(8,128)(2,1)S(1)}, bf16[2,64,2048]{2,1,0:T(8,128)(2,1)S(1)}, u32[]{:S(2)}, u32[]{:S(2)}) collective-permute-start(bf16[2,64,2048]{2,1,0:T(8,128)(2,1)S(1)} %get-tuple-element.24), channel_id=1, source_target_pairs={{1,2},{3,4},{5,6},{2,1},{4,3},{6,5},{9,10},{11,12},{13,14},{10,9},... | collective-permute-start | bytes 1572872 | tf_op jit(solution)/shard_map/ppermute | solution.py:402
  41.0 8.2 %collective-permute-start.1 = (bf16[2,64,2048]{2,1,0:T(8,128)(2,1)S(1)}, bf16[2,64,2048]{2,1,0:T(8,128)(2,1)S(1)}, u32[]{:S(2)}, u32[]{:S(2)}) collective-permute-start(bf16[2,64,2048]{2,1,0:T(8,128)(2,1)S(1)} %get-tuple-element.25), channel_id=1, source_target_pairs={{0,1},{1,0},{2,3},{3,2},{4,5},{5,4},{6,7},{7,6},{8,9},{9,8},{10,11... | collective-permute-start | bytes 1572872 | tf_op jit(solution)/shard_map/ppermute | solution.py:46
  41.0 3.7 %collective-permute-start.21 = (bf16[64,2048]{1,0:T(8,128)(2,1)S(1)}, bf16[64,2048]{1,0:T(8,128)(2,1)S(1)}, u32[]{:S(2)}, u32[]{:S(2)}) collective-permute-start(bf16[64,2048]{1,0:T(8,128)(2,1)S(1)} %get-tuple-element.38), channel_id=1, source_target_pairs={{0,1},{1,0},{2,3},{3,2},{4,5},{5,4},{6,7},{7,6},{8,9},{9,8},{10,11... | collective-permute-start | bytes 786440 | tf_op jit(solution)/shard_map/ppermute | solution.py:46
  41.9 12.3 %collective-permute-start.12 = (bf16[96,2048]{1,0:T(8,128)(2,1)S(1)}, bf16[96,2048]{1,0:T(8,128)(2,1)S(1)}, u32[]{:S(2)}, u32[]{:S(2)}) collective-permute-start(bf16[96,2048]{1,0:T(8,128)(2,1)S(1)} %pad_maximum_fusion.near_ref), channel_id=1, source_target_pairs={{0,1},{1,0},{2,3},{3,2},{4,5},{5,4},{6,7},{7,6},{8,9},{9,8},{10,11... | collective-permute-start | bytes 1179656 | tf_op jit(solution)/shard_map/ppermute | solution.py:46
  44.7 11.4 %collective-permute-start.18 = (bf16[64,2048]{1,0:T(8,128)(2,1)S(1)}, bf16[64,2048]{1,0:T(8,128)(2,1)S(1)}, u32[]{:S(2)}, u32[]{:S(2)}) collective-permute-start(bf16[64,2048]{1,0:T(8,128)(2,1)S(1)} %get-tuple-element.34), channel_id=1, source_target_pairs={{0,1},{1,0},{2,3},{3,2},{4,5},{5,4},{6,7},{7,6},{8,9},{9,8},{10,11... | collective-permute-start | bytes 786440 | tf_op jit(solution)/shard_map/ppermute | solution.py:46
  46.9 9.3 %collective-permute-start.22 = (bf16[64,2048]{1,0:T(8,128)(2,1)S(1)}, bf16[64,2048]{1,0:T(8,128)(2,1)S(1)}, u32[]{:S(2)}, u32[]{:S(2)}) collective-permute-start(bf16[64,2048]{1,0:T(8,128)(2,1)S(1)} %add_convert_fusion.1), channel_id=1, source_target_pairs={{0,8},{1,17},{8,0},{9,25},{16,24},{17,1},{24,16},{25,9},{2,10},{3,... | collective-permute-start | bytes 786440 | tf_op jit(solution)/shard_map/ppermute | solution.py:57
  48.4 7.8 %collective-permute-start.20 = (bf16[64,2048]{1,0:T(8,128)(2,1)S(1)}, bf16[64,2048]{1,0:T(8,128)(2,1)S(1)}, u32[]{:S(2)}, u32[]{:S(2)}) collective-permute-start(bf16[64,2048]{1,0:T(8,128)(2,1)S(1)} %add_convert_fusion.2), channel_id=1, source_target_pairs={{0,16},{1,9},{8,24},{9,1},{16,0},{17,25},{24,8},{25,17},{2,18},{3,... | collective-permute-start | bytes 786440 | tf_op jit(solution)/shard_map/ppermute | solution.py:57
  49.2 13.1 %collective-permute-start.26 = (bf16[64,2048]{1,0:T(8,128)(2,1)S(1)}, bf16[64,2048]{1,0:T(8,128)(2,1)S(1)}, u32[]{:S(2)}, u32[]{:S(2)}) collective-permute-start(bf16[64,2048]{1,0:T(8,128)(2,1)S(1)} %add_convert_fusion), channel_id=1, source_target_pairs={{0,24},{1,25},{8,16},{9,17},{16,8},{17,9},{24,0},{25,1},{2,26},{3,... | collective-permute-start | bytes 786440 | tf_op jit(solution)/shard_map/ppermute | solution.py:57
  62.7 4.7 %collective-permute-start.27 = (bf16[24,2048]{1,0:T(8,128)(2,1)S(1)}, bf16[24,2048]{1,0:T(8,128)(2,1)S(1)}, u32[]{:S(2)}, u32[]{:S(2)}) collective-permute-start(bf16[24,2048]{1,0:T(8,128)(2,1)S(1)} %get-tuple-element.42), channel_id=1, source_target_pairs={{0,2},{2,0},{4,6},{6,4},{1,3},{3,1},{5,7},{7,5},{8,10},{10,8},{12,... | collective-permute-start | bytes 294920 | tf_op jit(solution)/shard_map/ppermute | solution.py:51
  64.4 10.5 %collective-permute-start.28 = (bf16[24,2048]{1,0:T(8,128)(2,1)S(1)}, bf16[24,2048]{1,0:T(8,128)(2,1)S(1)}, u32[]{:S(2)}, u32[]{:S(2)}) collective-permute-start(bf16[24,2048]{1,0:T(8,128)(2,1)S(1)} %get-tuple-element.43), channel_id=1, source_target_pairs={{0,4},{2,6},{4,0},{6,2},{1,5},{3,7},{5,1},{7,3},{8,12},{10,14},{12... | collective-permute-start | bytes 294920 | tf_op jit(solution)/shard_map/ppermute | solution.py:51
  66.2 8.7 %collective-permute-start.29 = (bf16[24,2048]{1,0:T(8,128)(2,1)S(1)}, bf16[24,2048]{1,0:T(8,128)(2,1)S(1)}, u32[]{:S(2)}, u32[]{:S(2)}) collective-permute-start(bf16[24,2048]{1,0:T(8,128)(2,1)S(1)} %get-tuple-element.44), channel_id=1, source_target_pairs={{0,6},{2,4},{4,2},{6,0},{1,7},{3,5},{5,3},{7,1},{8,14},{10,12},{12... | collective-permute-start | bytes 294920 | tf_op jit(solution)/shard_map/ppermute | solution.py:51
  (13 other events, 100.6 us)

commit v7 on v6

--- a/solution.py
+++ b/solution.py
@@ -17,6 +17,7 @@
 HALF_WIN = 64
 MARK = 1048576.0
 F32, BF16 = jnp.float32, jnp.bfloat16
+SCALE = math.log2(math.e) / math.sqrt(HEAD_DIM)
 VMEM = pl.BlockSpec(memory_space=pltpu.VMEM)
 SMEM = pl.BlockSpec(memory_space=pltpu.SMEM)
 
@@ -117,44 +118,80 @@
 
 
 def compact_kernel(parts, *refs):
-    mine, peer, (out_ref, place_ref) = refs[:parts], refs[parts : 2 * parts], refs[2 * parts :]
+    blocks, out_ref = refs[: 2 * parts], refs[2 * parts]
     live_rows, width = out_ref.shape
-    n = mine[0].shape[0]
+    n = blocks[0].shape[0]
     core = lax.axis_index("fsdp")
+    group = 2 * parts if 2 * parts * n <= 512 else 1
+
+    def place_of(index):
+        other = index >= parts * n
+        index = jnp.where(other, index - parts * n, index)
+        turned = jnp.where(lax.rem(index, 2 * CAP) < CAP, index + CAP, index - CAP)
+        return jnp.where(other, turned, index)
+
+    def live_of(first, data):
+        index = iota((data.shape[0], 1), 0) + first * n
+        usable = (lax.rem(index, 2 * CAP) < CAP) == (core == 0)
+        return jnp.where(usable & (data[:, 0:128].astype(F32)[:, 0:1] < MARK / 2), 1.0, 0.0)
+
+    starts = range(0, 2 * parts, group)
+    datas = [jnp.concatenate([r[...] for r in blocks[f : f + group]], axis=0) for f in starts]
+    lives = [live_of(f, d) for f, d in zip(starts, datas)]
+    total = jnp.zeros((live_rows, width), F32)
+    m = group * n
+    up, side = iota((m, m), 0), iota((m, m), 1)
+    for f, data, live in zip(starts, datas, lives):
+        at = place_of(side + f * n)
+        ahead = jnp.zeros((1, m), F32)
+        for g, other in zip(starts, lives):
+            before = jnp.where(place_of(up + g * n) < at, other, 0.0)
+            ahead = ahead + jnp.sum(before, axis=0, keepdims=True)
+        there = jnp.sum(jnp.where(up == side, live, 0.0), axis=0, keepdims=True)
+        to_row = iota((live_rows, m), 0).astype(F32) == ahead
+        pick = jnp.where(to_row & (there > 0.5), 1.0, 0.0).astype(BF16)
+        total = total + jnp.dot(pick, data, preferred_element_type=F32)
+    out_ref[...] = total.astype(BF16)
+
+
+def compact(mine, peer, live_rows):
+    n, width = mine[0].shape
+    return call(
+        functools.partial(compact_kernel, len(mine)),
+        [struct((live_rows, width))],
+        [*mine, *peer],
+        0,
+        4 * len(mine) * n * live_rows * width,
+    )[0]
+
+
+def place_kernel(parts, *refs):
+    mine, peer, place_ref = refs[:parts], refs[parts : 2 * parts], refs[2 * parts]
+    _, n, live_rows = place_ref.shape
     up, side = iota((n, n), 0), iota((n, n), 1)
-    turned = jnp.where(lax.rem(side, 2 * CAP) < CAP, side + CAP, side - CAP)
-    own = (lax.rem(iota((n, 1), 0), 2 * CAP) < CAP) == (core == 0)
-    usable = (lax.rem(iota((1, n), 1), 2 * CAP) < CAP) == (core == 0)
+    own = (lax.rem(iota((n, 1), 0), 2 * CAP) < CAP) == (lax.axis_index("fsdp") == 0)
     base = jnp.zeros((1, 1), F32)
-    total = jnp.zeros((live_rows, width), F32)
     for k in range(parts):
         mark = jnp.where(
             own, mine[k][:, 0:128].astype(F32)[:, 0:1], peer[k][:, 0:128].astype(F32)[:, 0:1]
         )
         live = jnp.where(mark < MARK / 2, 1.0, 0.0)
-        for ref, at in ((mine[k], side), (peer[k], turned)):
-            there = jnp.sum(jnp.where(up == at, live, 0.0), axis=0, keepdims=True)
-            ahead = jnp.sum(jnp.where(up < at, live, 0.0), axis=0, keepdims=True) + base
-            to_row = iota((live_rows, n), 0).astype(F32) == ahead
-            pick = jnp.where(to_row & (there > 0.5) & usable, 1.0, 0.0).astype(BF16)
-            total = total + jnp.dot(pick, ref[...], preferred_element_type=F32)
         row = jnp.sum(jnp.where(up == side, live, 0.0), axis=0, keepdims=True)
         ahead = jnp.sum(jnp.where(side < up, row, 0.0), axis=1, keepdims=True) + base
         at = iota((n, live_rows), 1).astype(F32) == ahead
         place_ref[k, :, :] = jnp.where(at & (live > 0.5), 1.0, 0.0).astype(BF16)
         base = base + jnp.sum(live, axis=0, keepdims=True)
-    out_ref[...] = total.astype(BF16)
-
-
-def compact(mine, peer, live_rows):
-    n, width = mine[0].shape
-    return call(
-        functools.partial(compact_kernel, len(mine)),
-        [struct((live_rows, width)), struct((len(mine), n, live_rows))],
+
+
+def place(mine, peer, live_rows):
+    n = mine[0].shape[0]
+    return call(
+        functools.partial(place_kernel, len(mine)),
+        [struct((len(mine), n, live_rows))],
         [*mine, *peer],
         0,
-        4 * len(mine) * n * live_rows * width,
-    )
+        4 * len(mine) * n * live_rows,
+    )[0]
 
 
 def spread_kernel(parts, terms, place_ref, *refs):
@@ -321,7 +358,7 @@
     win, wout = load(win, wout)
     blocks = gather_seq(own)
     peers = [swap_core(x) for x in blocks]
-    x0, place = compact(blocks, peers, MEAN_LIVE * devices)
+    x0 = compact(blocks, peers, MEAN_LIVE * devices)
     heavy_qkv, counts_later, _ = lax.optimization_barrier((heavy_qkv, counts, x0))
     x1 = swap_doc(x0, NEAR)
     x2 = swap_doc(x0, OTHER)
@@ -334,8 +371,9 @@
     got2 = swap_doc(total(keep[2], back[1]), OTHER)
     send3, hidden = hide(enter((x3,), win), (p3,), win, wout)
     keep3 = leave(hidden, wout, 1)
+    back_to = place(blocks, peers, MEAN_LIVE * devices)
     got3 = swap_doc(total(keep3[0], swap_core(send3[0])), DIAGONAL)
-    summed = scatter_seq(spread(place, (keep[0], back[0], got1, got2, got3)))
+    summed = scatter_seq(spread(back_to, (keep[0], back[0], got1, got2, got3)))
     return finish(counts, summed, swap_core(summed), order, score), heavy_qkv, counts_later
 
 
@@ -363,10 +401,10 @@
         s = lax.dot_general(
             qkv_ref[0, :, at], keys, (((1,), (1,)), ((), ())), preferred_element_type=F32
         )
-        s = s * (1.0 / math.sqrt(HEAD_DIM)) + bias
-        e = jnp.exp(s - jnp.max(s, axis=1, keepdims=True))
+        s = s * SCALE + bias
+        e = jnp.exp2(s - jnp.max(s, axis=1, keepdims=True))
         y = jnp.dot(e.astype(BF16), values, preferred_element_type=F32)
-        out_ref[:, at] = (y / jnp.sum(e, axis=1, keepdims=True)).astype(BF16)
+        out_ref[:, at] = (y * (1.0 / jnp.sum(e, axis=1, keepdims=True))).astype(BF16)
 
 
 def halo_kernel(planes_ref, far_ref, near_ref, sems):
@@ -438,14 +476,14 @@
         s = lax.dot_general(
             q_ref[:, at], kv[:, at], (((1,), (1,)), ((), ())), preferred_element_type=F32
         )
-        s = jnp.where(usable, s * (1.0 / math.sqrt(HEAD_DIM)), -1e30)
-        e = jnp.exp(s - jnp.max(s, axis=1, keepdims=True))
+        s = jnp.where(usable, s * SCALE, -1e30)
+        e = jnp.exp2(s - jnp.max(s, axis=1, keepdims=True))
         y = jnp.dot(
             e.astype(BF16),
             kv[:, width + h * HEAD_DIM : width + (h + 1) * HEAD_DIM],
             preferred_element_type=F32,
         )
-        out_ref[:, at] = (y / jnp.sum(e, axis=1, keepdims=True)).astype(BF16)
+        out_ref[:, at] = (y * (1.0 / jnp.sum(e, axis=1, keepdims=True))).astype(BF16)
 
 
 def heavy_branch(qkv, slot_live):

time: 77.4 us -> 76.8 us (level)
  waiting for transfers between devices: 28.9 us -> 27.2 us
  starting transfers between devices: 26.1 us -> 27.4 us
    ppermute x9, waiting for transfers between devices: 14.7 us -> 12.8 us  [swap_seq(): return lax.ppermute(x, 'seq', [(i, i ^ mask) for i in range(n)])]
    ppermute x15, starting transfers between devices: 2.75 us -> 4.02 us  [swap_core(): return lax.ppermute(x, 'fsdp', [(0, 1), (1, 0)])]
    ppermute x15, waiting for transfers between devices: 2.79 us -> 3.87 us  [swap_core(): return lax.ppermute(x, 'fsdp', [(0, 1), (1, 0)])]
    ppermute x6, waiting for transfers between devices: 11.4 us -> 10.5 us  [swap_doc(): return lax.ppermute(x, ('dp', 'fsdp'), pairs)]
    pallas_call x11 -> x12, Pallas kernels: 10.6 us -> 10.4 us  [call(): pl.pallas_call(body, out_shape=outs, in_specs=[SMEM] * scalars + [VMEM] *...]
  transfers between devices with their start and end apart: 31 -> 31, of which waited for: 12 -> 13; matrix products, arithmetic and copies ran while one was open for 2% -> 2% of each run, Pallas kernels for 17% -> 18%
where the time goes in v7:
time: 76.8 us; the launch traced here: 76.6 us
  starting transfers between devices  27.4 us (36%)
  waiting for transfers between devices  27.2 us (35%)
  Pallas kernels  17.7 us (23%)
  local copies, waits for them, and re-layouts  1.59 us (2%)
  between operations  1.55 us (2%)
  other arithmetic  1.12 us (1%)
    ppermute x9, starting transfers between devices, swap_seq(): return lax.ppermute(x, 'seq', [(i, i ^ mask) for i in range(n)])  14.6 us
    ppermute x9, waiting for transfers between devices, swap_seq(): return lax.ppermute(x, 'seq', [(i, i ^ mask) for i in range(n)])  12.8 us
    ppermute x6, waiting for transfers between devices, swap_doc(): return lax.ppermute(x, ('dp', 'fsdp'), pairs)  10.5 us
    pallas_call x12, Pallas kernels, call(): pl.pallas_call(body, out_shape=outs, in_specs=[SMEM] * scalars + [VMEM] *...  10.4 us
    ppermute x6, starting transfers between devices, swap_doc(): return lax.ppermute(x, ('dp', 'fsdp'), pairs)  8.12 us
    ppermute x15, starting transfers between devices, swap_core(): return lax.ppermute(x, 'fsdp', [(0, 1), (1, 0)])  4.02 us
    ppermute x15, waiting for transfers between devices, swap_core(): return lax.ppermute(x, 'fsdp', [(0, 1), (1, 0)])  3.87 us
    pallas_call x1, Pallas kernels, light_branch(): return run(planes, far, near)  3.71 us
  transfers between devices with their start and end apart: 31, of which 13 were waited for; matrix products, arithmetic and copies ran while one was open for 2% of the time, Pallas kernels for 18%

profile of v7, /device:TPU:0, one launch (start us, length us, event | category | flops | bytes accessed | tf_op | source)
XLA Modules:
  0.0 76.6 jit_solution(15688629029952202022)
XLA Ops:
  1.3 2.4 %shard_map.114.refs_0_ = bf16[24,2048]{1,0:T(8,128)(2,1)} custom-call(s32[1,1]{1,0:T(1,128)} %copy.15.count_ref, bf16[128,4096]{1,0:T(8,128)(2,1)} %bitcast.29, s32[1,128]{1,0:T(1,128)} %bitcast.27, f32[1,4096]{1,0:T(1,128)} %bitcast.34), custom_call_target="tpu_custom_call" | custom-call | flops 25165824 | bytes 1163780 | tf_op jit(solution)/shard_map/pallas_call | solution.py:31
  3.6 3.1 %collective-permute-start.2 = (bf16[24,2048]{1,0:T(8,128)(2,1)}, bf16[24,2048]{1,0:T(8,128)(2,1)S(1)}, u32[]{:S(2)}, u32[]{:S(2)}) collective-permute-start(bf16[24,2048]{1,0:T(8,128)(2,1)} %shard_map.114.refs_0_), channel_id=1, source_target_pairs={{0,2},{2,0},{4,6},{6,4},{1,3},{3,1},{5,7},{7,5},{8,10},{10,8},{12,... | collective-permute-start | bytes 294920 | tf_op jit(solution)/shard_map/ppermute | solution.py:52
  6.7 2.6 %collective-permute-start.3 = (bf16[24,2048]{1,0:T(8,128)(2,1)}, bf16[24,2048]{1,0:T(8,128)(2,1)S(1)}, u32[]{:S(2)}, u32[]{:S(2)}) collective-permute-start(bf16[24,2048]{1,0:T(8,128)(2,1)} %shard_map.114.refs_0_), channel_id=1, source_target_pairs={{0,4},{2,6},{4,0},{6,2},{1,5},{3,7},{5,1},{7,3},{8,12},{10,14},{12... | collective-permute-start | bytes 294920 | tf_op jit(solution)/shard_map/ppermute | solution.py:52
  9.3 1.4 %copy-done = bf16[1,128,3,2048]{3,1,2,0:T(8,128)(2,1)S(1)} copy-done((bf16[1,128,3,2048]{3,1,2,0:T(8,128)(2,1)S(1)}, bf16[1,128,3,2048]{3,1,2,0:T(8,128)(2,1)}, u32[]{:S(2)}) %copy-start) | copy-done | bytes 1572888
  10.8 3.5 %shard_map.118 = (bf16[4096,512]{1,0:T(8,128)(2,1)S(1)}, bf16[512,4096]{1,0:T(8,128)(2,1)S(1)}) custom-call(bf16[4096,512]{1,0:T(8,128)(2,1)} %refs_0_.1, bf16[512,4096]{1,0:T(8,128)(2,1)} %refs_1_.1), custom_call_target="tpu_custom_call" | custom-call | bytes 8388608 | tf_op jit(solution)/shard_map/pallas_call | solution.py:333
  14.9 2.4 %collective-permute-done.3.refs_2_ = bf16[24,2048]{1,0:T(8,128)(2,1)S(1)} collective-permute-done((bf16[24,2048]{1,0:T(8,128)(2,1)}, bf16[24,2048]{1,0:T(8,128)(2,1)S(1)}, u32[]{:S(2)}, u32[]{:S(2)}) %collective-permute-start.3) | collective-permute-done | bytes 98336 | tf_op jit(solution)/shard_map/ppermute | solution.py:52
  19.2 1.6 %collective-permute-start.13 = (bf16[64,2048]{1,0:T(8,128)(2,1)S(1)}, bf16[64,2048]{1,0:T(8,128)(2,1)S(1)}, u32[]{:S(2)}, u32[]{:S(2)}) collective-permute-start(bf16[64,2048]{1,0:T(8,128)(2,1)S(1)} %shard_map.115.refs_0_), channel_id=1, source_target_pairs={{0,16},{1,9},{8,24},{9,1},{16,0},{17,25},{24,8},{25,17},{2,18},{3,... | collective-permute-start | bytes 786440 | tf_op jit(solution)/shard_map/ppermute | solution.py:58
  20.8 1.5 %collective-permute-start.14 = (bf16[64,2048]{1,0:T(8,128)(2,1)S(1)}, bf16[64,2048]{1,0:T(8,128)(2,1)S(1)}, u32[]{:S(2)}, u32[]{:S(2)}) collective-permute-start(bf16[64,2048]{1,0:T(8,128)(2,1)S(1)} %shard_map.115.refs_0_), channel_id=1, source_target_pairs={{0,8},{1,17},{8,0},{9,25},{16,24},{17,1},{24,16},{25,9},{2,10},{3,... | collective-permute-start | bytes 786440 | tf_op jit(solution)/shard_map/ppermute | solution.py:58
  22.5 5.3 %collective-permute-done.14.refs_2_ = bf16[64,2048]{1,0:T(8,128)(2,1)S(1)} collective-permute-done((bf16[64,2048]{1,0:T(8,128)(2,1)S(1)}, bf16[64,2048]{1,0:T(8,128)(2,1)S(1)}, u32[]{:S(2)}, u32[]{:S(2)}) %collective-permute-start.14) | collective-permute-done | bytes 262176 | tf_op jit(solution)/shard_map/ppermute | solution.py:58
  28.4 1.5 %collective-permute-start.23 = (bf16[64,2048]{1,0:T(8,128)(2,1)S(1)}, bf16[64,2048]{1,0:T(8,128)(2,1)S(1)}, u32[]{:S(2)}, u32[]{:S(2)}) collective-permute-start(bf16[64,2048]{1,0:T(8,128)(2,1)S(1)} %collective-permute-done.13.refs_1_), channel_id=1, source_target_pairs={{0,8},{1,17},{8,0},{9,25},{16,24},{17,1},{24,16},{25,9},{2,10},{3,... | collective-permute-start | bytes 786440 | tf_op jit(solution)/shard_map/ppermute | solution.py:58
  29.9 2.5 %collective-permute-start.11 = (bf16[24,2048]{1,0:T(8,128)(2,1)S(1)}, bf16[24,2048]{1,0:T(8,128)(2,1)S(1)}, u32[]{:S(2)}, u32[]{:S(2)}) collective-permute-start(bf16[24,2048]{1,0:T(8,128)(2,1)S(1)} %maximum_maximum_fusion), channel_id=1, source_target_pairs={{0,6},{2,4},{4,2},{6,0},{1,7},{3,5},{5,3},{7,1},{8,14},{10,12},{12... | collective-permute-start | bytes 294920 | tf_op jit(solution)/shard_map/ppermute | solution.py:52
  32.7 1.7 %collective-permute-start.9 = (bf16[24,2048]{1,0:T(8,128)(2,1)S(1)}, bf16[24,2048]{1,0:T(8,128)(2,1)S(1)}, u32[]{:S(2)}, u32[]{:S(2)}) collective-permute-start(bf16[24,2048]{1,0:T(8,128)(2,1)S(1)} %maximum_maximum_fusion), channel_id=1, source_target_pairs={{0,2},{2,0},{4,6},{6,4},{1,3},{3,1},{5,7},{7,5},{8,10},{10,8},{12,... | collective-permute-start | bytes 294920 | tf_op jit(solution)/shard_map/ppermute | solution.py:52
  35.7 1.1 %shard_map.120 = (bf16[64,2048]{1,0:T(8,128)(2,1)S(1)}, bf16[64,2048]{1,0:T(8,128)(2,1)S(1)}, bf16[64,2048]{1,0:T(8,128)(2,1)S(1)}, bf16[192,512]{1,0:T(8,128)(2,1)S(1)}) custom-call(f32[192,512]{1,0:T(8,128)S(1)} %shard_map.119.refs_0_, bf16[64,2048]{1,0:T(8,128)(2,1)S(1)} %collective-permute-done.15.refs_1_, ...), custom_call_target="tpu_custom_call" | custom-call | flops 805306368 | bytes 10551296 | tf_op jit(solution)/shard_map/pallas_call | solution.py:31
  38.6 3.6 %collective-permute-done.10 = bf16[24,2048]{1,0:T(8,128)(2,1)S(1)} collective-permute-done((bf16[24,2048]{1,0:T(8,128)(2,1)S(1)}, bf16[24,2048]{1,0:T(8,128)(2,1)S(1)}, u32[]{:S(2)}, u32[]{:S(2)}) %collective-permute-start.10) | collective-permute-done | bytes 98336 | tf_op jit(solution)/shard_map/ppermute | solution.py:52
  45.7 1.3 %collective-permute-done.21 = bf16[64,2048]{1,0:T(8,128)(2,1)S(1)} collective-permute-done((bf16[64,2048]{1,0:T(8,128)(2,1)S(1)}, bf16[64,2048]{1,0:T(8,128)(2,1)S(1)}, u32[]{:S(2)}, u32[]{:S(2)}) %collective-permute-start.21) | collective-permute-done | bytes 262176 | tf_op jit(solution)/shard_map/ppermute | solution.py:47
  49.2 1.1 %collective-permute-start.22 = (bf16[64,2048]{1,0:T(8,128)(2,1)S(1)}, bf16[64,2048]{1,0:T(8,128)(2,1)S(1)}, u32[]{:S(2)}, u32[]{:S(2)}) collective-permute-start(bf16[64,2048]{1,0:T(8,128)(2,1)S(1)} %add_convert_fusion.1), channel_id=1, source_target_pairs={{0,8},{1,17},{8,0},{9,25},{16,24},{17,1},{24,16},{25,9},{2,10},{3,... | collective-permute-start | bytes 786440 | tf_op jit(solution)/shard_map/ppermute | solution.py:58
  50.2 2.0 %collective-permute-start.26 = (bf16[64,2048]{1,0:T(8,128)(2,1)S(1)}, bf16[64,2048]{1,0:T(8,128)(2,1)S(1)}, u32[]{:S(2)}, u32[]{:S(2)}) collective-permute-start(bf16[64,2048]{1,0:T(8,128)(2,1)S(1)} %add_convert_fusion), channel_id=1, source_target_pairs={{0,24},{1,25},{8,16},{9,17},{16,8},{17,9},{24,0},{25,1},{2,26},{3,... | collective-permute-start | bytes 786440 | tf_op jit(solution)/shard_map/ppermute | solution.py:58
  52.5 3.7 %shard_map.113 = bf16[128,2048]{1,0:T(8,128)(2,1)} custom-call(bf16[3,128,2048]{2,1,0:T(8,128)(2,1)S(1)} %bitcast.26, bf16[2,64,2048]{2,1,0:T(8,128)(2,1)S(1)} %collective-permute-done.far_ref, bf16[2,64,2048]{2,1,0:T(8,128)(2,1)S(1)} %collective-permute-done.1.near_ref), custom_call_target="tpu_custom_call" | custom-call | flops 268435456 | bytes 3145728 | tf_op jit(solution)/shard_map/pallas_call | solution.py:460
  56.2 1.9 %shard_map.116 = bf16[24,1024]{1,0:T(8,128)(2,1)S(1)} custom-call(bf16[24,1024]{1,0:T(8,128)(2,1)S(1)} %pad_maximum_fusion.1.q_ref, bf16[96,2048]{1,0:T(8,128)(2,1)S(1)} %pad_maximum_fusion.near_ref, bf16[96,2048]{1,0:T(8,128)(2,1)S(1)} %collective-permute-done.12.far_ref), custom_call_target="tpu_custom_call" | custom-call | flops 18874368 | bytes 884736 | tf_op jit(solution)/shard_map/pallas_call | solution.py:31
  58.1 5.2 %collective-permute-done.20.refs_2_ = bf16[64,2048]{1,0:T(8,128)(2,1)S(1)} collective-permute-done((bf16[64,2048]{1,0:T(8,128)(2,1)S(1)}, bf16[64,2048]{1,0:T(8,128)(2,1)S(1)}, u32[]{:S(2)}, u32[]{:S(2)}) %collective-permute-start.20) | collective-permute-done | bytes 262176 | tf_op jit(solution)/shard_map/ppermute | solution.py:58
  63.8 2.9 %collective-permute-start.29 = (bf16[24,2048]{1,0:T(8,128)(2,1)S(1)}, bf16[24,2048]{1,0:T(8,128)(2,1)S(1)}, u32[]{:S(2)}, u32[]{:S(2)}) collective-permute-start(bf16[24,2048]{1,0:T(8,128)(2,1)S(1)} %get-tuple-element.40), channel_id=1, source_target_pairs={{0,6},{2,4},{4,2},{6,0},{1,7},{3,5},{5,3},{7,1},{8,14},{10,12},{12... | collective-permute-start | bytes 294920 | tf_op jit(solution)/shard_map/ppermute | solution.py:52
  66.6 1.6 %collective-permute-start.27 = (bf16[24,2048]{1,0:T(8,128)(2,1)S(1)}, bf16[24,2048]{1,0:T(8,128)(2,1)S(1)}, u32[]{:S(2)}, u32[]{:S(2)}) collective-permute-start(bf16[24,2048]{1,0:T(8,128)(2,1)S(1)} %get-tuple-element.38), channel_id=1, source_target_pairs={{0,2},{2,0},{4,6},{6,4},{1,3},{3,1},{5,7},{7,5},{8,10},{10,8},{12,... | collective-permute-start | bytes 294920 | tf_op jit(solution)/shard_map/ppermute | solution.py:52
  68.2 3.2 %collective-permute-done.29 = bf16[24,2048]{1,0:T(8,128)(2,1)S(1)} collective-permute-done((bf16[24,2048]{1,0:T(8,128)(2,1)S(1)}, bf16[24,2048]{1,0:T(8,128)(2,1)S(1)}, u32[]{:S(2)}, u32[]{:S(2)}) %collective-permute-start.29) | collective-permute-done | bytes 98336 | tf_op jit(solution)/shard_map/ppermute | solution.py:52
  71.4 2.8 %collective-permute-done.28 = bf16[24,2048]{1,0:T(8,128)(2,1)S(1)} collective-permute-done((bf16[24,2048]{1,0:T(8,128)(2,1)S(1)}, bf16[24,2048]{1,0:T(8,128)(2,1)S(1)}, u32[]{:S(2)}, u32[]{:S(2)}) %collective-permute-start.28) | collective-permute-done | bytes 98336 | tf_op jit(solution)/shard_map/ppermute | solution.py:52
  (80 shorter events, 15.2 us)
Async XLA Ops:
  3.6 10.7 %collective-permute-start.2 = (bf16[24,2048]{1,0:T(8,128)(2,1)}, bf16[24,2048]{1,0:T(8,128)(2,1)S(1)}, u32[]{:S(2)}, u32[]{:S(2)}) collective-permute-start(bf16[24,2048]{1,0:T(8,128)(2,1)} %shard_map.114.refs_0_), channel_id=1, source_target_pairs={{0,2},{2,0},{4,6},{6,4},{1,3},{3,1},{5,7},{7,5},{8,10},{10,8},{12,... | collective-permute-start | bytes 294920 | tf_op jit(solution)/shard_map/ppermute | solution.py:52
  6.7 10.7 %collective-permute-start.3 = (bf16[24,2048]{1,0:T(8,128)(2,1)}, bf16[24,2048]{1,0:T(8,128)(2,1)S(1)}, u32[]{:S(2)}, u32[]{:S(2)}) collective-permute-start(bf16[24,2048]{1,0:T(8,128)(2,1)} %shard_map.114.refs_0_), channel_id=1, source_target_pairs={{0,4},{2,6},{4,0},{6,2},{1,5},{3,7},{5,1},{7,3},{8,12},{10,14},{12... | collective-permute-start | bytes 294920 | tf_op jit(solution)/shard_map/ppermute | solution.py:52
  9.3 8.1 %collective-permute-start.4 = (bf16[24,2048]{1,0:T(8,128)(2,1)}, bf16[24,2048]{1,0:T(8,128)(2,1)S(1)}, u32[]{:S(2)}, u32[]{:S(2)}) collective-permute-start(bf16[24,2048]{1,0:T(8,128)(2,1)} %shard_map.114.refs_0_), channel_id=1, source_target_pairs={{0,6},{2,4},{4,2},{6,0},{1,7},{3,5},{5,3},{7,1},{8,14},{10,12},{12... | collective-permute-start | bytes 294920 | tf_op jit(solution)/shard_map/ppermute | solution.py:52
  9.3 8.6 %collective-permute-start.5 = (bf16[24,2048]{1,0:T(8,128)(2,1)}, bf16[24,2048]{1,0:T(8,128)(2,1)S(1)}, u32[]{:S(2)}, u32[]{:S(2)}) collective-permute-start(bf16[24,2048]{1,0:T(8,128)(2,1)} %shard_map.114.refs_0_), channel_id=1, source_target_pairs={{0,1},{1,0},{2,3},{3,2},{4,5},{5,4},{6,7},{7,6},{8,9},{9,8},{10,11... | collective-permute-start | bytes 294920 | tf_op jit(solution)/shard_map/ppermute | solution.py:47
  14.4 3.5 %collective-permute-start.6 = (bf16[24,2048]{1,0:T(8,128)(2,1)S(1)}, bf16[24,2048]{1,0:T(8,128)(2,1)S(1)}, u32[]{:S(2)}, u32[]{:S(2)}) collective-permute-start(bf16[24,2048]{1,0:T(8,128)(2,1)S(1)} %collective-permute-done.2.refs_1_), channel_id=1, source_target_pairs={{0,1},{1,0},{2,3},{3,2},{4,5},{5,4},{6,7},{7,6},{8,9},{9,8},{10,11... | collective-permute-start | bytes 294920 | tf_op jit(solution)/shard_map/ppermute | solution.py:47
  19.2 9.1 %collective-permute-start.13 = (bf16[64,2048]{1,0:T(8,128)(2,1)S(1)}, bf16[64,2048]{1,0:T(8,128)(2,1)S(1)}, u32[]{:S(2)}, u32[]{:S(2)}) collective-permute-start(bf16[64,2048]{1,0:T(8,128)(2,1)S(1)} %shard_map.115.refs_0_), channel_id=1, source_target_pairs={{0,16},{1,9},{8,24},{9,1},{16,0},{17,25},{24,8},{25,17},{2,18},{3,... | collective-permute-start | bytes 786440 | tf_op jit(solution)/shard_map/ppermute | solution.py:58
  20.8 7.0 %collective-permute-start.14 = (bf16[64,2048]{1,0:T(8,128)(2,1)S(1)}, bf16[64,2048]{1,0:T(8,128)(2,1)S(1)}, u32[]{:S(2)}, u32[]{:S(2)}) collective-permute-start(bf16[64,2048]{1,0:T(8,128)(2,1)S(1)} %shard_map.115.refs_0_), channel_id=1, source_target_pairs={{0,8},{1,17},{8,0},{9,25},{16,24},{17,1},{24,16},{25,9},{2,10},{3,... | collective-permute-start | bytes 786440 | tf_op jit(solution)/shard_map/ppermute | solution.py:58
  22.3 10.2 %collective-permute-start.15 = (bf16[64,2048]{1,0:T(8,128)(2,1)S(1)}, bf16[64,2048]{1,0:T(8,128)(2,1)S(1)}, u32[]{:S(2)}, u32[]{:S(2)}) collective-permute-start(bf16[64,2048]{1,0:T(8,128)(2,1)S(1)} %shard_map.115.refs_0_), channel_id=1, source_target_pairs={{0,1},{1,0},{2,3},{3,2},{4,5},{5,4},{6,7},{7,6},{8,9},{9,8},{10,11... | collective-permute-start | bytes 786440 | tf_op jit(solution)/shard_map/ppermute | solution.py:47
  27.8 4.9 %collective-permute-start.16 = (bf16[64,2048]{1,0:T(8,128)(2,1)S(1)}, bf16[64,2048]{1,0:T(8,128)(2,1)S(1)}, u32[]{:S(2)}, u32[]{:S(2)}) collective-permute-start(bf16[64,2048]{1,0:T(8,128)(2,1)S(1)} %collective-permute-done.14.refs_2_), channel_id=1, source_target_pairs={{0,1},{1,0},{2,3},{3,2},{4,5},{5,4},{6,7},{7,6},{8,9},{9,8},{10,11... | collective-permute-start | bytes 786440 | tf_op jit(solution)/shard_map/ppermute | solution.py:47
  28.3 6.7 %collective-permute-start.17 = (bf16[64,2048]{1,0:T(8,128)(2,1)S(1)}, bf16[64,2048]{1,0:T(8,128)(2,1)S(1)}, u32[]{:S(2)}, u32[]{:S(2)}) collective-permute-start(bf16[64,2048]{1,0:T(8,128)(2,1)S(1)} %collective-permute-done.13.refs_1_), channel_id=1, source_target_pairs={{0,1},{1,0},{2,3},{3,2},{4,5},{5,4},{6,7},{7,6},{8,9},{9,8},{10,11... | collective-permute-start | bytes 786440 | tf_op jit(solution)/shard_map/ppermute | solution.py:47
  28.4 13.8 %collective-permute-start.23 = (bf16[64,2048]{1,0:T(8,128)(2,1)S(1)}, bf16[64,2048]{1,0:T(8,128)(2,1)S(1)}, u32[]{:S(2)}, u32[]{:S(2)}) collective-permute-start(bf16[64,2048]{1,0:T(8,128)(2,1)S(1)} %collective-permute-done.13.refs_1_), channel_id=1, source_target_pairs={{0,8},{1,17},{8,0},{9,25},{16,24},{17,1},{24,16},{25,9},{2,10},{3,... | collective-permute-start | bytes 786440 | tf_op jit(solution)/shard_map/ppermute | solution.py:58
  29.9 7.6 %collective-permute-start.11 = (bf16[24,2048]{1,0:T(8,128)(2,1)S(1)}, bf16[24,2048]{1,0:T(8,128)(2,1)S(1)}, u32[]{:S(2)}, u32[]{:S(2)}) collective-permute-start(bf16[24,2048]{1,0:T(8,128)(2,1)S(1)} %maximum_maximum_fusion), channel_id=1, source_target_pairs={{0,6},{2,4},{4,2},{6,0},{1,7},{3,5},{5,3},{7,1},{8,14},{10,12},{12... | collective-permute-start | bytes 294920 | tf_op jit(solution)/shard_map/ppermute | solution.py:52
  32.5 9.7 %collective-permute-start.10 = (bf16[24,2048]{1,0:T(8,128)(2,1)S(1)}, bf16[24,2048]{1,0:T(8,128)(2,1)S(1)}, u32[]{:S(2)}, u32[]{:S(2)}) collective-permute-start(bf16[24,2048]{1,0:T(8,128)(2,1)S(1)} %maximum_maximum_fusion), channel_id=1, source_target_pairs={{0,4},{2,6},{4,0},{6,2},{1,5},{3,7},{5,1},{7,3},{8,12},{10,14},{12... | collective-permute-start | bytes 294920 | tf_op jit(solution)/shard_map/ppermute | solution.py:52
  32.7 10.0 %collective-permute-start.9 = (bf16[24,2048]{1,0:T(8,128)(2,1)S(1)}, bf16[24,2048]{1,0:T(8,128)(2,1)S(1)}, u32[]{:S(2)}, u32[]{:S(2)}) collective-permute-start(bf16[24,2048]{1,0:T(8,128)(2,1)S(1)} %maximum_maximum_fusion), channel_id=1, source_target_pairs={{0,2},{2,0},{4,6},{6,4},{1,3},{3,1},{5,7},{7,5},{8,10},{10,8},{12,... | collective-permute-start | bytes 294920 | tf_op jit(solution)/shard_map/ppermute | solution.py:52
  35.0 14.2 %collective-permute-start = (bf16[2,64,2048]{2,1,0:T(8,128)(2,1)S(1)}, bf16[2,64,2048]{2,1,0:T(8,128)(2,1)S(1)}, u32[]{:S(2)}, u32[]{:S(2)}) collective-permute-start(bf16[2,64,2048]{2,1,0:T(8,128)(2,1)S(1)} %get-tuple-element.22), channel_id=1, source_target_pairs={{1,2},{3,4},{5,6},{2,1},{4,3},{6,5},{9,10},{11,12},{13,14},{10,9},... | collective-permute-start | bytes 1572872 | tf_op jit(solution)/shard_map/ppermute | solution.py:440
  37.6 12.6 %collective-permute-start.1 = (bf16[2,64,2048]{2,1,0:T(8,128)(2,1)S(1)}, bf16[2,64,2048]{2,1,0:T(8,128)(2,1)S(1)}, u32[]{:S(2)}, u32[]{:S(2)}) collective-permute-start(bf16[2,64,2048]{2,1,0:T(8,128)(2,1)S(1)} %get-tuple-element.23), channel_id=1, source_target_pairs={{0,1},{1,0},{2,3},{3,2},{4,5},{5,4},{6,7},{7,6},{8,9},{9,8},{10,11... | collective-permute-start | bytes 1572872 | tf_op jit(solution)/shard_map/ppermute | solution.py:47
  42.8 13.5 %collective-permute-start.12 = (bf16[96,2048]{1,0:T(8,128)(2,1)S(1)}, bf16[96,2048]{1,0:T(8,128)(2,1)S(1)}, u32[]{:S(2)}, u32[]{:S(2)}) collective-permute-start(bf16[96,2048]{1,0:T(8,128)(2,1)S(1)} %pad_maximum_fusion.near_ref), channel_id=1, source_target_pairs={{0,1},{1,0},{2,3},{3,2},{4,5},{5,4},{6,7},{7,6},{8,9},{9,8},{10,11... | collective-permute-start | bytes 1179656 | tf_op jit(solution)/shard_map/ppermute | solution.py:47
  44.1 14.0 %collective-permute-start.18 = (bf16[64,2048]{1,0:T(8,128)(2,1)S(1)}, bf16[64,2048]{1,0:T(8,128)(2,1)S(1)}, u32[]{:S(2)}, u32[]{:S(2)}) collective-permute-start(bf16[64,2048]{1,0:T(8,128)(2,1)S(1)} %get-tuple-element.30), channel_id=1, source_target_pairs={{0,1},{1,0},{2,3},{3,2},{4,5},{5,4},{6,7},{7,6},{8,9},{9,8},{10,11... | collective-permute-start | bytes 786440 | tf_op jit(solution)/shard_map/ppermute | solution.py:47
  48.6 14.7 %collective-permute-start.20 = (bf16[64,2048]{1,0:T(8,128)(2,1)S(1)}, bf16[64,2048]{1,0:T(8,128)(2,1)S(1)}, u32[]{:S(2)}, u32[]{:S(2)}) collective-permute-start(bf16[64,2048]{1,0:T(8,128)(2,1)S(1)} %add_convert_fusion.2), channel_id=1, source_target_pairs={{0,16},{1,9},{8,24},{9,1},{16,0},{17,25},{24,8},{25,17},{2,18},{3,... | collective-permute-start | bytes 786440 | tf_op jit(solution)/shard_map/ppermute | solution.py:58
  49.2 14.2 %collective-permute-start.22 = (bf16[64,2048]{1,0:T(8,128)(2,1)S(1)}, bf16[64,2048]{1,0:T(8,128)(2,1)S(1)}, u32[]{:S(2)}, u32[]{:S(2)}) collective-permute-start(bf16[64,2048]{1,0:T(8,128)(2,1)S(1)} %add_convert_fusion.1), channel_id=1, source_target_pairs={{0,8},{1,17},{8,0},{9,25},{16,24},{17,1},{24,16},{25,9},{2,10},{3,... | collective-permute-start | bytes 786440 | tf_op jit(solution)/shard_map/ppermute | solution.py:58
  50.2 13.1 %collective-permute-start.26 = (bf16[64,2048]{1,0:T(8,128)(2,1)S(1)}, bf16[64,2048]{1,0:T(8,128)(2,1)S(1)}, u32[]{:S(2)}, u32[]{:S(2)}) collective-permute-start(bf16[64,2048]{1,0:T(8,128)(2,1)S(1)} %add_convert_fusion), channel_id=1, source_target_pairs={{0,24},{1,25},{8,16},{9,17},{16,8},{17,9},{24,0},{25,1},{2,26},{3,... | collective-permute-start | bytes 786440 | tf_op jit(solution)/shard_map/ppermute | solution.py:58
  63.8 7.6 %collective-permute-start.29 = (bf16[24,2048]{1,0:T(8,128)(2,1)S(1)}, bf16[24,2048]{1,0:T(8,128)(2,1)S(1)}, u32[]{:S(2)}, u32[]{:S(2)}) collective-permute-start(bf16[24,2048]{1,0:T(8,128)(2,1)S(1)} %get-tuple-element.40), channel_id=1, source_target_pairs={{0,6},{2,4},{4,2},{6,0},{1,7},{3,5},{5,3},{7,1},{8,14},{10,12},{12... | collective-permute-start | bytes 294920 | tf_op jit(solution)/shard_map/ppermute | solution.py:52
  66.6 7.6 %collective-permute-start.28 = (bf16[24,2048]{1,0:T(8,128)(2,1)S(1)}, bf16[24,2048]{1,0:T(8,128)(2,1)S(1)}, u32[]{:S(2)}, u32[]{:S(2)}) collective-permute-start(bf16[24,2048]{1,0:T(8,128)(2,1)S(1)} %get-tuple-element.39), channel_id=1, source_target_pairs={{0,4},{2,6},{4,0},{6,2},{1,5},{3,7},{5,1},{7,3},{8,12},{10,14},{12... | collective-permute-start | bytes 294920 | tf_op jit(solution)/shard_map/ppermute | solution.py:52
  66.6 7.6 %collective-permute-start.27 = (bf16[24,2048]{1,0:T(8,128)(2,1)S(1)}, bf16[24,2048]{1,0:T(8,128)(2,1)S(1)}, u32[]{:S(2)}, u32[]{:S(2)}) collective-permute-start(bf16[24,2048]{1,0:T(8,128)(2,1)S(1)} %get-tuple-element.38), channel_id=1, source_target_pairs={{0,2},{2,0},{4,6},{6,4},{1,3},{3,1},{5,7},{7,5},{8,10},{10,8},{12,... | collective-permute-start | bytes 294920 | tf_op jit(solution)/shard_map/ppermute | solution.py:52
  (13 other events, 96.1 us)

commit v8 on v7

--- a/solution.py
+++ b/solution.py
@@ -167,7 +167,7 @@
 
 def place_kernel(parts, *refs):
     mine, peer, place_ref = refs[:parts], refs[parts : 2 * parts], refs[2 * parts]
-    _, n, live_rows = place_ref.shape
+    n, live_rows = mine[0].shape[0], place_ref.shape[1]
     up, side = iota((n, n), 0), iota((n, n), 1)
     own = (lax.rem(iota((n, 1), 0), 2 * CAP) < CAP) == (lax.axis_index("fsdp") == 0)
     base = jnp.zeros((1, 1), F32)
@@ -179,7 +179,7 @@
         row = jnp.sum(jnp.where(up == side, live, 0.0), axis=0, keepdims=True)
         ahead = jnp.sum(jnp.where(side < up, row, 0.0), axis=1, keepdims=True) + base
         at = iota((n, live_rows), 1).astype(F32) == ahead
-        place_ref[k, :, :] = jnp.where(at & (live > 0.5), 1.0, 0.0).astype(BF16)
+        place_ref[k * n : (k + 1) * n, :] = jnp.where(at & (live > 0.5), 1.0, 0.0).astype(BF16)
         base = base + jnp.sum(live, axis=0, keepdims=True)
 
 
@@ -187,7 +187,7 @@
     n = mine[0].shape[0]
     return call(
         functools.partial(place_kernel, len(mine)),
-        [struct((len(mine), n, live_rows))],
+        [struct((len(mine) * n, live_rows))],
         [*mine, *peer],
         0,
         4 * len(mine) * n * live_rows,
@@ -196,14 +196,14 @@
 
 def spread_kernel(parts, terms, place_ref, *refs):
     rows = sum(r[...].astype(F32) for r in refs[:terms]).astype(BF16)
+    n = refs[terms].shape[0]
+    slots = jnp.dot(place_ref[...], rows, preferred_element_type=F32).astype(BF16)
     for k in range(parts):
-        refs[terms + k][...] = jnp.dot(
-            place_ref[k, :, :], rows, preferred_element_type=F32
-        ).astype(BF16)
-
-
-def spread(place, terms):
-    parts, n, live_rows = place.shape
+        refs[terms + k][...] = slots[k * n : (k + 1) * n]
+
+
+def spread(place, parts, terms):
+    n, live_rows = place.shape[0] // parts, place.shape[1]
     width = terms[0].shape[1]
     return call(
         functools.partial(spread_kernel, parts, len(terms)),
@@ -294,28 +294,30 @@
     )
 
 
-def finish_kernel(count_ref, mine_ref, peer_ref, order_ref, score_ref, out_ref):
-    rows, half = mine_ref.shape
-    core = lax.axis_index("fsdp")
-    pick = (iota((CAP, rows), 1) == iota((CAP, rows), 0) + core * CAP).astype(BF16)
+def score_kernel(count_ref, order_ref, score_ref, out_ref):
     lanes, slot = iota((CAP, TILE), 1), iota((CAP, TILE), 0)
     order = jnp.broadcast_to(order_ref[...], (CAP, TILE))
     row = jnp.sum(jnp.where(lanes == slot, order, 0), axis=1, keepdims=True)
     score = jnp.sum(jnp.where(lanes == row, score_ref[...].astype(F32), 0.0), axis=1, keepdims=True)
     score = jnp.where(iota((CAP, 1), 0) < count_ref[...], score, 0.0)
+    out_ref[...] = jnp.broadcast_to(score, out_ref.shape)
+
+
+def finish_kernel(mine_ref, peer_ref, score_ref, out_ref):
+    _, half = mine_ref.shape
+    core = lax.axis_index("fsdp")
+    score = score_ref[:, 0:1]
     for ref, start in ((mine_ref, core * half), (peer_ref, (1 - core) * half)):
-        y = jnp.dot(pick, ref[...], preferred_element_type=F32)
+        y = ref[...].astype(F32)
+        y = jnp.where(core == 0, y[:CAP], y[CAP:])
         out_ref[:, pl.ds(pl.multiple_of(start, 128), half)] = (score * y).astype(BF16)
 
 
 def finish(counts, mine, peer, order, score):
     rows, half = mine.shape
-    return call(
-        finish_kernel,
-        [struct((CAP, 2 * half))],
-        [counts, mine, peer, order, score],
-        0,
-        4 * CAP * rows * half,
+    score = call(score_kernel, [struct((CAP, TILE), F32)], [counts, order, score], 0, TILE)[0]
+    return call(
+        finish_kernel, [struct((CAP, 2 * half))], [mine, peer, score], 0, 4 * CAP * rows * half
     )[0]
 
 
@@ -373,7 +375,7 @@
     keep3 = leave(hidden, wout, 1)
     back_to = place(blocks, peers, MEAN_LIVE * devices)
     got3 = swap_doc(total(keep3[0], swap_core(send3[0])), DIAGONAL)
-    summed = scatter_seq(spread(back_to, (keep[0], back[0], got1, got2, got3)))
+    summed = scatter_seq(spread(back_to, len(blocks), (keep[0], back[0], got1, got2, got3)))
     return finish(counts, summed, swap_core(summed), order, score), heavy_qkv, counts_later
 
 
@@ -439,7 +441,7 @@
     pairs = [(i, i + 1) for i in range(1, n - 1, 2)]
     far = lax.ppermute(far, ("seq", "fsdp"), pairs + [(j, i) for i, j in pairs])
     near = swap_core(near)
-    wide = 4 * HEAD_DIM
+    wide = 8 * HEAD_DIM
     run = pl.pallas_call(
         light_kernel,
         out_shape=struct((rows, width)),

time: 76.8 us -> 76.5 us (level)
  Pallas kernels: 17.7 us -> 16.6 us
  waiting for transfers between devices: 27.2 us -> 28.1 us
    pallas_call x1, Pallas kernels: 3.71 us -> 2.61 us  [light_branch(): return run(planes, far, near)]
    ppermute x6, waiting for transfers between devices: 10.5 us -> 11.3 us  [swap_doc(): return lax.ppermute(x, ('dp', 'fsdp'), pairs)]
    pallas_call x12 -> x13, Pallas kernels: 10.4 us -> 10.4 us  [call(): pl.pallas_call(body, out_shape=outs, in_specs=[SMEM] * scalars + [VMEM] *...]
  transfers between devices with their start and end apart: 31 -> 31, of which waited for: 13 -> 13; matrix products, arithmetic and copies ran while one was open for 2% -> 2% of each run, Pallas kernels for 18% -> 17%
where the time goes in v8:
time: 76.5 us; the launch traced here: 76.3 us
  waiting for transfers between devices  28.1 us (37%)
  starting transfers between devices  27.4 us (36%)
  Pallas kernels  16.6 us (22%)
  local copies, waits for them, and re-layouts  1.59 us (2%)
  between operations  1.55 us (2%)
  other arithmetic  1.12 us (1%)
    ppermute x9, starting transfers between devices, swap_seq(): return lax.ppermute(x, 'seq', [(i, i ^ mask) for i in range(n)])  14.6 us
    ppermute x9, waiting for transfers between devices, swap_seq(): return lax.ppermute(x, 'seq', [(i, i ^ mask) for i in range(n)])  12.8 us
    ppermute x6, waiting for transfers between devices, swap_doc(): return lax.ppermute(x, ('dp', 'fsdp'), pairs)  11.3 us
    pallas_call x13, Pallas kernels, call(): pl.pallas_call(body, out_shape=outs, in_specs=[SMEM] * scalars + [VMEM] *...  10.4 us
    ppermute x6, starting transfers between devices, swap_doc(): return lax.ppermute(x, ('dp', 'fsdp'), pairs)  8.12 us
    ppermute x15, starting transfers between devices, swap_core(): return lax.ppermute(x, 'fsdp', [(0, 1), (1, 0)])  4.02 us
    ppermute x15, waiting for transfers between devices, swap_core(): return lax.ppermute(x, 'fsdp', [(0, 1), (1, 0)])  3.89 us
    pallas_call x1, Pallas kernels, load(): pl.pallas_call(load_kernel, out_shape=[struct(a.shape, a.dtype) for a in...  3.52 us
  transfers between devices with their start and end apart: 31, of which 13 were waited for; matrix products, arithmetic and copies ran while one was open for 2% of the time, Pallas kernels for 17%

profile of v8, /device:TPU:0, one launch (start us, length us, event | category | flops | bytes accessed | tf_op | source)
XLA Modules:
  0.0 76.3 jit_solution(5936807999793101418)
XLA Ops:
  1.3 2.4 %shard_map.114.refs_0_ = bf16[24,2048]{1,0:T(8,128)(2,1)} custom-call(s32[1,1]{1,0:T(1,128)} %copy.15.count_ref, bf16[128,4096]{1,0:T(8,128)(2,1)} %bitcast.29, s32[1,128]{1,0:T(1,128)} %bitcast.27, f32[1,4096]{1,0:T(1,128)} %bitcast.34), custom_call_target="tpu_custom_call" | custom-call | flops 25165824 | bytes 1163780 | tf_op jit(solution)/shard_map/pallas_call | solution.py:31
  3.6 3.1 %collective-permute-start.2 = (bf16[24,2048]{1,0:T(8,128)(2,1)}, bf16[24,2048]{1,0:T(8,128)(2,1)S(1)}, u32[]{:S(2)}, u32[]{:S(2)}) collective-permute-start(bf16[24,2048]{1,0:T(8,128)(2,1)} %shard_map.114.refs_0_), channel_id=1, source_target_pairs={{0,2},{2,0},{4,6},{6,4},{1,3},{3,1},{5,7},{7,5},{8,10},{10,8},{12,... | collective-permute-start | bytes 294920 | tf_op jit(solution)/shard_map/ppermute | solution.py:52
  6.7 2.6 %collective-permute-start.3 = (bf16[24,2048]{1,0:T(8,128)(2,1)}, bf16[24,2048]{1,0:T(8,128)(2,1)S(1)}, u32[]{:S(2)}, u32[]{:S(2)}) collective-permute-start(bf16[24,2048]{1,0:T(8,128)(2,1)} %shard_map.114.refs_0_), channel_id=1, source_target_pairs={{0,4},{2,6},{4,0},{6,2},{1,5},{3,7},{5,1},{7,3},{8,12},{10,14},{12... | collective-permute-start | bytes 294920 | tf_op jit(solution)/shard_map/ppermute | solution.py:52
  9.3 1.4 %copy-done = bf16[1,128,3,2048]{3,1,2,0:T(8,128)(2,1)S(1)} copy-done((bf16[1,128,3,2048]{3,1,2,0:T(8,128)(2,1)S(1)}, bf16[1,128,3,2048]{3,1,2,0:T(8,128)(2,1)}, u32[]{:S(2)}) %copy-start) | copy-done | bytes 1572888
  10.8 3.5 %shard_map.118 = (bf16[4096,512]{1,0:T(8,128)(2,1)S(1)}, bf16[512,4096]{1,0:T(8,128)(2,1)S(1)}) custom-call(bf16[4096,512]{1,0:T(8,128)(2,1)} %refs_0_.1, bf16[512,4096]{1,0:T(8,128)(2,1)} %refs_1_.1), custom_call_target="tpu_custom_call" | custom-call | bytes 8388608 | tf_op jit(solution)/shard_map/pallas_call | solution.py:335
  14.9 2.4 %collective-permute-done.3.refs_2_ = bf16[24,2048]{1,0:T(8,128)(2,1)S(1)} collective-permute-done((bf16[24,2048]{1,0:T(8,128)(2,1)}, bf16[24,2048]{1,0:T(8,128)(2,1)S(1)}, u32[]{:S(2)}, u32[]{:S(2)}) %collective-permute-start.3) | collective-permute-done | bytes 98336 | tf_op jit(solution)/shard_map/ppermute | solution.py:52
  19.2 1.6 %collective-permute-start.13 = (bf16[64,2048]{1,0:T(8,128)(2,1)S(1)}, bf16[64,2048]{1,0:T(8,128)(2,1)S(1)}, u32[]{:S(2)}, u32[]{:S(2)}) collective-permute-start(bf16[64,2048]{1,0:T(8,128)(2,1)S(1)} %shard_map.115.refs_0_), channel_id=1, source_target_pairs={{0,16},{1,9},{8,24},{9,1},{16,0},{17,25},{24,8},{25,17},{2,18},{3,... | collective-permute-start | bytes 786440 | tf_op jit(solution)/shard_map/ppermute | solution.py:58
  20.8 1.5 %collective-permute-start.14 = (bf16[64,2048]{1,0:T(8,128)(2,1)S(1)}, bf16[64,2048]{1,0:T(8,128)(2,1)S(1)}, u32[]{:S(2)}, u32[]{:S(2)}) collective-permute-start(bf16[64,2048]{1,0:T(8,128)(2,1)S(1)} %shard_map.115.refs_0_), channel_id=1, source_target_pairs={{0,8},{1,17},{8,0},{9,25},{16,24},{17,1},{24,16},{25,9},{2,10},{3,... | collective-permute-start | bytes 786440 | tf_op jit(solution)/shard_map/ppermute | solution.py:58
  22.5 5.3 %collective-permute-done.14.refs_2_ = bf16[64,2048]{1,0:T(8,128)(2,1)S(1)} collective-permute-done((bf16[64,2048]{1,0:T(8,128)(2,1)S(1)}, bf16[64,2048]{1,0:T(8,128)(2,1)S(1)}, u32[]{:S(2)}, u32[]{:S(2)}) %collective-permute-start.14) | collective-permute-done | bytes 262176 | tf_op jit(solution)/shard_map/ppermute | solution.py:58
  28.4 1.5 %collective-permute-start.23 = (bf16[64,2048]{1,0:T(8,128)(2,1)S(1)}, bf16[64,2048]{1,0:T(8,128)(2,1)S(1)}, u32[]{:S(2)}, u32[]{:S(2)}) collective-permute-start(bf16[64,2048]{1,0:T(8,128)(2,1)S(1)} %collective-permute-done.13.refs_1_), channel_id=1, source_target_pairs={{0,8},{1,17},{8,0},{9,25},{16,24},{17,1},{24,16},{25,9},{2,10},{3,... | collective-permute-start | bytes 786440 | tf_op jit(solution)/shard_map/ppermute | solution.py:58
  29.9 2.5 %collective-permute-start.11 = (bf16[24,2048]{1,0:T(8,128)(2,1)S(1)}, bf16[24,2048]{1,0:T(8,128)(2,1)S(1)}, u32[]{:S(2)}, u32[]{:S(2)}) collective-permute-start(bf16[24,2048]{1,0:T(8,128)(2,1)S(1)} %maximum_maximum_fusion), channel_id=1, source_target_pairs={{0,6},{2,4},{4,2},{6,0},{1,7},{3,5},{5,3},{7,1},{8,14},{10,12},{12... | collective-permute-start | bytes 294920 | tf_op jit(solution)/shard_map/ppermute | solution.py:52
  32.7 1.7 %collective-permute-start.9 = (bf16[24,2048]{1,0:T(8,128)(2,1)S(1)}, bf16[24,2048]{1,0:T(8,128)(2,1)S(1)}, u32[]{:S(2)}, u32[]{:S(2)}) collective-permute-start(bf16[24,2048]{1,0:T(8,128)(2,1)S(1)} %maximum_maximum_fusion), channel_id=1, source_target_pairs={{0,2},{2,0},{4,6},{6,4},{1,3},{3,1},{5,7},{7,5},{8,10},{10,8},{12,... | collective-permute-start | bytes 294920 | tf_op jit(solution)/shard_map/ppermute | solution.py:52
  35.7 1.1 %shard_map.120 = (bf16[64,2048]{1,0:T(8,128)(2,1)S(1)}, bf16[64,2048]{1,0:T(8,128)(2,1)S(1)}, bf16[64,2048]{1,0:T(8,128)(2,1)S(1)}, bf16[192,512]{1,0:T(8,128)(2,1)S(1)}) custom-call(f32[192,512]{1,0:T(8,128)S(1)} %shard_map.119.refs_0_, bf16[64,2048]{1,0:T(8,128)(2,1)S(1)} %collective-permute-done.15.refs_1_, ...), custom_call_target="tpu_custom_call" | custom-call | flops 805306368 | bytes 10551296 | tf_op jit(solution)/shard_map/pallas_call | solution.py:31
  38.6 3.6 %collective-permute-done.10 = bf16[24,2048]{1,0:T(8,128)(2,1)S(1)} collective-permute-done((bf16[24,2048]{1,0:T(8,128)(2,1)S(1)}, bf16[24,2048]{1,0:T(8,128)(2,1)S(1)}, u32[]{:S(2)}, u32[]{:S(2)}) %collective-permute-start.10) | collective-permute-done | bytes 98336 | tf_op jit(solution)/shard_map/ppermute | solution.py:52
  45.7 1.3 %collective-permute-done.21 = bf16[64,2048]{1,0:T(8,128)(2,1)S(1)} collective-permute-done((bf16[64,2048]{1,0:T(8,128)(2,1)S(1)}, bf16[64,2048]{1,0:T(8,128)(2,1)S(1)}, u32[]{:S(2)}, u32[]{:S(2)}) %collective-permute-start.21) | collective-permute-done | bytes 262176 | tf_op jit(solution)/shard_map/ppermute | solution.py:47
  49.2 1.1 %collective-permute-start.22 = (bf16[64,2048]{1,0:T(8,128)(2,1)S(1)}, bf16[64,2048]{1,0:T(8,128)(2,1)S(1)}, u32[]{:S(2)}, u32[]{:S(2)}) collective-permute-start(bf16[64,2048]{1,0:T(8,128)(2,1)S(1)} %add_convert_fusion.1), channel_id=1, source_target_pairs={{0,8},{1,17},{8,0},{9,25},{16,24},{17,1},{24,16},{25,9},{2,10},{3,... | collective-permute-start | bytes 786440 | tf_op jit(solution)/shard_map/ppermute | solution.py:58
  50.2 2.0 %collective-permute-start.26 = (bf16[64,2048]{1,0:T(8,128)(2,1)S(1)}, bf16[64,2048]{1,0:T(8,128)(2,1)S(1)}, u32[]{:S(2)}, u32[]{:S(2)}) collective-permute-start(bf16[64,2048]{1,0:T(8,128)(2,1)S(1)} %add_convert_fusion), channel_id=1, source_target_pairs={{0,24},{1,25},{8,16},{9,17},{16,8},{17,9},{24,0},{25,1},{2,26},{3,... | collective-permute-start | bytes 786440 | tf_op jit(solution)/shard_map/ppermute | solution.py:58
  52.8 2.6 %shard_map.113 = bf16[128,2048]{1,0:T(8,128)(2,1)} custom-call(bf16[3,128,2048]{2,1,0:T(8,128)(2,1)S(1)} %bitcast.26, bf16[2,64,2048]{2,1,0:T(8,128)(2,1)S(1)} %collective-permute-done.far_ref, bf16[2,64,2048]{2,1,0:T(8,128)(2,1)S(1)} %collective-permute-done.1.near_ref), custom_call_target="tpu_custom_call" | custom-call | flops 268435456 | bytes 3145728 | tf_op jit(solution)/shard_map/pallas_call | solution.py:462
  55.4 1.9 %shard_map.116 = bf16[24,1024]{1,0:T(8,128)(2,1)S(1)} custom-call(bf16[24,1024]{1,0:T(8,128)(2,1)S(1)} %pad_maximum_fusion.1.q_ref, bf16[96,2048]{1,0:T(8,128)(2,1)S(1)} %pad_maximum_fusion.near_ref, bf16[96,2048]{1,0:T(8,128)(2,1)S(1)} %collective-permute-done.12.far_ref), custom_call_target="tpu_custom_call" | custom-call | flops 18874368 | bytes 884736 | tf_op jit(solution)/shard_map/pallas_call | solution.py:31
  57.3 6.0 %collective-permute-done.20.refs_2_ = bf16[64,2048]{1,0:T(8,128)(2,1)S(1)} collective-permute-done((bf16[64,2048]{1,0:T(8,128)(2,1)S(1)}, bf16[64,2048]{1,0:T(8,128)(2,1)S(1)}, u32[]{:S(2)}, u32[]{:S(2)}) %collective-permute-start.20) | collective-permute-done | bytes 262176 | tf_op jit(solution)/shard_map/ppermute | solution.py:58
  63.7 2.9 %collective-permute-start.29 = (bf16[24,2048]{1,0:T(8,128)(2,1)S(1)}, bf16[24,2048]{1,0:T(8,128)(2,1)S(1)}, u32[]{:S(2)}, u32[]{:S(2)}) collective-permute-start(bf16[24,2048]{1,0:T(8,128)(2,1)S(1)} %get-tuple-element.40), channel_id=1, source_target_pairs={{0,6},{2,4},{4,2},{6,0},{1,7},{3,5},{5,3},{7,1},{8,14},{10,12},{12... | collective-permute-start | bytes 294920 | tf_op jit(solution)/shard_map/ppermute | solution.py:52
  66.6 1.6 %collective-permute-start.27 = (bf16[24,2048]{1,0:T(8,128)(2,1)S(1)}, bf16[24,2048]{1,0:T(8,128)(2,1)S(1)}, u32[]{:S(2)}, u32[]{:S(2)}) collective-permute-start(bf16[24,2048]{1,0:T(8,128)(2,1)S(1)} %get-tuple-element.38), channel_id=1, source_target_pairs={{0,2},{2,0},{4,6},{6,4},{1,3},{3,1},{5,7},{7,5},{8,10},{10,8},{12,... | collective-permute-start | bytes 294920 | tf_op jit(solution)/shard_map/ppermute | solution.py:52
  68.2 3.2 %collective-permute-done.29 = bf16[24,2048]{1,0:T(8,128)(2,1)S(1)} collective-permute-done((bf16[24,2048]{1,0:T(8,128)(2,1)S(1)}, bf16[24,2048]{1,0:T(8,128)(2,1)S(1)}, u32[]{:S(2)}, u32[]{:S(2)}) %collective-permute-start.29) | collective-permute-done | bytes 98336 | tf_op jit(solution)/shard_map/ppermute | solution.py:52
  71.3 2.8 %collective-permute-done.28 = bf16[24,2048]{1,0:T(8,128)(2,1)S(1)} collective-permute-done((bf16[24,2048]{1,0:T(8,128)(2,1)S(1)}, bf16[24,2048]{1,0:T(8,128)(2,1)S(1)}, u32[]{:S(2)}, u32[]{:S(2)}) %collective-permute-start.28) | collective-permute-done | bytes 98336 | tf_op jit(solution)/shard_map/ppermute | solution.py:52
  (81 shorter events, 15.2 us)
Async XLA Ops:
  3.6 10.7 %collective-permute-start.2 = (bf16[24,2048]{1,0:T(8,128)(2,1)}, bf16[24,2048]{1,0:T(8,128)(2,1)S(1)}, u32[]{:S(2)}, u32[]{:S(2)}) collective-permute-start(bf16[24,2048]{1,0:T(8,128)(2,1)} %shard_map.114.refs_0_), channel_id=1, source_target_pairs={{0,2},{2,0},{4,6},{6,4},{1,3},{3,1},{5,7},{7,5},{8,10},{10,8},{12,... | collective-permute-start | bytes 294920 | tf_op jit(solution)/shard_map/ppermute | solution.py:52
  6.7 10.7 %collective-permute-start.3 = (bf16[24,2048]{1,0:T(8,128)(2,1)}, bf16[24,2048]{1,0:T(8,128)(2,1)S(1)}, u32[]{:S(2)}, u32[]{:S(2)}) collective-permute-start(bf16[24,2048]{1,0:T(8,128)(2,1)} %shard_map.114.refs_0_), channel_id=1, source_target_pairs={{0,4},{2,6},{4,0},{6,2},{1,5},{3,7},{5,1},{7,3},{8,12},{10,14},{12... | collective-permute-start | bytes 294920 | tf_op jit(solution)/shard_map/ppermute | solution.py:52
  9.3 8.1 %collective-permute-start.4 = (bf16[24,2048]{1,0:T(8,128)(2,1)}, bf16[24,2048]{1,0:T(8,128)(2,1)S(1)}, u32[]{:S(2)}, u32[]{:S(2)}) collective-permute-start(bf16[24,2048]{1,0:T(8,128)(2,1)} %shard_map.114.refs_0_), channel_id=1, source_target_pairs={{0,6},{2,4},{4,2},{6,0},{1,7},{3,5},{5,3},{7,1},{8,14},{10,12},{12... | collective-permute-start | bytes 294920 | tf_op jit(solution)/shard_map/ppermute | solution.py:52
  9.3 8.6 %collective-permute-start.5 = (bf16[24,2048]{1,0:T(8,128)(2,1)}, bf16[24,2048]{1,0:T(8,128)(2,1)S(1)}, u32[]{:S(2)}, u32[]{:S(2)}) collective-permute-start(bf16[24,2048]{1,0:T(8,128)(2,1)} %shard_map.114.refs_0_), channel_id=1, source_target_pairs={{0,1},{1,0},{2,3},{3,2},{4,5},{5,4},{6,7},{7,6},{8,9},{9,8},{10,11... | collective-permute-start | bytes 294920 | tf_op jit(solution)/shard_map/ppermute | solution.py:47
  14.4 3.5 %collective-permute-start.6 = (bf16[24,2048]{1,0:T(8,128)(2,1)S(1)}, bf16[24,2048]{1,0:T(8,128)(2,1)S(1)}, u32[]{:S(2)}, u32[]{:S(2)}) collective-permute-start(bf16[24,2048]{1,0:T(8,128)(2,1)S(1)} %collective-permute-done.2.refs_1_), channel_id=1, source_target_pairs={{0,1},{1,0},{2,3},{3,2},{4,5},{5,4},{6,7},{7,6},{8,9},{9,8},{10,11... | collective-permute-start | bytes 294920 | tf_op jit(solution)/shard_map/ppermute | solution.py:47
  19.2 9.1 %collective-permute-start.13 = (bf16[64,2048]{1,0:T(8,128)(2,1)S(1)}, bf16[64,2048]{1,0:T(8,128)(2,1)S(1)}, u32[]{:S(2)}, u32[]{:S(2)}) collective-permute-start(bf16[64,2048]{1,0:T(8,128)(2,1)S(1)} %shard_map.115.refs_0_), channel_id=1, source_target_pairs={{0,16},{1,9},{8,24},{9,1},{16,0},{17,25},{24,8},{25,17},{2,18},{3,... | collective-permute-start | bytes 786440 | tf_op jit(solution)/shard_map/ppermute | solution.py:58
  20.8 7.0 %collective-permute-start.14 = (bf16[64,2048]{1,0:T(8,128)(2,1)S(1)}, bf16[64,2048]{1,0:T(8,128)(2,1)S(1)}, u32[]{:S(2)}, u32[]{:S(2)}) collective-permute-start(bf16[64,2048]{1,0:T(8,128)(2,1)S(1)} %shard_map.115.refs_0_), channel_id=1, source_target_pairs={{0,8},{1,17},{8,0},{9,25},{16,24},{17,1},{24,16},{25,9},{2,10},{3,... | collective-permute-start | bytes 786440 | tf_op jit(solution)/shard_map/ppermute | solution.py:58
  22.3 10.2 %collective-permute-start.15 = (bf16[64,2048]{1,0:T(8,128)(2,1)S(1)}, bf16[64,2048]{1,0:T(8,128)(2,1)S(1)}, u32[]{:S(2)}, u32[]{:S(2)}) collective-permute-start(bf16[64,2048]{1,0:T(8,128)(2,1)S(1)} %shard_map.115.refs_0_), channel_id=1, source_target_pairs={{0,1},{1,0},{2,3},{3,2},{4,5},{5,4},{6,7},{7,6},{8,9},{9,8},{10,11... | collective-permute-start | bytes 786440 | tf_op jit(solution)/shard_map/ppermute | solution.py:47
  27.8 4.9 %collective-permute-start.16 = (bf16[64,2048]{1,0:T(8,128)(2,1)S(1)}, bf16[64,2048]{1,0:T(8,128)(2,1)S(1)}, u32[]{:S(2)}, u32[]{:S(2)}) collective-permute-start(bf16[64,2048]{1,0:T(8,128)(2,1)S(1)} %collective-permute-done.14.refs_2_), channel_id=1, source_target_pairs={{0,1},{1,0},{2,3},{3,2},{4,5},{5,4},{6,7},{7,6},{8,9},{9,8},{10,11... | collective-permute-start | bytes 786440 | tf_op jit(solution)/shard_map/ppermute | solution.py:47
  28.3 6.7 %collective-permute-start.17 = (bf16[64,2048]{1,0:T(8,128)(2,1)S(1)}, bf16[64,2048]{1,0:T(8,128)(2,1)S(1)}, u32[]{:S(2)}, u32[]{:S(2)}) collective-permute-start(bf16[64,2048]{1,0:T(8,128)(2,1)S(1)} %collective-permute-done.13.refs_1_), channel_id=1, source_target_pairs={{0,1},{1,0},{2,3},{3,2},{4,5},{5,4},{6,7},{7,6},{8,9},{9,8},{10,11... | collective-permute-start | bytes 786440 | tf_op jit(solution)/shard_map/ppermute | solution.py:47
  28.4 13.8 %collective-permute-start.23 = (bf16[64,2048]{1,0:T(8,128)(2,1)S(1)}, bf16[64,2048]{1,0:T(8,128)(2,1)S(1)}, u32[]{:S(2)}, u32[]{:S(2)}) collective-permute-start(bf16[64,2048]{1,0:T(8,128)(2,1)S(1)} %collective-permute-done.13.refs_1_), channel_id=1, source_target_pairs={{0,8},{1,17},{8,0},{9,25},{16,24},{17,1},{24,16},{25,9},{2,10},{3,... | collective-permute-start | bytes 786440 | tf_op jit(solution)/shard_map/ppermute | solution.py:58
  29.9 7.6 %collective-permute-start.11 = (bf16[24,2048]{1,0:T(8,128)(2,1)S(1)}, bf16[24,2048]{1,0:T(8,128)(2,1)S(1)}, u32[]{:S(2)}, u32[]{:S(2)}) collective-permute-start(bf16[24,2048]{1,0:T(8,128)(2,1)S(1)} %maximum_maximum_fusion), channel_id=1, source_target_pairs={{0,6},{2,4},{4,2},{6,0},{1,7},{3,5},{5,3},{7,1},{8,14},{10,12},{12... | collective-permute-start | bytes 294920 | tf_op jit(solution)/shard_map/ppermute | solution.py:52
  32.5 9.7 %collective-permute-start.10 = (bf16[24,2048]{1,0:T(8,128)(2,1)S(1)}, bf16[24,2048]{1,0:T(8,128)(2,1)S(1)}, u32[]{:S(2)}, u32[]{:S(2)}) collective-permute-start(bf16[24,2048]{1,0:T(8,128)(2,1)S(1)} %maximum_maximum_fusion), channel_id=1, source_target_pairs={{0,4},{2,6},{4,0},{6,2},{1,5},{3,7},{5,1},{7,3},{8,12},{10,14},{12... | collective-permute-start | bytes 294920 | tf_op jit(solution)/shard_map/ppermute | solution.py:52
  32.7 10.0 %collective-permute-start.9 = (bf16[24,2048]{1,0:T(8,128)(2,1)S(1)}, bf16[24,2048]{1,0:T(8,128)(2,1)S(1)}, u32[]{:S(2)}, u32[]{:S(2)}) collective-permute-start(bf16[24,2048]{1,0:T(8,128)(2,1)S(1)} %maximum_maximum_fusion), channel_id=1, source_target_pairs={{0,2},{2,0},{4,6},{6,4},{1,3},{3,1},{5,7},{7,5},{8,10},{10,8},{12,... | collective-permute-start | bytes 294920 | tf_op jit(solution)/shard_map/ppermute | solution.py:52
  35.0 14.2 %collective-permute-start = (bf16[2,64,2048]{2,1,0:T(8,128)(2,1)S(1)}, bf16[2,64,2048]{2,1,0:T(8,128)(2,1)S(1)}, u32[]{:S(2)}, u32[]{:S(2)}) collective-permute-start(bf16[2,64,2048]{2,1,0:T(8,128)(2,1)S(1)} %get-tuple-element.22), channel_id=1, source_target_pairs={{1,2},{3,4},{5,6},{2,1},{4,3},{6,5},{9,10},{11,12},{13,14},{10,9},... | collective-permute-start | bytes 1572872 | tf_op jit(solution)/shard_map/ppermute | solution.py:442
  37.6 12.7 %collective-permute-start.1 = (bf16[2,64,2048]{2,1,0:T(8,128)(2,1)S(1)}, bf16[2,64,2048]{2,1,0:T(8,128)(2,1)S(1)}, u32[]{:S(2)}, u32[]{:S(2)}) collective-permute-start(bf16[2,64,2048]{2,1,0:T(8,128)(2,1)S(1)} %get-tuple-element.23), channel_id=1, source_target_pairs={{0,1},{1,0},{2,3},{3,2},{4,5},{5,4},{6,7},{7,6},{8,9},{9,8},{10,11... | collective-permute-start | bytes 1572872 | tf_op jit(solution)/shard_map/ppermute | solution.py:47
  42.8 12.6 %collective-permute-start.12 = (bf16[96,2048]{1,0:T(8,128)(2,1)S(1)}, bf16[96,2048]{1,0:T(8,128)(2,1)S(1)}, u32[]{:S(2)}, u32[]{:S(2)}) collective-permute-start(bf16[96,2048]{1,0:T(8,128)(2,1)S(1)} %pad_maximum_fusion.near_ref), channel_id=1, source_target_pairs={{0,1},{1,0},{2,3},{3,2},{4,5},{5,4},{6,7},{7,6},{8,9},{9,8},{10,11... | collective-permute-start | bytes 1179656 | tf_op jit(solution)/shard_map/ppermute | solution.py:47
  44.1 13.2 %collective-permute-start.18 = (bf16[64,2048]{1,0:T(8,128)(2,1)S(1)}, bf16[64,2048]{1,0:T(8,128)(2,1)S(1)}, u32[]{:S(2)}, u32[]{:S(2)}) collective-permute-start(bf16[64,2048]{1,0:T(8,128)(2,1)S(1)} %get-tuple-element.30), channel_id=1, source_target_pairs={{0,1},{1,0},{2,3},{3,2},{4,5},{5,4},{6,7},{7,6},{8,9},{9,8},{10,11... | collective-permute-start | bytes 786440 | tf_op jit(solution)/shard_map/ppermute | solution.py:47
  48.6 14.7 %collective-permute-start.20 = (bf16[64,2048]{1,0:T(8,128)(2,1)S(1)}, bf16[64,2048]{1,0:T(8,128)(2,1)S(1)}, u32[]{:S(2)}, u32[]{:S(2)}) collective-permute-start(bf16[64,2048]{1,0:T(8,128)(2,1)S(1)} %add_convert_fusion.2), channel_id=1, source_target_pairs={{0,16},{1,9},{8,24},{9,1},{16,0},{17,25},{24,8},{25,17},{2,18},{3,... | collective-permute-start | bytes 786440 | tf_op jit(solution)/shard_map/ppermute | solution.py:58
  49.2 14.2 %collective-permute-start.22 = (bf16[64,2048]{1,0:T(8,128)(2,1)S(1)}, bf16[64,2048]{1,0:T(8,128)(2,1)S(1)}, u32[]{:S(2)}, u32[]{:S(2)}) collective-permute-start(bf16[64,2048]{1,0:T(8,128)(2,1)S(1)} %add_convert_fusion.1), channel_id=1, source_target_pairs={{0,8},{1,17},{8,0},{9,25},{16,24},{17,1},{24,16},{25,9},{2,10},{3,... | collective-permute-start | bytes 786440 | tf_op jit(solution)/shard_map/ppermute | solution.py:58
  50.2 13.1 %collective-permute-start.26 = (bf16[64,2048]{1,0:T(8,128)(2,1)S(1)}, bf16[64,2048]{1,0:T(8,128)(2,1)S(1)}, u32[]{:S(2)}, u32[]{:S(2)}) collective-permute-start(bf16[64,2048]{1,0:T(8,128)(2,1)S(1)} %add_convert_fusion), channel_id=1, source_target_pairs={{0,24},{1,25},{8,16},{9,17},{16,8},{17,9},{24,0},{25,1},{2,26},{3,... | collective-permute-start | bytes 786440 | tf_op jit(solution)/shard_map/ppermute | solution.py:58
  63.7 7.6 %collective-permute-start.29 = (bf16[24,2048]{1,0:T(8,128)(2,1)S(1)}, bf16[24,2048]{1,0:T(8,128)(2,1)S(1)}, u32[]{:S(2)}, u32[]{:S(2)}) collective-permute-start(bf16[24,2048]{1,0:T(8,128)(2,1)S(1)} %get-tuple-element.40), channel_id=1, source_target_pairs={{0,6},{2,4},{4,2},{6,0},{1,7},{3,5},{5,3},{7,1},{8,14},{10,12},{12... | collective-permute-start | bytes 294920 | tf_op jit(solution)/shard_map/ppermute | solution.py:52
  66.6 7.6 %collective-permute-start.28 = (bf16[24,2048]{1,0:T(8,128)(2,1)S(1)}, bf16[24,2048]{1,0:T(8,128)(2,1)S(1)}, u32[]{:S(2)}, u32[]{:S(2)}) collective-permute-start(bf16[24,2048]{1,0:T(8,128)(2,1)S(1)} %get-tuple-element.39), channel_id=1, source_target_pairs={{0,4},{2,6},{4,0},{6,2},{1,5},{3,7},{5,1},{7,3},{8,12},{10,14},{12... | collective-permute-start | bytes 294920 | tf_op jit(solution)/shard_map/ppermute | solution.py:52
  66.6 7.6 %collective-permute-start.27 = (bf16[24,2048]{1,0:T(8,128)(2,1)S(1)}, bf16[24,2048]{1,0:T(8,128)(2,1)S(1)}, u32[]{:S(2)}, u32[]{:S(2)}) collective-permute-start(bf16[24,2048]{1,0:T(8,128)(2,1)S(1)} %get-tuple-element.38), channel_id=1, source_target_pairs={{0,2},{2,0},{4,6},{6,4},{1,3},{3,1},{5,7},{7,5},{8,10},{10,8},{12,... | collective-permute-start | bytes 294920 | tf_op jit(solution)/shard_map/ppermute | solution.py:52
  (13 other events, 54.2 us)
